TPU v7x, 512 devices: a whole 4x8x8 slice. The times are simulated.
512 devices in a mesh: rep: 16 (over x, z_lo, core), dp: 32 (over y, z_hi).
Axes of the slice: x: 4, y: 8, z: 8 (z_hi: 4, z_lo: 2; z = z_hi * 2 + z_lo), core: 2. Of those that a mesh axis runs over, the one named last changes fastest.
Arguments:
- image_features: bfloat16 [65536, 1408], P(('rep', 'dp')), parts along dimension 0, may hold values from -24 to 24
- text_embed: bfloat16 [65536, 512], P(('rep', 'dp')), parts along dimension 0, may hold values from -24 to 24
- image_head: bfloat16 [22528, 512], P(('rep', 'dp')), parts along dimension 0, may hold values from -1 to 3
- logit_scale: float32 [1], replicated, may hold values from 10 to 40
Outputs:
- image_features_grad: bfloat16 [65536, 1408], P(('rep', 'dp')), parts along dimension 0
- text_embed_grad: bfloat16 [65536, 512], P(('rep', 'dp')), parts along dimension 0
- image_head_grad: float32 [22528, 512], P(('rep', 'dp')), parts along dimension 0
There are 16 independent parts, one for each index of `rep`. A program takes and returns all parts, laid end to end along the dimension named above; an argument that names none is the same for every part. Nothing has to cross between parts.
All inputs are finite; a program needn't handle non-finite values.
Results may differ from a plain program's by a relative error of at most 0.02.
Values may be sent and summed in bfloat16 or wider, within the bound.
No kernel may reach another device: no remote copies, remote signals or barrier semaphores. Data moves between devices by JAX's collectives and lax.ppermute only.
A program may use at most 64 MiB of HBM per device.

v0:
```python
import jax
import jax.numpy as jnp
from jax import lax
from jax.sharding import Mesh
from jax.sharding import PartitionSpec as P


NQ, NP, NZ = 4, 2, 4
NY = NQ * NP
Q, PAIR, Z = "dp_q", "dp_pair", "dp_z"
Y = (Q, PAIR)
SAME = (Q, Z)


def matmul(left, right, left_dim=1, right_dim=0):
    return lax.dot_general(
        left, right, (((left_dim,), (right_dim,)), ((), ())), preferred_element_type=jnp.float32
    )


def to_all(array, axes, devices):
    copies = jnp.broadcast_to(array[None], (devices, *array.shape))
    return lax.all_to_all(copies, axes, 0, 0, tiled=True)


def swapped(array):
    return lax.ppermute(array, PAIR, [(0, 1), (1, 0)])


def shifted(array, distance):
    return lax.ppermute(array, Z, [(k, (k + distance) % NZ) for k in range(NZ)])


def inv_norm(embedding):
    return lax.rsqrt(jnp.sum(embedding * embedding, axis=1, keepdims=True) + 1e-06)


def norm_backward(embedding, inv, upstream):
    inner = jnp.sum(embedding * upstream, axis=1, keepdims=True)
    return (inv * upstream - embedding * (inv * inv * inv) * inner).astype(jnp.bfloat16)


def column_choice(width, padded, block, p):
    half = NQ * NZ * padded
    shape = (width, NP * half)
    col = lax.broadcasted_iota(jnp.int32, (1, shape[1]), 1)
    slot, place, c = col // half, (col % half) // padded, col % padded
    owner = (place // NZ * NP + (p + slot) % NP) * NZ + place % NZ
    source = jnp.where(c < block, owner * block + c, -1)
    return (lax.broadcasted_iota(jnp.int32, shape, 0) == source).astype(jnp.bfloat16)


def local(image_features, text_embed, image_head, logit_scale):
    scale = logit_scale[0]
    rows, width = image_features.shape
    block, emb_width = image_head.shape
    padded = -(-block // 16) * 16
    half = NQ * NZ * padded
    p, b = lax.axis_index(PAIR), lax.axis_index(Z)
    a = lax.axis_index(Y)

    head = to_all(jnp.pad(image_head, ((0, padded - block), (0, 0))), SAME, NQ * NZ)
    head = head.reshape(half, emb_width)
    choice = column_choice(width, padded, block, p)
    kept = matmul(image_features, choice[:, :half]).astype(jnp.bfloat16)
    given = matmul(image_features, choice[:, half:]).astype(jnp.bfloat16)
    taken = swapped(given)
    partner_part = matmul(taken, head).astype(jnp.bfloat16)

    txt_emb = text_embed.astype(jnp.float32)
    txt_inv = inv_norm(txt_emb)
    txt_unit = (txt_emb * txt_inv).astype(jnp.bfloat16)
    txt_sent, partner_part = lax.optimization_barrier((txt_unit, partner_part))
    texts = to_all(txt_sent, Y, NY).reshape(NY * rows, emb_width)
    returned = swapped(partner_part)

    img_emb = matmul(kept, head) + returned.astype(jnp.float32)
    img_inv = inv_norm(img_emb)
    img_unit = (img_emb * img_inv).astype(jnp.bfloat16)
    images = lax.all_gather(img_unit, Z, axis=0, tiled=True)

    exps = jnp.exp(scale * matmul(images, texts, 1, 1))
    row_part = jnp.sum(exps, axis=1)
    col_part = jnp.sum(exps, axis=0)

    col_sum = jnp.sum(to_all(col_part.reshape(NY, rows), Y, NY), axis=0).reshape(NY * rows)
    row_sum = lax.psum(row_part, Z)

    i = lax.broadcasted_iota(jnp.int32, exps.shape, 0) - b * rows
    j = lax.broadcasted_iota(jnp.int32, exps.shape, 1) - a * rows
    label = jnp.where((i == j) & (i >= 0) & (i < rows), 2.0, 0.0)
    coef = exps * ((1.0 / row_sum)[:, None] + (1.0 / col_sum)[None, :])
    coef = (coef - label).astype(jnp.bfloat16)

    img_part = matmul(coef, texts)
    txt_part = matmul(coef, images, 0, 0)
    txt_grads = lax.all_to_all(
        txt_part.astype(jnp.bfloat16).reshape(NY, rows, emb_width), Y, 0, 0, tiled=True
    )
    origin = jnp.uint32(0)
    img_sum = lax.dynamic_slice(
        img_part, (b.astype(jnp.uint32) * rows, origin), (rows, emb_width)
    )
    for k in range(1, NZ):
        start = ((b + NZ - k) & (NZ - 1)).astype(jnp.uint32) * rows
        piece = lax.dynamic_slice(img_part, (start, origin), (rows, emb_width))
        img_sum = img_sum + shifted(piece.astype(jnp.bfloat16), -k).astype(jnp.float32)
    img_emb_grad = norm_backward(img_emb, img_inv, scale * img_sum)
    partner_grad = swapped(img_emb_grad)

    head_part = matmul(kept, img_emb_grad, 0, 0) + matmul(taken, partner_grad, 0, 0)
    head_part, txt_grads = lax.optimization_barrier((head_part.astype(jnp.bfloat16), txt_grads))
    head_grads = lax.all_to_all(
        head_part.reshape(NQ * NZ, padded, emb_width), SAME, 0, 0, tiled=True
    )
    kept_grad = matmul(img_emb_grad, head, 1, 1).astype(jnp.bfloat16)
    given_grad = swapped(matmul(partner_grad, head, 1, 1).astype(jnp.bfloat16))
    image_features_grad = (
        matmul(kept_grad, choice[:, :half], 1, 1) + matmul(given_grad, choice[:, half:], 1, 1)
    ).astype(jnp.bfloat16)

    txt_own = lax.dynamic_slice(
        txt_part, (a.astype(jnp.uint32) * rows, origin), (rows, emb_width)
    )
    ids = jnp.arange(NY, dtype=jnp.int32)[:, None, None]
    others = jnp.where(ids == a, 0.0, txt_grads.astype(jnp.float32))
    txt_unit_grad = scale * (jnp.sum(others, axis=0) + txt_own)
    text_embed_grad = norm_backward(txt_emb, txt_inv, txt_unit_grad)
    image_head_grad = jnp.sum(head_grads.astype(jnp.float32), axis=0)[:block]
    return (image_features_grad, text_embed_grad, image_head_grad)


def solution(mesh):
    split = Mesh(mesh.devices.reshape(mesh.shape["rep"], NQ, NP, NZ), ("rep", Q, PAIR, Z))
    spec = P(("rep", Q, PAIR, Z), None)

    return jax.shard_map(
        local,
        mesh=split,
        in_specs=(spec, spec, spec, P(None)),
        out_specs=(spec, spec, spec),
        check_vma=False,
    )
```

profile of v0, /device:TPU:6, one launch (start us, length us, event | category | flops | bytes accessed | tf_op | source)
XLA Modules:
  0.0 192.5 jit_solution(2620621735079500011)
XLA Ops:
  0.6 0.0 copy-start
  0.6 0.9 pad.4
  1.5 1.0 broadcast_in_dim.26
  2.5 15.7 %all-to-all-start = ((bf16[16,48,512]{2,1,0:T(8,128)(2,1)}), bf16[16,48,512]{2,1,0:T(8,128)(2,1)S(1)}, u32[]{:S(2)}, u32[]{:S(2)}) async-start(bf16[16,48,512]{2,1,0:T(8,128)(2,1)} %broadcast_in_dim.26), calls=%async_computation | async-start | bytes 1572864 | tf_op jit(solution)/shard_map/all_to_all | solution.py:23
  18.2 1.8 iota_compare_fusion
  20.0 0.0 copy-done
  20.0 0.0 copy-start.1
  20.0 0.0 copy-start.3
  20.0 0.9 fusion.14
  20.9 2.6 %collective-permute-start = (bf16[128,768]{0,1:T(8,128)(2,1)S(1)}, bf16[128,768]{0,1:T(8,128)(2,1)S(1)}, u32[]{:S(2)}, u32[]{:S(2)}) collective-permute-start(bf16[128,768]{0,1:T(8,128)(2,1)S(1)} %fusion.14), channel_id=1, source_target_pairs={{0,4},{4,0},{1,5},{5,1},{2,6},{6,2},{3,7},{7,3},{8,12},{12,8},{9,1... | collective-permute-start | bytes 589832 | tf_op jit(solution)/shard_map/ppermute | solution.py:27
  23.5 0.0 copy-done.3
  23.5 0.1 fusion.15
  23.6 0.8 fusion.16
  24.4 16.1 %collective-permute-done = bf16[128,768]{0,1:T(8,128)(2,1)S(1)} collective-permute-done((bf16[128,768]{0,1:T(8,128)(2,1)S(1)}, bf16[128,768]{0,1:T(8,128)(2,1)S(1)}, u32[]{:S(2)}, u32[]{:S(2)}) %collective-permute-start) | collective-permute-done | bytes 196640 | tf_op jit(solution)/shard_map/ppermute | solution.py:27
  40.4 5.4 %all-to-all-done = bf16[16,48,512]{2,1,0:T(8,128)(2,1)S(1)} async-done(((bf16[16,48,512]{2,1,0:T(8,128)(2,1)}), bf16[16,48,512]{2,1,0:T(8,128)(2,1)S(1)}, u32[]{:S(2)}, u32[]{:S(2)}) %all-to-all-start) | async-done | bytes 786464 | tf_op jit(solution)/shard_map/all_to_all | solution.py:23
  45.8 1.0 convolution_convert_fusion.2
  46.8 2.0 %broadcast_in_dim.31 = bf16[8,128,512]{2,1,0:T(8,128)(2,1)} broadcast(bf16[128,512]{1,0:T(8,128)(2,1)} %fusion.16), dimensions={1,2} | broadcast | bytes 1179648 | tf_op jit(solution)/shard_map/broadcast_in_dim | solution.py:22
  48.8 4.6 %all-to-all-start.1 = ((bf16[8,128,512]{2,1,0:T(8,128)(2,1)}), bf16[8,128,512]{2,1,0:T(8,128)(2,1)}, u32[]{:S(2)}, u32[]{:S(2)}) async-start(bf16[8,128,512]{2,1,0:T(8,128)(2,1)} %broadcast_in_dim.31), calls=%async_computation.1 | async-start | bytes 2097152 | tf_op jit(solution)/shard_map/all_to_all | solution.py:23
  53.4 0.9 fusion.13
  54.3 0.0 copy-start.6
  54.3 3.9 %collective-permute-start.1 = (bf16[128,512]{1,0:T(8,128)(2,1)}, bf16[128,512]{1,0:T(8,128)(2,1)S(1)}, u32[]{:S(2)}, u32[]{:S(2)}) collective-permute-start(bf16[128,512]{1,0:T(8,128)(2,1)} %convolution_convert_fusion.2), channel_id=1, source_target_pairs={{0,4},{4,0},{1,5},{5,1},{2,6},{6,2},{3,7},{7,3},{8,12},{12,8},{9,1... | collective-permute-start | bytes 393224 | tf_op jit(solution)/shard_map/ppermute | solution.py:27
  58.9 20.4 %collective-permute-done.1 = bf16[128,512]{1,0:T(8,128)(2,1)S(1)} collective-permute-done((bf16[128,512]{1,0:T(8,128)(2,1)}, bf16[128,512]{1,0:T(8,128)(2,1)S(1)}, u32[]{:S(2)}, u32[]{:S(2)}) %collective-permute-start.1) | collective-permute-done | bytes 131104 | tf_op jit(solution)/shard_map/ppermute | solution.py:27
  79.3 0.4 multiply_reduce_fusion.1
  79.7 0.3 copy-done.2
  80.0 0.1 multiply_convert_fusion
  80.1 17.4 %all_gather.3 = bf16[512,512]{1,0:T(8,128)(2,1)S(1)} all-gather(bf16[128,512]{1,0:T(8,128)(2,1)S(1)} %multiply_convert_fusion), channel_id=1, replica_groups=mesh['rep'=16,'dp_q'=4,'dp_pair'=2,'dp_z'=4] {'dp_z'}, dimensions={0}, use_global_device_ids=true | all-gather | bytes 655360 | tf_op jit(solution)/shard_map/all_gather | solution.py:80
  97.5 0.0 all-to-all-done.1
  97.5 3.3 %fusion.46 = (f32[512]{0:T(512)S(1)}, f32[1024]{0:T(1024)S(1)}, f32[512,1024]{1,0:T(8,128)}) fusion(bf16[512,512]{1,0:T(8,128)(2,1)S(1)} %all_gather.3, bf16[1024,512]{1,0:T(8,128)(2,1)} %bitcast.3, f32[]{:T(128)} %bitcast.33), kind=kOutput, calls=%fused_computation.95 | convolution fusion | flops 538442240 | bytes 3676164 | tf_op jit(solution)/shard_map/dot_general | solution.py:16
  100.8 0.0 copy-done.6
  100.8 0.6 broadcast_in_dim.51
  101.5 5.3 %all-to-all-start.2 = ((f32[8,8,128]{2,1,0:T(8,128)}), f32[8,8,128]{2,1,0:T(8,128)S(1)}, u32[]{:S(2)}, u32[]{:S(2)}) async-start(f32[8,8,128]{2,1,0:T(8,128)} %broadcast_in_dim.51), calls=%async_computation.2 | async-start | bytes 65536 | tf_op jit(solution)/shard_map/all_to_all | solution.py:23
  106.7 10.2 %psum.7 = f32[512]{0:T(512)S(1)} all-reduce(f32[512]{0:T(512)S(1)} %get-tuple-element.11), channel_id=1, replica_groups=mesh['rep'=16,'dp_q'=4,'dp_pair'=2,'dp_z'=4] {'dp_z'}, use_global_device_ids=true, to_apply=%region_3.4 | all-reduce | flops 512 | bytes 4096 | tf_op jit(solution)/shard_map/psum | solution.py:87
  117.0 0.0 all-to-all-done.2
  117.0 2.1 %subtract_convert_fusion = bf16[512,1024]{1,0:T(8,128)(2,1)S(1)} fusion(f32[512,1024]{1,0:T(8,128)} %get-tuple-element.22, s32[1024]{0:T(1024)S(1)} %iota_subtract_fusion, f32[1024]{0:T(1024)S(1)} %divide_bitcast_fusion, f32[512]{0:T(512)S(1)} %broadcast_divide_fusion, s32[512]{0:T(512)S(1)} %iota_subtract_fusion.1, pred[512]{0:T(512)(128)(4,1)S(1)} %get-tuple-element.25, ...), kind=kLoop, calls=%fused_computation.12 | loop fusion | flops 4194304 | bytes 3159040 | tf_op jit(solution)/shard_map/convert_element_type | solution.py:93
  119.1 2.4 %fusion.47 = (bf16[1024,512]{1,0:T(8,128)(2,1)}, f32[1024,512]{1,0:T(8,128)}) fusion(bf16[512,1024]{1,0:T(8,128)(2,1)S(1)} %subtract_convert_fusion, bf16[512,512]{1,0:T(8,128)(2,1)S(1)} %all_gather.3), kind=kOutput, calls=%fused_computation.96 | convolution fusion | flops 537395200 | bytes 4718592 | tf_op jit(solution)/shard_map/dot_general | solution.py:16
  121.6 7.2 %all-to-all-start.3 = ((bf16[8,128,512]{2,1,0:T(8,128)(2,1)}), bf16[8,128,512]{2,1,0:T(8,128)(2,1)S(1)}, u32[]{:S(2)}, u32[]{:S(2)}) async-start(bf16[8,128,512]{2,1,0:T(8,128)(2,1)} %bitcast.41), calls=%async_computation.3 | async-start | bytes 2097152 | tf_op jit(solution)/shard_map/all_to_all | solution.py:97
  128.7 1.9 %fusion.48 = f32[512,512]{1,0:T(8,128)S(1)} fusion(bf16[512,1024]{1,0:T(8,128)(2,1)S(1)} %subtract_convert_fusion, bf16[1024,512]{1,0:T(8,128)(2,1)} %bitcast.3), kind=kOutput, calls=%fused_computation.97 | convolution fusion | flops 536870912 | bytes 3145728 | tf_op jit(solution)/shard_map/dot_general | solution.py:16
  130.7 0.0 copy-start.5
  130.7 1.0 copy-done.5
  131.7 0.7 dynamic-slice_convert_fusion.2
  132.4 3.3 %collective-permute-start.4 = (bf16[128,512]{1,0:T(8,128)(2,1)}, bf16[128,512]{1,0:T(8,128)(2,1)S(1)}, u32[]{:S(2)}, u32[]{:S(2)}) collective-permute-start(bf16[128,512]{1,0:T(8,128)(2,1)} %get-tuple-element.15), channel_id=1, source_target_pairs={{0,1},{1,2},{2,3},{3,0},{4,5},{5,6},{6,7},{7,4},{8,9},{9,10},{10,1... | collective-permute-start | bytes 393224 | tf_op jit(solution)/shard_map/ppermute | solution.py:31
  135.7 5.0 %collective-permute-start.3 = (bf16[128,512]{1,0:T(8,128)(2,1)S(1)}, bf16[128,512]{1,0:T(8,128)(2,1)S(1)}, u32[]{:S(2)}, u32[]{:S(2)}) collective-permute-start(bf16[128,512]{1,0:T(8,128)(2,1)S(1)} %get-tuple-element.14), channel_id=1, source_target_pairs={{0,2},{1,3},{2,0},{3,1},{4,6},{5,7},{6,4},{7,5},{8,10},{9,11},{10,... | collective-permute-start | bytes 393224 | tf_op jit(solution)/shard_map/ppermute | solution.py:31
  140.8 5.2 %collective-permute-start.2 = (bf16[128,512]{1,0:T(8,128)(2,1)S(1)}, bf16[128,512]{1,0:T(8,128)(2,1)S(1)}, u32[]{:S(2)}, u32[]{:S(2)}) collective-permute-start(bf16[128,512]{1,0:T(8,128)(2,1)S(1)} %get-tuple-element.13), channel_id=1, source_target_pairs={{0,3},{1,0},{2,1},{3,2},{4,7},{5,4},{6,5},{7,6},{8,11},{9,8},{10,9... | collective-permute-start | bytes 393224 | tf_op jit(solution)/shard_map/ppermute | solution.py:31
  145.9 0.0 collective-permute-done.4
  146.0 1.3 collective-permute-done.3
  147.3 4.4 %collective-permute-done.2 = bf16[128,512]{1,0:T(8,128)(2,1)S(1)} collective-permute-done((bf16[128,512]{1,0:T(8,128)(2,1)S(1)}, bf16[128,512]{1,0:T(8,128)(2,1)S(1)}, u32[]{:S(2)}, u32[]{:S(2)}) %collective-permute-start.2) | collective-permute-done | bytes 131104 | tf_op jit(solution)/shard_map/ppermute | solution.py:31
  151.6 1.2 multiply_reduce_fusion
  152.8 1.1 subtract_convert_fusion.1
  154.0 3.9 %collective-permute-start.5 = (bf16[128,512]{1,0:T(8,128)(2,1)S(1)}, bf16[128,512]{1,0:T(8,128)(2,1)S(1)}, u32[]{:S(2)}, u32[]{:S(2)}) collective-permute-start(bf16[128,512]{1,0:T(8,128)(2,1)S(1)} %subtract_convert_fusion.1), channel_id=1, source_target_pairs={{0,4},{4,0},{1,5},{5,1},{2,6},{6,2},{3,7},{7,3},{8,12},{12,8},{9,1... | collective-permute-start | bytes 393224 | tf_op jit(solution)/shard_map/ppermute | solution.py:27
  157.9 0.3 fusion.49
  158.3 2.6 %collective-permute-done.5 = bf16[128,512]{1,0:T(8,128)(2,1)S(1)} collective-permute-done((bf16[128,512]{1,0:T(8,128)(2,1)S(1)}, bf16[128,512]{1,0:T(8,128)(2,1)S(1)}, u32[]{:S(2)}, u32[]{:S(2)}) %collective-permute-start.5) | collective-permute-done | bytes 131104 | tf_op jit(solution)/shard_map/ppermute | solution.py:27
  160.9 1.3 add_convert_fusion
  162.1 0.0 all-to-all-done.3
  162.1 9.7 %all-to-all-start.4 = ((bf16[16,48,512]{2,1,0:T(8,128)(2,1)}), bf16[16,48,512]{2,1,0:T(8,128)(2,1)S(1)}, u32[]{:S(2)}, u32[]{:S(2)}) async-start(bf16[16,48,512]{2,1,0:T(8,128)(2,1)} %bitcast.42), calls=%async_computation.4 | async-start | bytes 1572864 | tf_op jit(solution)/shard_map/all_to_all | solution.py:113
  171.8 1.1 convolution_convert_fusion
  172.9 2.5 %collective-permute-start.6 = (bf16[128,768]{1,0:T(8,128)(2,1)}, bf16[128,768]{1,0:T(8,128)(2,1)}, u32[]{:S(2)}, u32[]{:S(2)}) collective-permute-start(bf16[128,768]{1,0:T(8,128)(2,1)} %convolution_convert_fusion), channel_id=1, source_target_pairs={{0,4},{4,0},{1,5},{5,1},{2,6},{6,2},{3,7},{7,3},{8,12},{12,8},{9,1... | collective-permute-start | bytes 589832 | tf_op jit(solution)/shard_map/ppermute | solution.py:27
  175.4 3.1 %fusion.2 = f32[128,1408]{1,0:T(8,128)} fusion(pred[1408,1536]{1,0:T(32,128)(4,1)} %copy-done.1, bf16[128,512]{1,0:T(8,128)(2,1)S(1)} %subtract_convert_fusion.1, bf16[768,512]{1,0:T(8,128)(2,1)S(1)} %bitcast.40), kind=kOutput, calls=%fused_computation.4 | convolution fusion | flops 377585664 | bytes 2719744 | tf_op jit(solution)/shard_map/dot_general | solution.py:16
  178.4 7.1 %collective-permute-done.6 = bf16[128,768]{1,0:T(8,128)(2,1)} collective-permute-done((bf16[128,768]{1,0:T(8,128)(2,1)}, bf16[128,768]{1,0:T(8,128)(2,1)}, u32[]{:S(2)}, u32[]{:S(2)}) %collective-permute-start.6) | collective-permute-done | bytes 196640 | tf_op jit(solution)/shard_map/ppermute | solution.py:27
  185.5 3.1 %fusion.7 = bf16[128,1408]{1,0:T(8,128)(2,1)} fusion(f32[128,1408]{1,0:T(8,128)} %fusion.2, bf16[128,768]{1,0:T(8,128)(2,1)} %collective-permute-done.6, pred[1408,1536]{1,0:T(32,128)(4,1)} %copy-done.1), kind=kOutput, calls=%fused_computation.8 | convolution fusion | flops 277184512 | bytes 2359296 | tf_op jit(solution)/shard_map/dot_general | solution.py:16
  188.7 0.3 select_reduce_fusion
  189.0 1.1 fusion.20
  190.0 1.7 fusion.19
  191.8 0.0 all-to-all-done.4
  191.8 0.8 convert_reduce_fusion
  (20 shorter events, 0.1 us)
Async XLA Ops:
  0.6 19.4 %copy-start = (bf16[128,1408]{1,0:T(8,128)(2,1)S(1)}, bf16[128,1408]{1,0:T(8,128)(2,1)}, u32[]{:S(2)}) copy-start(bf16[128,1408]{1,0:T(8,128)(2,1)} %param.4) | copy-start | bytes 1081348
  2.5 43.4 %all-to-all-start = ((bf16[16,48,512]{2,1,0:T(8,128)(2,1)}), bf16[16,48,512]{2,1,0:T(8,128)(2,1)S(1)}, u32[]{:S(2)}, u32[]{:S(2)}) async-start(bf16[16,48,512]{2,1,0:T(8,128)(2,1)} %broadcast_in_dim.26), calls=%async_computation | async-start | bytes 1572864 | tf_op jit(solution)/shard_map/all_to_all | solution.py:23
  20.0 33.4 %copy-start.1 = (pred[1408,1536]{1,0:T(32,128)(4,1)}, pred[1408,1536]{1,0:T(32,128)(4,1)S(1)}, u32[]{:S(2)}) copy-start(pred[1408,1536]{1,0:T(32,128)(4,1)S(1)} %iota_compare_fusion) | copy-start | bytes 6488068
  20.0 3.5 %copy-start.3 = (bf16[128,512]{1,0:T(8,128)(2,1)S(1)}, bf16[128,512]{1,0:T(8,128)(2,1)}, u32[]{:S(2)}) copy-start(bf16[128,512]{1,0:T(8,128)(2,1)} %param.5) | copy-start | bytes 393220
  20.9 19.5 %collective-permute-start = (bf16[128,768]{0,1:T(8,128)(2,1)S(1)}, bf16[128,768]{0,1:T(8,128)(2,1)S(1)}, u32[]{:S(2)}, u32[]{:S(2)}) collective-permute-start(bf16[128,768]{0,1:T(8,128)(2,1)S(1)} %fusion.14), channel_id=1, source_target_pairs={{0,4},{4,0},{1,5},{5,1},{2,6},{6,2},{3,7},{7,3},{8,12},{12,8},{9,1... | collective-permute-start | bytes 589832 | tf_op jit(solution)/shard_map/ppermute | solution.py:27
  40.4 8.3 %copy-start.8 = (bf16[128,768]{0,1:T(8,128)(2,1)}, bf16[128,768]{0,1:T(8,128)(2,1)S(1)}, u32[]{:S(2)}) copy-start(bf16[128,768]{0,1:T(8,128)(2,1)S(1)} %collective-permute-done) | copy-start | bytes 589828
  48.8 48.7 %all-to-all-start.1 = ((bf16[8,128,512]{2,1,0:T(8,128)(2,1)}), bf16[8,128,512]{2,1,0:T(8,128)(2,1)}, u32[]{:S(2)}, u32[]{:S(2)}) async-start(bf16[8,128,512]{2,1,0:T(8,128)(2,1)} %broadcast_in_dim.31), calls=%async_computation.1 | async-start | bytes 2097152 | tf_op jit(solution)/shard_map/all_to_all | solution.py:23
  54.3 46.5 %copy-start.6 = (bf16[768,128]{1,0:T(8,128)(2,1)}, bf16[768,128]{1,0:T(8,128)(2,1)S(1)}, u32[]{:S(2)}) copy-start(bf16[768,128]{1,0:T(8,128)(2,1)S(1)} %fusion.13) | copy-start | bytes 589828
  54.3 25.0 %collective-permute-start.1 = (bf16[128,512]{1,0:T(8,128)(2,1)}, bf16[128,512]{1,0:T(8,128)(2,1)S(1)}, u32[]{:S(2)}, u32[]{:S(2)}) collective-permute-start(bf16[128,512]{1,0:T(8,128)(2,1)} %convolution_convert_fusion.2), channel_id=1, source_target_pairs={{0,4},{4,0},{1,5},{5,1},{2,6},{6,2},{3,7},{7,3},{8,12},{12,8},{9,1... | collective-permute-start | bytes 393224 | tf_op jit(solution)/shard_map/ppermute | solution.py:27
  79.3 0.7 copy-start.2
  101.5 15.5 %all-to-all-start.2 = ((f32[8,8,128]{2,1,0:T(8,128)}), f32[8,8,128]{2,1,0:T(8,128)S(1)}, u32[]{:S(2)}, u32[]{:S(2)}) async-start(f32[8,8,128]{2,1,0:T(8,128)} %broadcast_in_dim.51), calls=%async_computation.2 | async-start | bytes 65536 | tf_op jit(solution)/shard_map/all_to_all | solution.py:23
  121.6 40.6 %all-to-all-start.3 = ((bf16[8,128,512]{2,1,0:T(8,128)(2,1)}), bf16[8,128,512]{2,1,0:T(8,128)(2,1)S(1)}, u32[]{:S(2)}, u32[]{:S(2)}) async-start(bf16[8,128,512]{2,1,0:T(8,128)(2,1)} %bitcast.41), calls=%async_computation.3 | async-start | bytes 2097152 | tf_op jit(solution)/shard_map/all_to_all | solution.py:97
  130.7 1.0 copy-start.5
  131.7 26.2 %copy-start.7 = (bf16[768,128]{1,0:T(8,128)(2,1)S(1)}, bf16[768,128]{1,0:T(8,128)(2,1)}, u32[]{:S(2)}) copy-start(bf16[768,128]{1,0:T(8,128)(2,1)} %copy-done.6) | copy-start | bytes 589828
  132.4 28.4 %copy-start.9 = (bf16[128,768]{0,1:T(8,128)(2,1)S(1)}, bf16[128,768]{0,1:T(8,128)(2,1)}, u32[]{:S(2)}) copy-start(bf16[128,768]{0,1:T(8,128)(2,1)} %copy-done.8) | copy-start | bytes 589828
  132.4 13.5 %collective-permute-start.4 = (bf16[128,512]{1,0:T(8,128)(2,1)}, bf16[128,512]{1,0:T(8,128)(2,1)S(1)}, u32[]{:S(2)}, u32[]{:S(2)}) collective-permute-start(bf16[128,512]{1,0:T(8,128)(2,1)} %get-tuple-element.15), channel_id=1, source_target_pairs={{0,1},{1,2},{2,3},{3,0},{4,5},{5,6},{6,7},{7,4},{8,9},{9,10},{10,1... | collective-permute-start | bytes 393224 | tf_op jit(solution)/shard_map/ppermute | solution.py:31
  135.7 11.5 %collective-permute-start.3 = (bf16[128,512]{1,0:T(8,128)(2,1)S(1)}, bf16[128,512]{1,0:T(8,128)(2,1)S(1)}, u32[]{:S(2)}, u32[]{:S(2)}) collective-permute-start(bf16[128,512]{1,0:T(8,128)(2,1)S(1)} %get-tuple-element.14), channel_id=1, source_target_pairs={{0,2},{1,3},{2,0},{3,1},{4,6},{5,7},{6,4},{7,5},{8,10},{9,11},{10,... | collective-permute-start | bytes 393224 | tf_op jit(solution)/shard_map/ppermute | solution.py:31
  140.8 10.9 %collective-permute-start.2 = (bf16[128,512]{1,0:T(8,128)(2,1)S(1)}, bf16[128,512]{1,0:T(8,128)(2,1)S(1)}, u32[]{:S(2)}, u32[]{:S(2)}) collective-permute-start(bf16[128,512]{1,0:T(8,128)(2,1)S(1)} %get-tuple-element.13), channel_id=1, source_target_pairs={{0,3},{1,0},{2,1},{3,2},{4,7},{5,4},{6,5},{7,6},{8,11},{9,8},{10,9... | collective-permute-start | bytes 393224 | tf_op jit(solution)/shard_map/ppermute | solution.py:31
  154.0 6.9 %collective-permute-start.5 = (bf16[128,512]{1,0:T(8,128)(2,1)S(1)}, bf16[128,512]{1,0:T(8,128)(2,1)S(1)}, u32[]{:S(2)}, u32[]{:S(2)}) collective-permute-start(bf16[128,512]{1,0:T(8,128)(2,1)S(1)} %subtract_convert_fusion.1), channel_id=1, source_target_pairs={{0,4},{4,0},{1,5},{5,1},{2,6},{6,2},{3,7},{7,3},{8,12},{12,8},{9,1... | collective-permute-start | bytes 393224 | tf_op jit(solution)/shard_map/ppermute | solution.py:27
  162.1 29.6 %all-to-all-start.4 = ((bf16[16,48,512]{2,1,0:T(8,128)(2,1)}), bf16[16,48,512]{2,1,0:T(8,128)(2,1)S(1)}, u32[]{:S(2)}, u32[]{:S(2)}) async-start(bf16[16,48,512]{2,1,0:T(8,128)(2,1)} %bitcast.42), calls=%async_computation.4 | async-start | bytes 1572864 | tf_op jit(solution)/shard_map/all_to_all | solution.py:113
  172.9 12.6 %collective-permute-start.6 = (bf16[128,768]{1,0:T(8,128)(2,1)}, bf16[128,768]{1,0:T(8,128)(2,1)}, u32[]{:S(2)}, u32[]{:S(2)}) collective-permute-start(bf16[128,768]{1,0:T(8,128)(2,1)} %convolution_convert_fusion), channel_id=1, source_target_pairs={{0,4},{4,0},{1,5},{5,1},{2,6},{6,2},{3,7},{7,3},{8,12},{12,8},{9,1... | collective-permute-start | bytes 589832 | tf_op jit(solution)/shard_map/ppermute | solution.py:27
  178.4 10.5 %copy-start.4 = (bf16[128,512]{1,0:T(8,128)(2,1)S(1)}, bf16[128,512]{1,0:T(8,128)(2,1)}, u32[]{:S(2)}) copy-start(bf16[128,512]{1,0:T(8,128)(2,1)} %param.5) | copy-start | bytes 393220
where the time goes:
time: 195 us; the launch traced here: 193 us
  starting transfers between devices  68.8 us (35%)
  waiting for transfers between devices  57.2 us (29%)
  blocking collectives  27.7 us (14%)
  matrix products  19.7 us (10%)
  other arithmetic  11.2 us (6%)
  local copies, waits for them, and re-layouts  6.43 us (3%)
    ppermute x4, waiting for transfers between devices, swapped(): return lax.ppermute(array, PAIR, [(0, 1), (1, 0)])  46.1 us
    all_to_all x3, starting transfers between devices, to_all(): return lax.all_to_all(copies, axes, 0, 0, tiled=True)  25.6 us
    dot_general x12, matrix products, matmul(): lax.dot_general(left, right, (((left_dim,), (right_dim,)), ((), ())), pre...  19.7 us
    all_gather x1, blocking collectives, local(): images = lax.all_gather(img_unit, Z, axis=0, tiled=True)  17.4 us
    ppermute x3, starting transfers between devices, shifted(): return lax.ppermute(array, Z, [(k, (k + distance) % NZ) for k in range(NZ)])  13.5 us
    ppermute x4, starting transfers between devices, swapped(): return lax.ppermute(array, PAIR, [(0, 1), (1, 0)])  12.9 us
    psum x1, blocking collectives, local(): row_sum = lax.psum(row_part, Z)  10.2 us
    all_to_all x1, starting transfers between devices, local(): lax.all_to_all(head_part.reshape(NQ * NZ, padded, emb_width), SAME, 0, 0,...  9.68 us
  transfers between devices with their start and end apart: 12, of which 7 were waited for; matrix products, arithmetic and copies ran while one was open for 11% of the time, Pallas kernels for 0%

commit v1 on v0

--- a/solution.py
+++ b/solution.py
@@ -70,8 +70,7 @@
     txt_emb = text_embed.astype(jnp.float32)
     txt_inv = inv_norm(txt_emb)
     txt_unit = (txt_emb * txt_inv).astype(jnp.bfloat16)
-    txt_sent, partner_part = lax.optimization_barrier((txt_unit, partner_part))
-    texts = to_all(txt_sent, Y, NY).reshape(NY * rows, emb_width)
+    texts = lax.all_gather(txt_unit, Y, axis=0, tiled=True)
     returned = swapped(partner_part)
 
     img_emb = matmul(kept, head) + returned.astype(jnp.float32)
@@ -94,8 +93,8 @@
 
     img_part = matmul(coef, texts)
     txt_part = matmul(coef, images, 0, 0)
-    txt_grads = lax.all_to_all(
-        txt_part.astype(jnp.bfloat16).reshape(NY, rows, emb_width), Y, 0, 0, tiled=True
+    txt_sum = lax.psum_scatter(
+        txt_part.astype(jnp.bfloat16), Y, scatter_dimension=0, tiled=True
     )
     origin = jnp.uint32(0)
     img_sum = lax.dynamic_slice(
@@ -109,9 +108,8 @@
     partner_grad = swapped(img_emb_grad)
 
     head_part = matmul(kept, img_emb_grad, 0, 0) + matmul(taken, partner_grad, 0, 0)
-    head_part, txt_grads = lax.optimization_barrier((head_part.astype(jnp.bfloat16), txt_grads))
     head_grads = lax.all_to_all(
-        head_part.reshape(NQ * NZ, padded, emb_width), SAME, 0, 0, tiled=True
+        head_part.astype(jnp.bfloat16).reshape(NQ * NZ, padded, emb_width), SAME, 0, 0, tiled=True
     )
     kept_grad = matmul(img_emb_grad, head, 1, 1).astype(jnp.bfloat16)
     given_grad = swapped(matmul(partner_grad, head, 1, 1).astype(jnp.bfloat16))
@@ -119,12 +117,7 @@
         matmul(kept_grad, choice[:, :half], 1, 1) + matmul(given_grad, choice[:, half:], 1, 1)
     ).astype(jnp.bfloat16)
 
-    txt_own = lax.dynamic_slice(
-        txt_part, (a.astype(jnp.uint32) * rows, origin), (rows, emb_width)
-    )
-    ids = jnp.arange(NY, dtype=jnp.int32)[:, None, None]
-    others = jnp.where(ids == a, 0.0, txt_grads.astype(jnp.float32))
-    txt_unit_grad = scale * (jnp.sum(others, axis=0) + txt_own)
+    txt_unit_grad = scale * txt_sum.astype(jnp.float32)
     text_embed_grad = norm_backward(txt_emb, txt_inv, txt_unit_grad)
     image_head_grad = jnp.sum(head_grads.astype(jnp.float32), axis=0)[:block]
     return (image_features_grad, text_embed_grad, image_head_grad)

time: 195 us -> 184 us (0.944)
  starting transfers between devices: 68.8 us -> 55.3 us
  between operations: 1.57 us -> 15 us
  waiting for transfers between devices: 57.2 us -> 49.2 us
  local copies, waits for them, and re-layouts: 6.43 us -> 4.3 us
  matrix products: 19.7 us -> 21.8 us
    ppermute x4, waiting for transfers between devices: 46.1 us -> 39.1 us  [swapped(): return lax.ppermute(array, PAIR, [(0, 1), (1, 0)])]
    all_to_all x2 -> x1, starting transfers between devices: 16.9 us -> 10.8 us  [local(): lax.all_to_all(head_part.astype(jnp.bfloat16).reshape(NQ * NZ, padded, em...]
    all_to_all x3 -> x2, starting transfers between devices: 25.6 us -> 21.7 us  [to_all(): return lax.all_to_all(copies, axes, 0, 0, tiled=True)]
    all_to_all x2 -> x1, waiting for transfers between devices: 0.01 us -> 2.55 us  [local(): lax.all_to_all(head_part.astype(jnp.bfloat16).reshape(NQ * NZ, padded, em...]
    dot_general x12, matrix products: 19.7 us -> 21.8 us  [matmul(): lax.dot_general(left, right, (((left_dim,), (right_dim,)), ((), ())), pre...]
    ppermute x4, starting transfers between devices: 12.9 us -> 10.8 us  [swapped(): return lax.ppermute(array, PAIR, [(0, 1), (1, 0)])]
    broadcast_in_dim x3 -> x2, local copies, waits for them, and re-layouts: 3.55 us -> 1.58 us  [to_all(): copies = jnp.broadcast_to(array[None], (devices, *array.shape))]
    all_to_all x3 -> x2, waiting for transfers between devices: 5.39 us -> 3.7 us  [to_all(): return lax.all_to_all(copies, axes, 0, 0, tiled=True)]
  transfers between devices with their start and end apart: 12 -> 12, of which waited for: 7 -> 8; matrix products, arithmetic and copies ran while one was open for 11% -> 12% of each run, Pallas kernels for 0% -> 0%
where the time goes in v1:
time: 184 us; the launch traced here: 183 us
  starting transfers between devices  55.3 us (30%)
  waiting for transfers between devices  49.2 us (27%)
  blocking collectives  26.9 us (15%)
  matrix products  21.8 us (12%)
  between operations  15 us (8%)
  other arithmetic  10.6 us (6%)
  local copies, waits for them, and re-layouts  4.3 us (2%)
    ppermute x4, waiting for transfers between devices, swapped(): return lax.ppermute(array, PAIR, [(0, 1), (1, 0)])  39.1 us
    dot_general x12, matrix products, matmul(): lax.dot_general(left, right, (((left_dim,), (right_dim,)), ((), ())), pre...  21.8 us
    all_to_all x2, starting transfers between devices, to_all(): return lax.all_to_all(copies, axes, 0, 0, tiled=True)  21.7 us
    all_gather x1, blocking collectives, local(): images = lax.all_gather(img_unit, Z, axis=0, tiled=True)  16.4 us
    ppermute x3, starting transfers between devices, shifted(): return lax.ppermute(array, Z, [(k, (k + distance) % NZ) for k in range(NZ)])  11.9 us
    ppermute x4, starting transfers between devices, swapped(): return lax.ppermute(array, PAIR, [(0, 1), (1, 0)])  10.8 us
    all_to_all x1, starting transfers between devices, local(): lax.all_to_all(head_part.astype(jnp.bfloat16).reshape(NQ * NZ, padded, em...  10.8 us
    psum x1, blocking collectives, local(): row_sum = lax.psum(row_part, Z)  10.5 us
  transfers between devices with their start and end apart: 12, of which 8 were waited for; matrix products, arithmetic and copies ran while one was open for 12% of the time, Pallas kernels for 0%

profile of v1, /device:TPU:6, one launch (start us, length us, event | category | flops | bytes accessed | tf_op | source)
XLA Modules:
  0.0 183.1 jit_solution(1611113847971946091)
XLA Ops:
  7.2 0.0 copy-start
  7.2 0.0 copy-start.2
  7.2 0.9 pad.4
  8.1 1.0 broadcast_in_dim.16
  9.0 15.7 %all-to-all-start = ((bf16[16,48,512]{2,1,0:T(8,128)(2,1)}), bf16[16,48,512]{2,1,0:T(8,128)(2,1)S(1)}, u32[]{:S(2)}, u32[]{:S(2)}) async-start(bf16[16,48,512]{2,1,0:T(8,128)(2,1)} %broadcast_in_dim.16), calls=%async_computation | async-start | bytes 1572864 | tf_op jit(solution)/shard_map/all_to_all | solution.py:23
  24.7 0.0 all-gather.2.cloned.1.call-start
  24.8 0.0 copy-done.2
  24.8 0.1 fusion.15
  24.9 0.8 fusion.16
  25.7 0.0 all-gather.2.cloned.1.call-update
  25.7 1.8 iota_compare_fusion
  27.5 0.0 copy-done
  27.5 0.0 copy-start.1
  27.6 1.6 fusion.14
  29.1 2.6 %collective-permute-start = (bf16[128,768]{0,1:T(8,128)(2,1)}, bf16[128,768]{0,1:T(8,128)(2,1)}, u32[]{:S(2)}, u32[]{:S(2)}) collective-permute-start(bf16[128,768]{0,1:T(8,128)(2,1)} %fusion.14), channel_id=1, source_target_pairs={{0,4},{4,0},{1,5},{5,1},{2,6},{6,2},{3,7},{7,3},{8,12},{12,8},{9,1... | collective-permute-start | bytes 589832 | tf_op jit(solution)/shard_map/ppermute | solution.py:27
  31.7 0.0 copy-done.1
  31.7 1.6 fusion.13
  33.3 15.4 %collective-permute-done = bf16[128,768]{0,1:T(8,128)(2,1)} collective-permute-done((bf16[128,768]{0,1:T(8,128)(2,1)}, bf16[128,768]{0,1:T(8,128)(2,1)}, u32[]{:S(2)}, u32[]{:S(2)}) %collective-permute-start) | collective-permute-done | bytes 196640 | tf_op jit(solution)/shard_map/ppermute | solution.py:27
  48.7 3.7 %all-to-all-done = bf16[16,48,512]{2,1,0:T(8,128)(2,1)S(1)} async-done(((bf16[16,48,512]{2,1,0:T(8,128)(2,1)}), bf16[16,48,512]{2,1,0:T(8,128)(2,1)S(1)}, u32[]{:S(2)}, u32[]{:S(2)}) %all-to-all-start) | async-done | bytes 786464 | tf_op jit(solution)/shard_map/all_to_all | solution.py:23
  52.4 1.2 convolution_convert_fusion.3
  53.6 1.9 %collective-permute-start.1 = (bf16[128,512]{1,0:T(8,128)(2,1)S(1)}, bf16[128,512]{1,0:T(8,128)(2,1)S(1)}, u32[]{:S(2)}, u32[]{:S(2)}) collective-permute-start(bf16[128,512]{1,0:T(8,128)(2,1)S(1)} %convolution_convert_fusion.3), channel_id=1, source_target_pairs={{0,4},{4,0},{1,5},{5,1},{2,6},{6,2},{3,7},{7,3},{8,12},{12,8},{9,1... | collective-permute-start | bytes 393224 | tf_op jit(solution)/shard_map/ppermute | solution.py:27
  56.2 5.1 %collective-permute-done.1 = bf16[128,512]{1,0:T(8,128)(2,1)S(1)} collective-permute-done((bf16[128,512]{1,0:T(8,128)(2,1)S(1)}, bf16[128,512]{1,0:T(8,128)(2,1)S(1)}, u32[]{:S(2)}, u32[]{:S(2)}) %collective-permute-start.1) | collective-permute-done | bytes 131104 | tf_op jit(solution)/shard_map/ppermute | solution.py:27
  61.4 1.3 multiply_reduce_fusion.1
  62.7 0.1 multiply_convert_fusion
  62.8 16.4 %all_gather.6 = bf16[512,512]{1,0:T(8,128)(2,1)S(1)} all-gather(bf16[128,512]{1,0:T(8,128)(2,1)S(1)} %multiply_convert_fusion), channel_id=1, replica_groups=mesh['rep'=16,'dp_q'=4,'dp_pair'=2,'dp_z'=4] {'dp_z'}, dimensions={0}, use_global_device_ids=true | all-gather | bytes 655360 | tf_op jit(solution)/shard_map/all_gather | solution.py:79
  79.2 0.0 copy-start.4
  79.2 0.0 all-gather.2.cloned.1.call-done
  79.2 3.5 %fusion.46 = (f32[512]{0:T(512)S(1)}, f32[1024]{0:T(1024)S(1)}, f32[512,1024]{1,0:T(8,128)}) fusion(bf16[512,512]{1,0:T(8,128)(2,1)S(1)} %all_gather.6, bf16[1024,512]{1,0:T(8,128)(2,1)} %all-gather.2.cloned.1.call-done, f32[]{:T(128)} %bitcast.31), kind=kOutput, calls=%fused_computation.94 | convolution fusion | flops 538442240 | bytes 3676164 | tf_op jit(solution)/shard_map/dot_general | solution.py:16
  82.7 0.0 copy-done.4
  82.7 0.6 broadcast_in_dim.18
  83.4 6.0 %all-to-all-start.1 = ((f32[8,8,128]{2,1,0:T(8,128)}), f32[8,8,128]{2,1,0:T(8,128)S(1)}, u32[]{:S(2)}, u32[]{:S(2)}) async-start(f32[8,8,128]{2,1,0:T(8,128)} %broadcast_in_dim.18), calls=%async_computation.1 | async-start | bytes 65536 | tf_op jit(solution)/shard_map/all_to_all | solution.py:23
  89.4 0.0 reduce-scatter.2.cloned.1.call-start
  89.4 10.5 %psum.7 = f32[512]{0:T(512)S(1)} all-reduce(f32[512]{0:T(512)S(1)} %get-tuple-element.3), channel_id=1, replica_groups=mesh['rep'=16,'dp_q'=4,'dp_pair'=2,'dp_z'=4] {'dp_z'}, use_global_device_ids=true, to_apply=%region_3.4 | all-reduce | flops 512 | bytes 4096 | tf_op jit(solution)/shard_map/psum | solution.py:86
  99.9 0.0 all-to-all-done.1
  100.0 2.1 %subtract_convert_fusion = bf16[512,1024]{1,0:T(8,128)(2,1)S(1)} fusion(f32[512,1024]{1,0:T(8,128)} %get-tuple-element.14, s32[1024]{0:T(1024)S(1)} %iota_subtract_fusion, f32[1024]{0:T(1024)S(1)} %divide_bitcast_fusion, f32[512]{0:T(512)S(1)} %broadcast_divide_fusion, s32[512]{0:T(512)S(1)} %iota_subtract_fusion.1, pred[512]{0:T(512)(128)(4,1)S(1)} %get-tuple-element.15, ...), kind=kLoop, calls=%fused_computation.11 | loop fusion | flops 4194304 | bytes 3159040 | tf_op jit(solution)/shard_map/convert_element_type | solution.py:92
  102.1 0.0 copy-start.5
  102.1 3.0 %fusion.47 = f32[512,512]{1,0:T(8,128)} fusion(bf16[512,1024]{1,0:T(8,128)(2,1)S(1)} %subtract_convert_fusion, bf16[1024,512]{1,0:T(8,128)(2,1)} %all-gather.2.cloned.1.call-done), kind=kOutput, calls=%fused_computation.95 | convolution fusion | flops 536870912 | bytes 3145728 | tf_op jit(solution)/shard_map/dot_general | solution.py:16
  105.1 1.8 dynamic-slice_convert_fusion.2
  106.9 4.1 %collective-permute-start.2 = (bf16[128,512]{1,0:T(8,128)(2,1)}, bf16[128,512]{1,0:T(8,128)(2,1)S(1)}, u32[]{:S(2)}, u32[]{:S(2)}) collective-permute-start(bf16[128,512]{1,0:T(8,128)(2,1)} %get-tuple-element.5), channel_id=1, source_target_pairs={{0,3},{1,0},{2,1},{3,2},{4,7},{5,4},{6,5},{7,6},{8,11},{9,8},{10,9... | collective-permute-start | bytes 393224 | tf_op jit(solution)/shard_map/ppermute | solution.py:31
  111.0 4.4 %collective-permute-start.3 = (bf16[128,512]{1,0:T(8,128)(2,1)S(1)}, bf16[128,512]{1,0:T(8,128)(2,1)S(1)}, u32[]{:S(2)}, u32[]{:S(2)}) collective-permute-start(bf16[128,512]{1,0:T(8,128)(2,1)S(1)} %get-tuple-element.6), channel_id=1, source_target_pairs={{0,2},{1,3},{2,0},{3,1},{4,6},{5,7},{6,4},{7,5},{8,10},{9,11},{10,... | collective-permute-start | bytes 393224 | tf_op jit(solution)/shard_map/ppermute | solution.py:31
  115.3 3.4 %collective-permute-start.4 = (bf16[128,512]{1,0:T(8,128)(2,1)S(1)}, bf16[128,512]{1,0:T(8,128)(2,1)S(1)}, u32[]{:S(2)}, u32[]{:S(2)}) collective-permute-start(bf16[128,512]{1,0:T(8,128)(2,1)S(1)} %get-tuple-element.7), channel_id=1, source_target_pairs={{0,1},{1,2},{2,3},{3,0},{4,5},{5,6},{6,7},{7,4},{8,9},{9,10},{10,1... | collective-permute-start | bytes 393224 | tf_op jit(solution)/shard_map/ppermute | solution.py:31
  118.8 0.0 copy-done.5
  118.8 1.7 convolution_convert_fusion
  120.5 0.0 reduce-scatter.2.cloned.1.call-update
  120.5 0.0 collective-permute-done.2
  120.6 2.2 %collective-permute-done.3 = bf16[128,512]{1,0:T(8,128)(2,1)S(1)} collective-permute-done((bf16[128,512]{1,0:T(8,128)(2,1)S(1)}, bf16[128,512]{1,0:T(8,128)(2,1)S(1)}, u32[]{:S(2)}, u32[]{:S(2)}) %collective-permute-start.3) | collective-permute-done | bytes 131104 | tf_op jit(solution)/shard_map/ppermute | solution.py:31
  122.8 1.6 collective-permute-done.4
  124.4 1.1 multiply_reduce_fusion
  125.5 1.1 subtract_convert_fusion.1
  126.6 3.9 %collective-permute-start.5 = (bf16[128,512]{1,0:T(8,128)(2,1)S(1)}, bf16[128,512]{1,0:T(8,128)(2,1)S(1)}, u32[]{:S(2)}, u32[]{:S(2)}) collective-permute-start(bf16[128,512]{1,0:T(8,128)(2,1)S(1)} %subtract_convert_fusion.1), channel_id=1, source_target_pairs={{0,4},{4,0},{1,5},{5,1},{2,6},{6,2},{3,7},{7,3},{8,12},{12,8},{9,1... | collective-permute-start | bytes 393224 | tf_op jit(solution)/shard_map/ppermute | solution.py:27
  130.5 0.0 copy-done.3
  130.5 0.3 fusion.48
  130.8 2.6 %collective-permute-done.5 = bf16[128,512]{1,0:T(8,128)(2,1)S(1)} collective-permute-done((bf16[128,512]{1,0:T(8,128)(2,1)S(1)}, bf16[128,512]{1,0:T(8,128)(2,1)S(1)}, u32[]{:S(2)}, u32[]{:S(2)}) %collective-permute-start.5) | collective-permute-done | bytes 131104 | tf_op jit(solution)/shard_map/ppermute | solution.py:27
  133.5 2.1 %add_convert_fusion = bf16[768,512]{1,0:T(8,128)(2,1)} fusion(f32[768,512]{1,0:T(8,128)S(1)} %fusion.48, bf16[128,768]{0,1:T(8,128)(2,1)} %collective-permute-done, bf16[128,512]{1,0:T(8,128)(2,1)S(1)} %collective-permute-done.5), kind=kOutput, calls=%fused_computation.14 | convolution fusion | flops 101449728 | bytes 2686976 | tf_op jit(solution)/shard_map/dot_general | solution.py:16
  135.6 10.8 %all-to-all-start.2 = ((bf16[16,48,512]{2,1,0:T(8,128)(2,1)}), bf16[16,48,512]{2,1,0:T(8,128)(2,1)S(1)}, u32[]{:S(2)}, u32[]{:S(2)}) async-start(bf16[16,48,512]{2,1,0:T(8,128)(2,1)} %bitcast.5), calls=%async_computation.3 | async-start | bytes 1572864 | tf_op jit(solution)/shard_map/all_to_all | solution.py:111
  146.4 0.4 convolution_convert_fusion.1
  146.8 2.5 %collective-permute-start.6 = (bf16[128,768]{1,0:T(8,128)(2,1)S(1)}, bf16[128,768]{1,0:T(8,128)(2,1)S(1)}, u32[]{:S(2)}, u32[]{:S(2)}) collective-permute-start(bf16[128,768]{1,0:T(8,128)(2,1)S(1)} %convolution_convert_fusion.1), channel_id=1, source_target_pairs={{0,4},{4,0},{1,5},{5,1},{2,6},{6,2},{3,7},{7,3},{8,12},{12,8},{9,1... | collective-permute-start | bytes 589832 | tf_op jit(solution)/shard_map/ppermute | solution.py:27
  149.3 2.2 %fusion.2 = f32[128,1408]{1,0:T(8,128)S(1)} fusion(pred[1408,1536]{1,0:T(32,128)(4,1)} %copy-done.1, bf16[128,512]{1,0:T(8,128)(2,1)S(1)} %subtract_convert_fusion.1, bf16[768,512]{1,0:T(8,128)(2,1)S(1)} %bitcast.38), kind=kOutput, calls=%fused_computation.4 | convolution fusion | flops 377585664 | bytes 2719744 | tf_op jit(solution)/shard_map/dot_general | solution.py:16
  151.5 15.9 %collective-permute-done.6 = bf16[128,768]{1,0:T(8,128)(2,1)S(1)} collective-permute-done((bf16[128,768]{1,0:T(8,128)(2,1)S(1)}, bf16[128,768]{1,0:T(8,128)(2,1)S(1)}, u32[]{:S(2)}, u32[]{:S(2)}) %collective-permute-start.6) | collective-permute-done | bytes 196640 | tf_op jit(solution)/shard_map/ppermute | solution.py:27
  167.5 2.8 %fusion.7 = bf16[128,1408]{1,0:T(8,128)(2,1)} fusion(f32[128,1408]{1,0:T(8,128)S(1)} %fusion.2, bf16[128,768]{1,0:T(8,128)(2,1)S(1)} %collective-permute-done.6, pred[1408,1536]{1,0:T(32,128)(4,1)} %copy-done.1), kind=kOutput, calls=%fused_computation.8 | convolution fusion | flops 277184512 | bytes 2359296 | tf_op jit(solution)/shard_map/dot_general | solution.py:16
  170.3 2.5 %all-to-all-done.2 = bf16[16,48,512]{2,1,0:T(8,128)(2,1)S(1)} async-done(((bf16[16,48,512]{2,1,0:T(8,128)(2,1)}), bf16[16,48,512]{2,1,0:T(8,128)(2,1)S(1)}, u32[]{:S(2)}, u32[]{:S(2)}) %all-to-all-start.2) | async-done | bytes 786464 | tf_op jit(solution)/shard_map/all_to_all | solution.py:111
  172.8 0.8 convert_reduce_fusion
  173.6 1.0 fusion.20
  174.6 1.7 fusion.19
  (11 shorter events, 0.1 us)
Async XLA Ops:
  7.2 20.4 %copy-start = (bf16[128,1408]{1,0:T(8,128)(2,1)S(1)}, bf16[128,1408]{1,0:T(8,128)(2,1)}, u32[]{:S(2)}) copy-start(bf16[128,1408]{1,0:T(8,128)(2,1)} %param.4) | copy-start | bytes 1081348
  7.2 17.6 %copy-start.2 = (bf16[128,512]{1,0:T(8,128)(2,1)S(1)}, bf16[128,512]{1,0:T(8,128)(2,1)}, u32[]{:S(2)}) copy-start(bf16[128,512]{1,0:T(8,128)(2,1)} %param.5) | copy-start | bytes 393220
  9.0 43.4 %all-to-all-start = ((bf16[16,48,512]{2,1,0:T(8,128)(2,1)}), bf16[16,48,512]{2,1,0:T(8,128)(2,1)S(1)}, u32[]{:S(2)}, u32[]{:S(2)}) async-start(bf16[16,48,512]{2,1,0:T(8,128)(2,1)} %broadcast_in_dim.16), calls=%async_computation | async-start | bytes 1572864 | tf_op jit(solution)/shard_map/all_to_all | solution.py:23
  24.7 54.5 %all-gather.2.cloned.1.call-start = ((), (), s32[]{:S(2)}) async-start(), calls=%async_computation.4 | async-start | bytes 1179648 | tf_op jit(solution)/shard_map/all_gather | solution.py:73
  27.5 4.2 %copy-start.1 = (pred[1408,1536]{1,0:T(32,128)(4,1)}, pred[1408,1536]{1,0:T(32,128)(4,1)S(1)}, u32[]{:S(2)}) copy-start(pred[1408,1536]{1,0:T(32,128)(4,1)S(1)} %iota_compare_fusion) | copy-start | bytes 6488068
  29.1 19.6 %collective-permute-start = (bf16[128,768]{0,1:T(8,128)(2,1)}, bf16[128,768]{0,1:T(8,128)(2,1)}, u32[]{:S(2)}, u32[]{:S(2)}) collective-permute-start(bf16[128,768]{0,1:T(8,128)(2,1)} %fusion.14), channel_id=1, source_target_pairs={{0,4},{4,0},{1,5},{5,1},{2,6},{6,2},{3,7},{7,3},{8,12},{12,8},{9,1... | collective-permute-start | bytes 589832 | tf_op jit(solution)/shard_map/ppermute | solution.py:27
  53.6 7.7 %collective-permute-start.1 = (bf16[128,512]{1,0:T(8,128)(2,1)S(1)}, bf16[128,512]{1,0:T(8,128)(2,1)S(1)}, u32[]{:S(2)}, u32[]{:S(2)}) collective-permute-start(bf16[128,512]{1,0:T(8,128)(2,1)S(1)} %convolution_convert_fusion.3), channel_id=1, source_target_pairs={{0,4},{4,0},{1,5},{5,1},{2,6},{6,2},{3,7},{7,3},{8,12},{12,8},{9,1... | collective-permute-start | bytes 393224 | tf_op jit(solution)/shard_map/ppermute | solution.py:27
  79.2 3.5 %copy-start.4 = (bf16[512,512]{1,0:T(8,128)(2,1)}, bf16[512,512]{1,0:T(8,128)(2,1)S(1)}, u32[]{:S(2)}) copy-start(bf16[512,512]{1,0:T(8,128)(2,1)S(1)} %all_gather.6) | copy-start | bytes 1572868
  83.4 16.6 %all-to-all-start.1 = ((f32[8,8,128]{2,1,0:T(8,128)}), f32[8,8,128]{2,1,0:T(8,128)S(1)}, u32[]{:S(2)}, u32[]{:S(2)}) async-start(f32[8,8,128]{2,1,0:T(8,128)} %broadcast_in_dim.18), calls=%async_computation.1 | async-start | bytes 65536 | tf_op jit(solution)/shard_map/all_to_all | solution.py:23
  89.4 84.2 %reduce-scatter.2.cloned.1.call-start = ((), (), s32[]{:S(2)}) async-start(), calls=%async_computation.5 | async-start | bytes 1179648 | tf_op jit(solution)/shard_map/reduce_scatter | solution.py:96
  102.1 16.7 %copy-start.5 = (bf16[512,512]{1,0:T(8,128)(2,1)S(1)}, bf16[512,512]{1,0:T(8,128)(2,1)}, u32[]{:S(2)}) copy-start(bf16[512,512]{1,0:T(8,128)(2,1)} %copy-done.4) | copy-start | bytes 1572868
  106.9 13.7 %collective-permute-start.2 = (bf16[128,512]{1,0:T(8,128)(2,1)}, bf16[128,512]{1,0:T(8,128)(2,1)S(1)}, u32[]{:S(2)}, u32[]{:S(2)}) collective-permute-start(bf16[128,512]{1,0:T(8,128)(2,1)} %get-tuple-element.5), channel_id=1, source_target_pairs={{0,3},{1,0},{2,1},{3,2},{4,7},{5,4},{6,5},{7,6},{8,11},{9,8},{10,9... | collective-permute-start | bytes 393224 | tf_op jit(solution)/shard_map/ppermute | solution.py:31
  111.0 11.8 %collective-permute-start.3 = (bf16[128,512]{1,0:T(8,128)(2,1)S(1)}, bf16[128,512]{1,0:T(8,128)(2,1)S(1)}, u32[]{:S(2)}, u32[]{:S(2)}) collective-permute-start(bf16[128,512]{1,0:T(8,128)(2,1)S(1)} %get-tuple-element.6), channel_id=1, source_target_pairs={{0,2},{1,3},{2,0},{3,1},{4,6},{5,7},{6,4},{7,5},{8,10},{9,11},{10,... | collective-permute-start | bytes 393224 | tf_op jit(solution)/shard_map/ppermute | solution.py:31
  115.3 9.0 %collective-permute-start.4 = (bf16[128,512]{1,0:T(8,128)(2,1)S(1)}, bf16[128,512]{1,0:T(8,128)(2,1)S(1)}, u32[]{:S(2)}, u32[]{:S(2)}) collective-permute-start(bf16[128,512]{1,0:T(8,128)(2,1)S(1)} %get-tuple-element.7), channel_id=1, source_target_pairs={{0,1},{1,2},{2,3},{3,0},{4,5},{5,6},{6,7},{7,4},{8,9},{9,10},{10,1... | collective-permute-start | bytes 393224 | tf_op jit(solution)/shard_map/ppermute | solution.py:31
  120.5 10.0 %copy-start.3 = (bf16[768,128]{1,0:T(8,128)(2,1)S(1)}, bf16[768,128]{1,0:T(8,128)(2,1)}, u32[]{:S(2)}) copy-start(bf16[768,128]{1,0:T(8,128)(2,1)} %fusion.13) | copy-start | bytes 589828
  126.6 6.9 %collective-permute-start.5 = (bf16[128,512]{1,0:T(8,128)(2,1)S(1)}, bf16[128,512]{1,0:T(8,128)(2,1)S(1)}, u32[]{:S(2)}, u32[]{:S(2)}) collective-permute-start(bf16[128,512]{1,0:T(8,128)(2,1)S(1)} %subtract_convert_fusion.1), channel_id=1, source_target_pairs={{0,4},{4,0},{1,5},{5,1},{2,6},{6,2},{3,7},{7,3},{8,12},{12,8},{9,1... | collective-permute-start | bytes 393224 | tf_op jit(solution)/shard_map/ppermute | solution.py:27
  135.6 37.2 %all-to-all-start.2 = ((bf16[16,48,512]{2,1,0:T(8,128)(2,1)}), bf16[16,48,512]{2,1,0:T(8,128)(2,1)S(1)}, u32[]{:S(2)}, u32[]{:S(2)}) async-start(bf16[16,48,512]{2,1,0:T(8,128)(2,1)} %bitcast.5), calls=%async_computation.3 | async-start | bytes 1572864 | tf_op jit(solution)/shard_map/all_to_all | solution.py:111
  146.8 20.7 %collective-permute-start.6 = (bf16[128,768]{1,0:T(8,128)(2,1)S(1)}, bf16[128,768]{1,0:T(8,128)(2,1)S(1)}, u32[]{:S(2)}, u32[]{:S(2)}) collective-permute-start(bf16[128,768]{1,0:T(8,128)(2,1)S(1)} %convolution_convert_fusion.1), channel_id=1, source_target_pairs={{0,4},{4,0},{1,5},{5,1},{2,6},{6,2},{3,7},{7,3},{8,12},{12,8},{9,1... | collective-permute-start | bytes 589832 | tf_op jit(solution)/shard_map/ppermute | solution.py:27
Sparse Core Ops, SparseCore 0:
  28.2 42.2 all-gather.1
  120.7 45.8 reduce-scatter.1

commit v2 on v1

v2 whole, which is shorter than its diff:
```python
import jax
import jax.numpy as jnp
from jax import lax
from jax.sharding import Mesh
from jax.sharding import PartitionSpec as P


NQ, NP, NZ = 4, 2, 4
NY = NQ * NP
Q, PAIR, Z = "dp_q", "dp_pair", "dp_z"
Y = (Q, PAIR)
SAME = (Q, Z)


def matmul(left, right, left_dim=1, right_dim=0):
    return lax.dot_general(
        left, right, (((left_dim,), (right_dim,)), ((), ())), preferred_element_type=jnp.float32
    )


def to_all(array, axes, devices):
    copies = jnp.broadcast_to(array[None], (devices, *array.shape))
    return lax.all_to_all(copies, axes, 0, 0, tiled=True)


def swapped(array):
    return lax.ppermute(array, PAIR, [(0, 1), (1, 0)])


def shifted(array, distance):
    return lax.ppermute(array, Z, [(k, (k + distance) % NZ) for k in range(NZ)])


def inv_norm(embedding):
    return lax.rsqrt(jnp.sum(embedding * embedding, axis=1, keepdims=True) + 1e-06)


def norm_backward(embedding, inv, upstream):
    inner = jnp.sum(embedding * upstream, axis=1, keepdims=True)
    return (inv * upstream - embedding * (inv * inv * inv) * inner).astype(jnp.bfloat16)


def column_choice(width, padded, block):
    shape = (width, NP * NQ * NZ * padded)
    col = lax.broadcasted_iota(jnp.int32, (1, shape[1]), 1)
    place, c = col // padded, col % padded
    owner = (place // NZ % NQ * NP + place // (NQ * NZ)) * NZ + place % NZ
    source = jnp.where(c < block, owner * block + c, -1)
    return (lax.broadcasted_iota(jnp.int32, shape, 0) == source).astype(jnp.bfloat16)


def rows_of(array, index, rows):
    start = index.astype(jnp.uint32) * rows
    return lax.dynamic_slice(array, (start, jnp.uint32(0)), (rows, array.shape[1]))


def local(image_features, text_embed, image_head, logit_scale):
    scale = logit_scale[0]
    rows, width = image_features.shape
    block, emb_width = image_head.shape
    padded = -(-block // 16) * 16
    half = NQ * NZ * padded
    p, b = lax.axis_index(PAIR), lax.axis_index(Z)
    a = lax.axis_index(Y)
    below = [(b + NZ - k) & (NZ - 1) for k in range(NZ)]

    head = to_all(jnp.pad(image_head, ((0, padded - block), (0, 0))), SAME, NQ * NZ)
    head = head.reshape(half, emb_width)
    choice = column_choice(width, padded, block)
    own_features = matmul(image_features, choice).astype(jnp.bfloat16)
    first, second = own_features[:, :half], own_features[:, half:]
    kept, given = jnp.where(p == 0, first, second), jnp.where(p == 0, second, first)
    taken = swapped(given)
    features = jnp.concatenate([own_features] + [shifted(own_features, k) for k in range(1, NZ)])
    partner_part = matmul(taken, head).astype(jnp.bfloat16)

    txt_emb = text_embed.astype(jnp.float32)
    txt_inv = inv_norm(txt_emb)
    txt_unit = (txt_emb * txt_inv).astype(jnp.bfloat16)
    texts = lax.all_gather(txt_unit, Y, axis=0, tiled=True)
    returned = swapped(partner_part)
    other_head = swapped(head)

    img_emb = matmul(kept, head) + returned.astype(jnp.float32)
    img_inv = inv_norm(img_emb)
    img_unit = (img_emb * img_inv).astype(jnp.bfloat16)
    images = lax.all_gather(img_unit, Z, axis=0, tiled=True)

    exps = jnp.exp(scale * matmul(images, texts, 1, 1))
    row_part = jnp.sum(exps, axis=1)
    col_part = jnp.sum(exps, axis=0)
    col_parts = to_all(col_part.reshape(NY, rows), Y, NY)
    col_sum = jnp.sum(col_parts, axis=0).reshape(NY * rows)
    own_slot = (jnp.arange(NZ, dtype=jnp.int32) == b)[:, None]
    inv_slots = jnp.where(own_slot, img_inv.reshape(1, rows), 0.0)
    both = lax.psum(jnp.concatenate([row_part, inv_slots.reshape(NZ * rows)]), Z)
    row_sum, inv_all = both[: NZ * rows], both[NZ * rows :].reshape(NZ * rows, 1)

    i = lax.broadcasted_iota(jnp.int32, exps.shape, 0) - b * rows
    j = lax.broadcasted_iota(jnp.int32, exps.shape, 1) - a * rows
    label = jnp.where((i == j) & (i >= 0) & (i < rows), 2.0, 0.0)
    coef = exps * ((1.0 / row_sum)[:, None] + (1.0 / col_sum)[None, :])
    coef = (coef - label).astype(jnp.bfloat16)

    txt_part = matmul(coef, images, 0, 0).astype(jnp.bfloat16)
    coef, txt_part = lax.optimization_barrier((coef, txt_part))
    txt_sum = lax.psum_scatter(txt_part, Y, scatter_dimension=0, tiled=True)

    img_part = scale * matmul(coef, texts)
    units = images.astype(jnp.float32)
    inner = jnp.sum(units * img_part, axis=1, keepdims=True)
    grad_part = (inv_all * (img_part - units * inner)).astype(jnp.bfloat16)
    grad_part = jnp.concatenate([rows_of(grad_part, below[k], rows) for k in range(NZ)])
    head_part = matmul(features, grad_part, 0, 0).astype(jnp.bfloat16)
    head_grads = lax.all_to_all(
        head_part.reshape(NP * NQ * NZ, padded, emb_width), (PAIR, Q, Z), 0, 0, tiled=True
    )

    img_sum = rows_of(img_part, b, rows)
    for k in range(1, NZ):
        piece = rows_of(img_part, below[k], rows).astype(jnp.bfloat16)
        received = shifted(piece, -k)
        img_sum = img_sum + received.astype(jnp.float32)
    img_emb_grad = norm_backward(img_emb, img_inv, img_sum)
    first = matmul(img_emb_grad, jnp.where(p == 0, head, other_head), 1, 1)
    second = matmul(img_emb_grad, jnp.where(p == 0, other_head, head), 1, 1)
    feat_grad = jnp.concatenate([first, second], axis=1).astype(jnp.bfloat16)
    image_features_grad = matmul(feat_grad, choice, 1, 1).astype(jnp.bfloat16)

    text_embed_grad = norm_backward(txt_emb, txt_inv, scale * txt_sum.astype(jnp.float32))
    image_head_grad = jnp.sum(head_grads.astype(jnp.float32), axis=0)[:block]
    return (image_features_grad, text_embed_grad, image_head_grad)


def solution(mesh):
    split = Mesh(mesh.devices.reshape(mesh.shape["rep"], NQ, NP, NZ), ("rep", Q, PAIR, Z))
    spec = P(("rep", Q, PAIR, Z), None)

    return jax.shard_map(
        local,
        mesh=split,
        in_specs=(spec, spec, spec, P(None)),
        out_specs=(spec, spec, spec),
        check_vma=False,
    )
```

time: 184 us -> 211 us (1.15)
  blocking collectives: 26.9 us -> 43.7 us
  starting transfers between devices: 55.3 us -> 69.4 us
  matrix products: 21.8 us -> 19.2 us
  waiting for transfers between devices: 49.2 us -> 47 us
    ppermute x3 -> x6, waiting for transfers between devices: 3.84 us -> 26.1 us  [shifted(): return lax.ppermute(array, Z, [(k, (k + distance) % NZ) for k in range(NZ)])]
    ppermute x4 -> x3, waiting for transfers between devices: 39.1 us -> 17.2 us  [swapped(): return lax.ppermute(array, PAIR, [(0, 1), (1, 0)])]
    ppermute x3 -> x6, starting transfers between devices: 11.9 us -> 29.7 us  [shifted(): return lax.ppermute(array, Z, [(k, (k + distance) % NZ) for k in range(NZ)])]
    all_gather x1, blocking collectives: 16.4 us -> 30.6 us  [local(): images = lax.all_gather(img_unit, Z, axis=0, tiled=True)]
    ppermute x4 -> x3, starting transfers between devices: 10.8 us -> 8.21 us  [swapped(): return lax.ppermute(array, PAIR, [(0, 1), (1, 0)])]
    dot_general x12 -> x10, matrix products: 21.8 us -> 19.2 us  [matmul(): lax.dot_general(left, right, (((left_dim,), (right_dim,)), ((), ())), pre...]
    psum x1, blocking collectives: 10.5 us -> 13.1 us  [local(): lax.psum(jnp.concatenate([row_part, inv_slots.reshape(NZ * rows)]), Z)]
    all_to_all x1, waiting for transfers between devices: 2.55 us -> 0.01 us  [local(): lax.all_to_all(head_part.reshape(NP * NQ * NZ, padded, emb_width), (PAIR,...]
  transfers between devices with their start and end apart: 12 -> 14, of which waited for: 8 -> 7; matrix products, arithmetic and copies ran while one was open for 12% -> 13% of each run, Pallas kernels for 0% -> 0%
where the time goes in v2:
time: 211 us; the launch traced here: 208 us
  starting transfers between devices  69.4 us (33%)
  waiting for transfers between devices  47 us (22%)
  blocking collectives  43.7 us (21%)
  matrix products  19.2 us (9%)
  between operations  15 us (7%)
  other arithmetic  10.5 us (5%)
  local copies, waits for them, and re-layouts  3.25 us (2%)
    all_gather x1, blocking collectives, local(): images = lax.all_gather(img_unit, Z, axis=0, tiled=True)  30.6 us
    ppermute x6, starting transfers between devices, shifted(): return lax.ppermute(array, Z, [(k, (k + distance) % NZ) for k in range(NZ)])  29.7 us
    ppermute x6, waiting for transfers between devices, shifted(): return lax.ppermute(array, Z, [(k, (k + distance) % NZ) for k in range(NZ)])  26.1 us
    all_to_all x2, starting transfers between devices, to_all(): return lax.all_to_all(copies, axes, 0, 0, tiled=True)  21.5 us
    dot_general x10, matrix products, matmul(): lax.dot_general(left, right, (((left_dim,), (right_dim,)), ((), ())), pre...  19.2 us
    ppermute x3, waiting for transfers between devices, swapped(): return lax.ppermute(array, PAIR, [(0, 1), (1, 0)])  17.2 us
    psum x1, blocking collectives, local(): lax.psum(jnp.concatenate([row_part, inv_slots.reshape(NZ * rows)]), Z)  13.1 us
    all_to_all x1, starting transfers between devices, local(): lax.all_to_all(head_part.reshape(NP * NQ * NZ, padded, emb_width), (PAIR,...  9.92 us
  transfers between devices with their start and end apart: 14, of which 7 were waited for; matrix products, arithmetic and copies ran while one was open for 13% of the time, Pallas kernels for 0%

profile of v2, /device:TPU:6, one launch (start us, length us, event | category | flops | bytes accessed | tf_op | source)
XLA Modules:
  0.0 208.1 jit_solution(4023518978058816642)
XLA Ops:
  7.2 0.0 copy-start
  7.2 0.9 pad.4
  8.0 1.0 broadcast_in_dim.51
  9.0 15.7 %all-to-all-start = ((bf16[16,48,512]{2,1,0:T(8,128)(2,1)}), bf16[16,48,512]{2,1,0:T(8,128)(2,1)S(1)}, u32[]{:S(2)}, u32[]{:S(2)}) async-start(bf16[16,48,512]{2,1,0:T(8,128)(2,1)} %broadcast_in_dim.51), calls=%async_computation | async-start | bytes 1572864 | tf_op jit(solution)/shard_map/all_to_all | solution.py:23
  24.7 0.0 all-gather.2.cloned.1.call-start
  24.8 0.0 copy-done
  24.8 0.0 copy-start.3
  24.8 2.4 %fusion.6 = bf16[128,1536]{1,0:T(8,128)(2,1)} fusion(bf16[128,1408]{1,0:T(8,128)(2,1)S(1)} %copy-done, s32[1536]{0:T(1024)S(1)} %fusion.56), kind=kOutput, calls=%fused_computation.9 | convolution fusion | flops 556007424 | bytes 759808 | tf_op jit(solution)/shard_map/dot_general | solution.py:16
  27.2 5.9 %collective-permute-start.8 = (bf16[128,1536]{1,0:T(8,128)(2,1)}, bf16[128,1536]{1,0:T(8,128)(2,1)}, u32[]{:S(2)}, u32[]{:S(2)}) collective-permute-start(bf16[128,1536]{1,0:T(8,128)(2,1)} %fusion.6), channel_id=1, source_target_pairs={{0,3},{1,0},{2,1},{3,2},{4,7},{5,4},{6,5},{7,6},{8,11},{9,8},{10,9... | collective-permute-start | bytes 1179656 | tf_op jit(solution)/shard_map/ppermute | solution.py:31
  33.1 4.3 %collective-permute-start.7 = (bf16[128,1536]{1,0:T(8,128)(2,1)}, bf16[128,1536]{1,0:T(8,128)(2,1)}, u32[]{:S(2)}, u32[]{:S(2)}) collective-permute-start(bf16[128,1536]{1,0:T(8,128)(2,1)} %fusion.6), channel_id=1, source_target_pairs={{0,2},{1,3},{2,0},{3,1},{4,6},{5,7},{6,4},{7,5},{8,10},{9,11},{10,... | collective-permute-start | bytes 1179656 | tf_op jit(solution)/shard_map/ppermute | solution.py:31
  37.4 4.3 %collective-permute-start.6 = (bf16[128,1536]{1,0:T(8,128)(2,1)}, bf16[128,1536]{1,0:T(8,128)(2,1)}, u32[]{:S(2)}, u32[]{:S(2)}) collective-permute-start(bf16[128,1536]{1,0:T(8,128)(2,1)} %fusion.6), channel_id=1, source_target_pairs={{0,1},{1,2},{2,3},{3,0},{4,5},{5,6},{6,7},{7,4},{8,9},{9,10},{10,1... | collective-permute-start | bytes 1179656 | tf_op jit(solution)/shard_map/ppermute | solution.py:31
  41.7 1.0 broadcast_select_fusion
  42.7 2.6 %collective-permute-start = (bf16[128,768]{1,0:T(8,128)(2,1)S(1)}, bf16[128,768]{1,0:T(8,128)(2,1)S(1)}, u32[]{:S(2)}, u32[]{:S(2)}) collective-permute-start(bf16[128,768]{1,0:T(8,128)(2,1)S(1)} %broadcast_select_fusion), channel_id=1, source_target_pairs={{0,4},{4,0},{1,5},{5,1},{2,6},{6,2},{3,7},{7,3},{8,12},{12,8},{9,1... | collective-permute-start | bytes 589832 | tf_op jit(solution)/shard_map/ppermute | solution.py:27
  45.3 0.0 copy-done.3
  45.3 0.1 fusion.32
  45.5 0.8 fusion.33
  46.2 0.0 all-gather.2.cloned.1.call-update
  46.3 4.0 %collective-permute-done = bf16[128,768]{1,0:T(8,128)(2,1)S(1)} collective-permute-done((bf16[128,768]{1,0:T(8,128)(2,1)S(1)}, bf16[128,768]{1,0:T(8,128)(2,1)S(1)}, u32[]{:S(2)}, u32[]{:S(2)}) %collective-permute-start) | collective-permute-done | bytes 196640 | tf_op jit(solution)/shard_map/ppermute | solution.py:27
  50.3 3.0 %all-to-all-done = bf16[16,48,512]{2,1,0:T(8,128)(2,1)S(1)} async-done(((bf16[16,48,512]{2,1,0:T(8,128)(2,1)}), bf16[16,48,512]{2,1,0:T(8,128)(2,1)S(1)}, u32[]{:S(2)}, u32[]{:S(2)}) %all-to-all-start) | async-done | bytes 786464 | tf_op jit(solution)/shard_map/all_to_all | solution.py:23
  53.3 0.0 copy-start.1
  53.3 0.3 convolution_convert_fusion.4
  53.6 1.9 collective-permute-start.1
  56.2 5.0 %collective-permute-done.1 = bf16[128,512]{1,0:T(8,128)(2,1)S(1)} collective-permute-done((bf16[128,512]{1,0:T(8,128)(2,1)S(1)}, bf16[128,512]{1,0:T(8,128)(2,1)S(1)}, u32[]{:S(2)}, u32[]{:S(2)}) %collective-permute-start.1) | collective-permute-done | bytes 131104 | tf_op jit(solution)/shard_map/ppermute | solution.py:27
  61.2 1.4 multiply_reduce_fusion.1
  62.6 0.1 multiply_convert_fusion
  62.7 30.6 %all_gather.6 = bf16[512,512]{1,0:T(8,128)(2,1)S(1)} all-gather(bf16[128,512]{1,0:T(8,128)(2,1)S(1)} %multiply_convert_fusion), channel_id=1, replica_groups=mesh['rep'=16,'dp_q'=4,'dp_pair'=2,'dp_z'=4] {'dp_z'}, dimensions={0}, use_global_device_ids=true | all-gather | bytes 655360 | tf_op jit(solution)/shard_map/all_gather | solution.py:87
  93.4 0.1 select_bitcast_fusion
  93.4 3.4 %fusion.68 = (f32[512]{0:T(512)S(1)}, f32[1024]{0:T(1024)S(1)}, f32[512,1024]{1,0:T(8,128)}) fusion(bf16[512,512]{1,0:T(8,128)(2,1)S(1)} %all_gather.6, bf16[1024,512]{1,0:T(8,128)(2,1)} %all-gather.2.cloned.1.call-done, f32[]{:T(128)} %bitcast.24), kind=kOutput, calls=%fused_computation.126 | convolution fusion | flops 538442240 | bytes 3676164 | tf_op jit(solution)/shard_map/dot_general | solution.py:16
  96.8 0.0 copy-done.1
  96.8 0.6 broadcast_in_dim.56
  97.4 5.8 %all-to-all-start.1 = ((f32[8,8,128]{2,1,0:T(8,128)}), f32[8,8,128]{2,1,0:T(8,128)S(1)}, u32[]{:S(2)}, u32[]{:S(2)}) async-start(f32[8,8,128]{2,1,0:T(8,128)} %broadcast_in_dim.56), calls=%async_computation.1 | async-start | bytes 65536 | tf_op jit(solution)/shard_map/all_to_all | solution.py:23
  103.2 13.1 %psum.7 = f32[1024]{0:T(1024)S(1)} all-reduce(f32[1024]{0:T(1024)S(1)} %pad_maximum_fusion), channel_id=1, replica_groups=mesh['rep'=16,'dp_q'=4,'dp_pair'=2,'dp_z'=4] {'dp_z'}, use_global_device_ids=true, to_apply=%region_3.4 | all-reduce | flops 1024 | bytes 8192 | tf_op jit(solution)/shard_map/psum | solution.py:96
  116.3 0.0 all-to-all-done.1
  116.4 2.1 %subtract_convert_fusion = bf16[512,1024]{1,0:T(8,128)(2,1)S(1)} fusion(f32[512,1024]{1,0:T(8,128)} %get-tuple-element.24, s32[1024]{0:T(1024)S(1)} %iota_subtract_fusion, f32[1024]{0:T(1024)S(1)} %divide_bitcast_fusion, f32[512]{0:T(512)S(1)} %get-tuple-element.17, s32[512]{0:T(512)S(1)} %iota_subtract_fusion.1, pred[512]{0:T(512)(128)(4,1)S(1)} %get-tuple-element.27, ...), kind=kLoop, calls=%fused_computation.10 | loop fusion | flops 4194304 | bytes 3159040 | tf_op jit(solution)/shard_map/convert_element_type | solution.py:103
  118.5 1.7 convolution_convert_fusion.1
  120.2 2.0 fusion.14
  122.2 0.3 fusion.17
  122.5 0.0 collective-permute-done.8
  122.6 0.0 collective-permute-done.7
  122.6 0.0 collective-permute-done.6
  122.6 3.5 %convolution_convert_fusion = bf16[1536,512]{1,0:T(8,128)(2,1)} fusion(bf16[128,1536]{1,0:T(8,128)(2,1)} %collective-permute-done.8, bf16[128,1536]{1,0:T(8,128)(2,1)} %collective-permute-done.7, bf16[128,1536]{1,0:T(8,128)(2,1)} %collective-permute-done.6, bf16[128,1536]{1,0:T(8,128)(2,1)} %fusion.6, bf16[128,512]{1,0:T(8,128)(2,1)S(1)} %get-tuple-element.13, ...), kind=kOutput, calls=%fused_computation.6 | convolution fusion | flops 814481408 | bytes 3670016 | tf_op jit(solution)/shard_map/dot_general | solution.py:16
  126.1 9.9 %all-to-all-start.2 = ((bf16[32,48,512]{2,1,0:T(8,128)(2,1)}), bf16[32,48,512]{2,1,0:T(8,128)(2,1)S(1)}, u32[]{:S(2)}, u32[]{:S(2)}) async-start(bf16[32,48,512]{2,1,0:T(8,128)(2,1)} %bitcast.32), calls=%async_computation.3 | async-start | bytes 3145728 | tf_op jit(solution)/shard_map/all_to_all | solution.py:115
  136.0 0.0 reduce-scatter.2.cloned.1.call-start
  136.1 0.7 reduce-scatter.2.cloned.1.call-update
  136.8 3.7 %collective-permute-start.5 = (bf16[768,512]{1,0:T(8,128)(2,1)}, bf16[768,512]{1,0:T(8,128)(2,1)}, u32[]{:S(2)}, u32[]{:S(2)}) collective-permute-start(bf16[768,512]{1,0:T(8,128)(2,1)} %bitcast.29), channel_id=1, source_target_pairs={{0,4},{4,0},{1,5},{5,1},{2,6},{6,2},{3,7},{7,3},{8,12},{12,8},{9,1... | collective-permute-start | bytes 2359304 | tf_op jit(solution)/shard_map/ppermute | solution.py:27
  140.5 0.8 dynamic-slice_convert_fusion.2
  141.2 4.3 %collective-permute-start.4 = (bf16[128,512]{1,0:T(8,128)(2,1)}, bf16[128,512]{1,0:T(8,128)(2,1)}, u32[]{:S(2)}, u32[]{:S(2)}) collective-permute-start(bf16[128,512]{1,0:T(8,128)(2,1)} %get-tuple-element.10), channel_id=1, source_target_pairs={{0,1},{1,2},{2,3},{3,0},{4,5},{5,6},{6,7},{7,4},{8,9},{9,10},{10,1... | collective-permute-start | bytes 393224 | tf_op jit(solution)/shard_map/ppermute | solution.py:31
  145.5 5.5 %collective-permute-start.3 = (bf16[128,512]{1,0:T(8,128)(2,1)}, bf16[128,512]{1,0:T(8,128)(2,1)}, u32[]{:S(2)}, u32[]{:S(2)}) collective-permute-start(bf16[128,512]{1,0:T(8,128)(2,1)} %get-tuple-element.11), channel_id=1, source_target_pairs={{0,2},{1,3},{2,0},{3,1},{4,6},{5,7},{6,4},{7,5},{8,10},{9,11},{10,... | collective-permute-start | bytes 393224 | tf_op jit(solution)/shard_map/ppermute | solution.py:31
  151.0 5.5 %collective-permute-start.2 = (bf16[128,512]{1,0:T(8,128)(2,1)}, bf16[128,512]{1,0:T(8,128)(2,1)}, u32[]{:S(2)}, u32[]{:S(2)}) collective-permute-start(bf16[128,512]{1,0:T(8,128)(2,1)} %get-tuple-element.9), channel_id=1, source_target_pairs={{0,3},{1,0},{2,1},{3,2},{4,7},{5,4},{6,5},{7,6},{8,11},{9,8},{10,9... | collective-permute-start | bytes 393224 | tf_op jit(solution)/shard_map/ppermute | solution.py:31
  156.5 0.0 copy-start.2
  156.5 21.6 %collective-permute-done.4 = bf16[128,512]{1,0:T(8,128)(2,1)} collective-permute-done((bf16[128,512]{1,0:T(8,128)(2,1)}, bf16[128,512]{1,0:T(8,128)(2,1)}, u32[]{:S(2)}, u32[]{:S(2)}) %collective-permute-start.4) | collective-permute-done | bytes 131104 | tf_op jit(solution)/shard_map/ppermute | solution.py:31
  178.1 3.8 %collective-permute-done.3 = bf16[128,512]{1,0:T(8,128)(2,1)} collective-permute-done((bf16[128,512]{1,0:T(8,128)(2,1)}, bf16[128,512]{1,0:T(8,128)(2,1)}, u32[]{:S(2)}, u32[]{:S(2)}) %collective-permute-start.3) | collective-permute-done | bytes 131104 | tf_op jit(solution)/shard_map/ppermute | solution.py:31
  181.9 0.7 collective-permute-done.2
  182.6 1.2 multiply_reduce_fusion
  183.8 1.2 subtract_convert_fusion.1
  185.0 8.1 %collective-permute-done.5 = bf16[768,512]{1,0:T(8,128)(2,1)} collective-permute-done((bf16[768,512]{1,0:T(8,128)(2,1)}, bf16[768,512]{1,0:T(8,128)(2,1)}, u32[]{:S(2)}, u32[]{:S(2)}) %collective-permute-start.5) | collective-permute-done | bytes 786464 | tf_op jit(solution)/shard_map/ppermute | solution.py:27
  193.1 0.0 copy-done.2
  193.1 1.5 convolution_convert_fusion.2
  194.6 0.4 convolution_convert_fusion.3
  195.0 2.6 %fusion.5 = bf16[128,1408]{1,0:T(8,128)(2,1)} fusion(s32[1536]{0:T(1024)S(1)} %fusion.56, bf16[128,768]{1,0:T(8,128)(2,1)S(1)} %convolution_convert_fusion.2, bf16[128,768]{1,0:T(8,128)(2,1)S(1)} %convolution_convert_fusion.3), kind=kOutput, calls=%fused_computation.8 | convolution fusion | flops 556777472 | bytes 759808 | tf_op jit(solution)/shard_map/dot_general | solution.py:16
  197.6 1.0 fusion.37
  198.7 1.7 fusion.36
  200.3 0.0 all-to-all-done.2
  200.4 0.9 convert_reduce_fusion
  (14 shorter events, 0.2 us)
Async XLA Ops:
  7.2 17.6 %copy-start = (bf16[128,1408]{1,0:T(8,128)(2,1)S(1)}, bf16[128,1408]{1,0:T(8,128)(2,1)}, u32[]{:S(2)}) copy-start(bf16[128,1408]{1,0:T(8,128)(2,1)} %param.4) | copy-start | bytes 1081348
  9.0 44.3 %all-to-all-start = ((bf16[16,48,512]{2,1,0:T(8,128)(2,1)}), bf16[16,48,512]{2,1,0:T(8,128)(2,1)S(1)}, u32[]{:S(2)}, u32[]{:S(2)}) async-start(bf16[16,48,512]{2,1,0:T(8,128)(2,1)} %broadcast_in_dim.51), calls=%async_computation | async-start | bytes 1572864 | tf_op jit(solution)/shard_map/all_to_all | solution.py:23
  24.7 68.8 %all-gather.2.cloned.1.call-start = ((), (), s32[]{:S(2)}) async-start(), calls=%async_computation.4 | async-start | bytes 1179648 | tf_op jit(solution)/shard_map/all_gather | solution.py:80
  24.8 20.6 %copy-start.3 = (bf16[128,512]{1,0:T(8,128)(2,1)S(1)}, bf16[128,512]{1,0:T(8,128)(2,1)}, u32[]{:S(2)}) copy-start(bf16[128,512]{1,0:T(8,128)(2,1)} %param.5) | copy-start | bytes 393220
  27.2 95.4 %collective-permute-start.8 = (bf16[128,1536]{1,0:T(8,128)(2,1)}, bf16[128,1536]{1,0:T(8,128)(2,1)}, u32[]{:S(2)}, u32[]{:S(2)}) collective-permute-start(bf16[128,1536]{1,0:T(8,128)(2,1)} %fusion.6), channel_id=1, source_target_pairs={{0,3},{1,0},{2,1},{3,2},{4,7},{5,4},{6,5},{7,6},{8,11},{9,8},{10,9... | collective-permute-start | bytes 1179656 | tf_op jit(solution)/shard_map/ppermute | solution.py:31
  33.1 89.4 %collective-permute-start.7 = (bf16[128,1536]{1,0:T(8,128)(2,1)}, bf16[128,1536]{1,0:T(8,128)(2,1)}, u32[]{:S(2)}, u32[]{:S(2)}) collective-permute-start(bf16[128,1536]{1,0:T(8,128)(2,1)} %fusion.6), channel_id=1, source_target_pairs={{0,2},{1,3},{2,0},{3,1},{4,6},{5,7},{6,4},{7,5},{8,10},{9,11},{10,... | collective-permute-start | bytes 1179656 | tf_op jit(solution)/shard_map/ppermute | solution.py:31
  37.4 85.2 %collective-permute-start.6 = (bf16[128,1536]{1,0:T(8,128)(2,1)}, bf16[128,1536]{1,0:T(8,128)(2,1)}, u32[]{:S(2)}, u32[]{:S(2)}) collective-permute-start(bf16[128,1536]{1,0:T(8,128)(2,1)} %fusion.6), channel_id=1, source_target_pairs={{0,1},{1,2},{2,3},{3,0},{4,5},{5,6},{6,7},{7,4},{8,9},{9,10},{10,1... | collective-permute-start | bytes 1179656 | tf_op jit(solution)/shard_map/ppermute | solution.py:31
  42.7 7.6 %collective-permute-start = (bf16[128,768]{1,0:T(8,128)(2,1)S(1)}, bf16[128,768]{1,0:T(8,128)(2,1)S(1)}, u32[]{:S(2)}, u32[]{:S(2)}) collective-permute-start(bf16[128,768]{1,0:T(8,128)(2,1)S(1)} %broadcast_select_fusion), channel_id=1, source_target_pairs={{0,4},{4,0},{1,5},{5,1},{2,6},{6,2},{3,7},{7,3},{8,12},{12,8},{9,1... | collective-permute-start | bytes 589832 | tf_op jit(solution)/shard_map/ppermute | solution.py:27
  53.3 43.5 %copy-start.1 = (bf16[16,48,512]{2,1,0:T(8,128)(2,1)}, bf16[16,48,512]{2,1,0:T(8,128)(2,1)S(1)}, u32[]{:S(2)}) copy-start(bf16[16,48,512]{2,1,0:T(8,128)(2,1)S(1)} %all-to-all-done) | copy-start | bytes 2359300
  53.6 7.6 %collective-permute-start.1 = (bf16[128,512]{1,0:T(8,128)(2,1)S(1)}, bf16[128,512]{1,0:T(8,128)(2,1)S(1)}, u32[]{:S(2)}, u32[]{:S(2)}) collective-permute-start(bf16[128,512]{1,0:T(8,128)(2,1)S(1)} %convolution_convert_fusion.4), channel_id=1, source_target_pairs={{0,4},{4,0},{1,5},{5,1},{2,6},{6,2},{3,7},{7,3},{8,12},{12,8},{9,1... | collective-permute-start | bytes 393224 | tf_op jit(solution)/shard_map/ppermute | solution.py:27
  97.4 18.9 %all-to-all-start.1 = ((f32[8,8,128]{2,1,0:T(8,128)}), f32[8,8,128]{2,1,0:T(8,128)S(1)}, u32[]{:S(2)}, u32[]{:S(2)}) async-start(f32[8,8,128]{2,1,0:T(8,128)} %broadcast_in_dim.56), calls=%async_computation.1 | async-start | bytes 65536 | tf_op jit(solution)/shard_map/all_to_all | solution.py:23
  126.1 74.2 %all-to-all-start.2 = ((bf16[32,48,512]{2,1,0:T(8,128)(2,1)}), bf16[32,48,512]{2,1,0:T(8,128)(2,1)S(1)}, u32[]{:S(2)}, u32[]{:S(2)}) async-start(bf16[32,48,512]{2,1,0:T(8,128)(2,1)} %bitcast.32), calls=%async_computation.3 | async-start | bytes 3145728 | tf_op jit(solution)/shard_map/all_to_all | solution.py:115
  136.0 61.6 %reduce-scatter.2.cloned.1.call-start = ((), (), s32[]{:S(2)}) async-start(), calls=%async_computation.5 | async-start | bytes 1179648 | tf_op jit(solution)/shard_map/reduce_scatter | solution.py:107
  136.8 56.3 %collective-permute-start.5 = (bf16[768,512]{1,0:T(8,128)(2,1)}, bf16[768,512]{1,0:T(8,128)(2,1)}, u32[]{:S(2)}, u32[]{:S(2)}) collective-permute-start(bf16[768,512]{1,0:T(8,128)(2,1)} %bitcast.29), channel_id=1, source_target_pairs={{0,4},{4,0},{1,5},{5,1},{2,6},{6,2},{3,7},{7,3},{8,12},{12,8},{9,1... | collective-permute-start | bytes 2359304 | tf_op jit(solution)/shard_map/ppermute | solution.py:27
  141.2 36.8 %collective-permute-start.4 = (bf16[128,512]{1,0:T(8,128)(2,1)}, bf16[128,512]{1,0:T(8,128)(2,1)}, u32[]{:S(2)}, u32[]{:S(2)}) collective-permute-start(bf16[128,512]{1,0:T(8,128)(2,1)} %get-tuple-element.10), channel_id=1, source_target_pairs={{0,1},{1,2},{2,3},{3,0},{4,5},{5,6},{6,7},{7,4},{8,9},{9,10},{10,1... | collective-permute-start | bytes 393224 | tf_op jit(solution)/shard_map/ppermute | solution.py:31
  145.5 36.4 %collective-permute-start.3 = (bf16[128,512]{1,0:T(8,128)(2,1)}, bf16[128,512]{1,0:T(8,128)(2,1)}, u32[]{:S(2)}, u32[]{:S(2)}) collective-permute-start(bf16[128,512]{1,0:T(8,128)(2,1)} %get-tuple-element.11), channel_id=1, source_target_pairs={{0,2},{1,3},{2,0},{3,1},{4,6},{5,7},{6,4},{7,5},{8,10},{9,11},{10,... | collective-permute-start | bytes 393224 | tf_op jit(solution)/shard_map/ppermute | solution.py:31
  151.0 31.6 %collective-permute-start.2 = (bf16[128,512]{1,0:T(8,128)(2,1)}, bf16[128,512]{1,0:T(8,128)(2,1)}, u32[]{:S(2)}, u32[]{:S(2)}) collective-permute-start(bf16[128,512]{1,0:T(8,128)(2,1)} %get-tuple-element.9), channel_id=1, source_target_pairs={{0,3},{1,0},{2,1},{3,2},{4,7},{5,4},{6,5},{7,6},{8,11},{9,8},{10,9... | collective-permute-start | bytes 393224 | tf_op jit(solution)/shard_map/ppermute | solution.py:31
  156.5 36.6 %copy-start.2 = (bf16[16,48,512]{2,1,0:T(8,128)(2,1)S(1)}, bf16[16,48,512]{2,1,0:T(8,128)(2,1)}, u32[]{:S(2)}) copy-start(bf16[16,48,512]{2,1,0:T(8,128)(2,1)} %copy-done.1) | copy-start | bytes 2359300
Sparse Core Ops, SparseCore 0:
  46.4 38.3 all-gather.1
  139.7 47.5 reduce-scatter.1

commit v3 on v0

--- a/solution.py
+++ b/solution.py
@@ -1,15 +1,17 @@
 import jax
 import jax.numpy as jnp
 from jax import lax
+from jax.experimental import pallas as pl
+from jax.experimental.pallas import tpu as pltpu
 from jax.sharding import Mesh
 from jax.sharding import PartitionSpec as P
 
 
-NQ, NP, NZ = 4, 2, 4
-NY = NQ * NP
-Q, PAIR, Z = "dp_q", "dp_pair", "dp_z"
-Y = (Q, PAIR)
-SAME = (Q, Z)
+NY, NH, NP = 8, 2, 2
+NZ = NH * NP
+Y, ZH, PAIR = "dp_y", "dp_zh", "dp_pair"
+Z = (ZH, PAIR)
+SAME = (Y, ZH)
 
 
 def matmul(left, right, left_dim=1, right_dim=0):
@@ -31,6 +33,47 @@
     return lax.ppermute(array, Z, [(k, (k + distance) % NZ) for k in range(NZ)])
 
 
+def from_above(array, distance):
+    return lax.ppermute(array, Y, [(k, (k - distance) % NY) for k in range(NY)])
+
+
+def exps_kernel(place, scale, images, *refs):
+    pieces, (exps, texts, sums, cols) = refs[:NY], refs[NY:]
+    rows = pieces[0].shape[0]
+    total = jnp.zeros(sums.shape, jnp.float32)
+    for k in range(NY):
+        index = (place[0] + k) & (NY - 1)
+        at = pl.ds(pl.multiple_of(index * rows, rows), rows)
+        product = lax.dot_general(
+            images[...], pieces[k][...], (((1,), (1,)), ((), ())), preferred_element_type=jnp.float32
+        )
+        values = jnp.exp(scale[0] * product)
+        exps[:, at] = values
+        texts[at, :] = pieces[k][...]
+        cols[pl.ds(index, 1), :] = jnp.sum(values, axis=0, keepdims=True)
+        total = total + values
+    sums[...] = total
+
+
+def exps_and_sums(place, scale, images, pieces):
+    count, width = images.shape
+    rows = pieces[0].shape[0]
+    smem = pl.BlockSpec(memory_space=pltpu.SMEM)
+    vmem = pl.BlockSpec(memory_space=pltpu.VMEM)
+    return pl.pallas_call(
+        exps_kernel,
+        in_specs=[smem, smem] + [vmem] * (1 + NY),
+        out_specs=[vmem] * 4,
+        out_shape=[
+            jax.ShapeDtypeStruct((count, NY * rows), jnp.float32),
+            jax.ShapeDtypeStruct((NY * rows, width), jnp.bfloat16),
+            jax.ShapeDtypeStruct((count, rows), jnp.float32),
+            jax.ShapeDtypeStruct((NY, rows), jnp.float32),
+        ],
+        name="exps",
+    )(place.reshape(1), scale, images, *pieces)
+
+
 def inv_norm(embedding):
     return lax.rsqrt(jnp.sum(embedding * embedding, axis=1, keepdims=True) + 1e-06)
 
@@ -41,11 +84,11 @@
 
 
 def column_choice(width, padded, block, p):
-    half = NQ * NZ * padded
+    half = NY * NH * padded
     shape = (width, NP * half)
     col = lax.broadcasted_iota(jnp.int32, (1, shape[1]), 1)
     slot, place, c = col // half, (col % half) // padded, col % padded
-    owner = (place // NZ * NP + (p + slot) % NP) * NZ + place % NZ
+    owner = place * NP + (p + slot) % NP
     source = jnp.where(c < block, owner * block + c, -1)
     return (lax.broadcasted_iota(jnp.int32, shape, 0) == source).astype(jnp.bfloat16)
 
@@ -55,11 +98,11 @@
     rows, width = image_features.shape
     block, emb_width = image_head.shape
     padded = -(-block // 16) * 16
-    half = NQ * NZ * padded
+    half = NY * NH * padded
     p, b = lax.axis_index(PAIR), lax.axis_index(Z)
     a = lax.axis_index(Y)
 
-    head = to_all(jnp.pad(image_head, ((0, padded - block), (0, 0))), SAME, NQ * NZ)
+    head = to_all(jnp.pad(image_head, ((0, padded - block), (0, 0))), SAME, NY * NH)
     head = head.reshape(half, emb_width)
     choice = column_choice(width, padded, block, p)
     kept = matmul(image_features, choice[:, :half]).astype(jnp.bfloat16)
@@ -70,8 +113,7 @@
     txt_emb = text_embed.astype(jnp.float32)
     txt_inv = inv_norm(txt_emb)
     txt_unit = (txt_emb * txt_inv).astype(jnp.bfloat16)
-    txt_sent, partner_part = lax.optimization_barrier((txt_unit, partner_part))
-    texts = to_all(txt_sent, Y, NY).reshape(NY * rows, emb_width)
+    pieces = [txt_unit] + [from_above(txt_unit, k) for k in range(1, NY)]
     returned = swapped(partner_part)
 
     img_emb = matmul(kept, head) + returned.astype(jnp.float32)
@@ -79,12 +121,10 @@
     img_unit = (img_emb * img_inv).astype(jnp.bfloat16)
     images = lax.all_gather(img_unit, Z, axis=0, tiled=True)
 
-    exps = jnp.exp(scale * matmul(images, texts, 1, 1))
-    row_part = jnp.sum(exps, axis=1)
-    col_part = jnp.sum(exps, axis=0)
-
-    col_sum = jnp.sum(to_all(col_part.reshape(NY, rows), Y, NY), axis=0).reshape(NY * rows)
-    row_sum = lax.psum(row_part, Z)
+    exps, texts, row_part, col_part = exps_and_sums(a, logit_scale, images, pieces)
+    col_parts = to_all(col_part, Y, NY)
+    col_sum = jnp.sum(col_parts, axis=0).reshape(NY * rows)
+    row_sum = lax.psum(jnp.sum(row_part, axis=1), Z)
 
     i = lax.broadcasted_iota(jnp.int32, exps.shape, 0) - b * rows
     j = lax.broadcasted_iota(jnp.int32, exps.shape, 1) - a * rows
@@ -111,7 +151,7 @@
     head_part = matmul(kept, img_emb_grad, 0, 0) + matmul(taken, partner_grad, 0, 0)
     head_part, txt_grads = lax.optimization_barrier((head_part.astype(jnp.bfloat16), txt_grads))
     head_grads = lax.all_to_all(
-        head_part.reshape(NQ * NZ, padded, emb_width), SAME, 0, 0, tiled=True
+        head_part.reshape(NY * NH, padded, emb_width), SAME, 0, 0, tiled=True
     )
     kept_grad = matmul(img_emb_grad, head, 1, 1).astype(jnp.bfloat16)
     given_grad = swapped(matmul(partner_grad, head, 1, 1).astype(jnp.bfloat16))
@@ -131,8 +171,8 @@
 
 
 def solution(mesh):
-    split = Mesh(mesh.devices.reshape(mesh.shape["rep"], NQ, NP, NZ), ("rep", Q, PAIR, Z))
-    spec = P(("rep", Q, PAIR, Z), None)
+    split = Mesh(mesh.devices.reshape(mesh.shape["rep"], NY, NH, NP), ("rep", Y, ZH, PAIR))
+    spec = P(("rep", Y, ZH, PAIR), None)
 
     return jax.shard_map(
         local,

time: 195 us -> 220 us (1.13)
  starting transfers between devices: 68.8 us -> 86 us
  waiting for transfers between devices: 57.2 us -> 61.8 us
  Pallas kernels: 0 us -> 4.45 us
  other arithmetic: 11.2 us -> 14.1 us
    ppermute x0 -> x7, starting transfers between devices: none -> 31 us  [from_above(): return lax.ppermute(array, Y, [(k, (k - distance) % NY) for k in range(NY)])]
    all_to_all x3 -> x2, starting transfers between devices: 25.6 us -> 15.8 us  [to_all(): return lax.all_to_all(copies, axes, 0, 0, tiled=True)]
    ppermute x4, waiting for transfers between devices: 46.1 us -> 53.5 us  [swapped(): return lax.ppermute(array, PAIR, [(0, 1), (1, 0)])]
    all_to_all x3 -> x2, waiting for transfers between devices: 5.39 us -> 0.01 us  [to_all(): return lax.all_to_all(copies, axes, 0, 0, tiled=True)]
    pallas_call x0 -> x1, Pallas kernels: none -> 4.45 us  [exps_and_sums(): pl.pallas_call(exps_kernel, in_specs=[smem, smem] + [vmem] * (1 + NY), ou...]
    ppermute x4, starting transfers between devices: 12.9 us -> 10.1 us  [swapped(): return lax.ppermute(array, PAIR, [(0, 1), (1, 0)])]
    ppermute x3, waiting for transfers between devices: 5.7 us -> 8.26 us  [shifted(): return lax.ppermute(array, Z, [(k, (k + distance) % NZ) for k in range(NZ)])]
    dot_general x12 -> x11, matrix products: 19.7 us -> 18.2 us  [matmul(): lax.dot_general(left, right, (((left_dim,), (right_dim,)), ((), ())), pre...]
  transfers between devices with their start and end apart: 12 -> 18, of which waited for: 7 -> 6; matrix products, arithmetic and copies ran while one was open for 11% -> 12% of each run, Pallas kernels for 0% -> 0%
where the time goes in v3:
time: 220 us; the launch traced here: 219 us
  starting transfers between devices  86 us (39%)
  waiting for transfers between devices  61.8 us (28%)
  blocking collectives  27.8 us (13%)
  matrix products  18.2 us (8%)
  other arithmetic  14.1 us (6%)
  local copies, waits for them, and re-layouts  4.89 us (2%)
  Pallas kernels  4.45 us (2%)
    ppermute x4, waiting for transfers between devices, swapped(): return lax.ppermute(array, PAIR, [(0, 1), (1, 0)])  53.5 us
    ppermute x7, starting transfers between devices, from_above(): return lax.ppermute(array, Y, [(k, (k - distance) % NY) for k in range(NY)])  31 us
    all_gather x1, blocking collectives, local(): images = lax.all_gather(img_unit, Z, axis=0, tiled=True)  19.1 us
    dot_general x11, matrix products, matmul(): lax.dot_general(left, right, (((left_dim,), (right_dim,)), ((), ())), pre...  18.2 us
    all_to_all x2, starting transfers between devices, to_all(): return lax.all_to_all(copies, axes, 0, 0, tiled=True)  15.8 us
    ppermute x3, starting transfers between devices, shifted(): return lax.ppermute(array, Z, [(k, (k + distance) % NZ) for k in range(NZ)])  13.3 us
    ppermute x4, starting transfers between devices, swapped(): return lax.ppermute(array, PAIR, [(0, 1), (1, 0)])  10.1 us
    all_to_all x1, starting transfers between devices, local(): lax.all_to_all(head_part.reshape(NY * NH, padded, emb_width), SAME, 0, 0,...  8.71 us
  transfers between devices with their start and end apart: 18, of which 6 were waited for; matrix products, arithmetic and copies ran while one was open for 12% of the time, Pallas kernels for 0%

profile of v3, /device:TPU:6, one launch (start us, length us, event | category | flops | bytes accessed | tf_op | source)
XLA Modules:
  0.0 218.9 jit_solution(5255626830034107954)
XLA Ops:
  0.6 0.0 copy-start
  0.6 1.1 fusion.15
  1.7 1.7 fusion.16.refs_0_
  3.4 5.4 %collective-permute-start.2 = (bf16[128,512]{1,0:T(8,128)(2,1)}, bf16[128,512]{1,0:T(8,128)(2,1)}, u32[]{:S(2)}, u32[]{:S(2)}) collective-permute-start(bf16[128,512]{1,0:T(8,128)(2,1)} %fusion.16.refs_0_), channel_id=1, source_target_pairs={{0,28},{4,0},{8,4},{12,8},{16,12},{20,16},{24,20},{28,24},{1,29},{... | collective-permute-start | bytes 393224 | tf_op jit(solution)/shard_map/ppermute | solution.py:37
  8.8 4.0 %collective-permute-start.3 = (bf16[128,512]{1,0:T(8,128)(2,1)}, bf16[128,512]{1,0:T(8,128)(2,1)}, u32[]{:S(2)}, u32[]{:S(2)}) collective-permute-start(bf16[128,512]{1,0:T(8,128)(2,1)} %fusion.16.refs_0_), channel_id=1, source_target_pairs={{0,24},{4,28},{8,0},{12,4},{16,8},{20,12},{24,16},{28,20},{1,25},{... | collective-permute-start | bytes 393224 | tf_op jit(solution)/shard_map/ppermute | solution.py:37
  12.8 3.0 %collective-permute-start.4 = (bf16[128,512]{1,0:T(8,128)(2,1)}, bf16[128,512]{1,0:T(8,128)(2,1)}, u32[]{:S(2)}, u32[]{:S(2)}) collective-permute-start(bf16[128,512]{1,0:T(8,128)(2,1)} %fusion.16.refs_0_), channel_id=1, source_target_pairs={{0,20},{4,24},{8,28},{12,0},{16,4},{20,8},{24,12},{28,16},{1,21},{... | collective-permute-start | bytes 393224 | tf_op jit(solution)/shard_map/ppermute | solution.py:37
  15.8 5.9 %collective-permute-start.5 = (bf16[128,512]{1,0:T(8,128)(2,1)}, bf16[128,512]{1,0:T(8,128)(2,1)}, u32[]{:S(2)}, u32[]{:S(2)}) collective-permute-start(bf16[128,512]{1,0:T(8,128)(2,1)} %fusion.16.refs_0_), channel_id=1, source_target_pairs={{0,16},{4,20},{8,24},{12,28},{16,0},{20,4},{24,8},{28,12},{1,17},{... | collective-permute-start | bytes 393224 | tf_op jit(solution)/shard_map/ppermute | solution.py:37
  21.8 0.8 pad.4
  22.6 1.0 broadcast_in_dim.22
  23.6 12.0 %all-to-all-start = ((bf16[16,48,512]{2,1,0:T(8,128)(2,1)}), bf16[16,48,512]{2,1,0:T(8,128)(2,1)S(1)}, u32[]{:S(2)}, u32[]{:S(2)}) async-start(bf16[16,48,512]{2,1,0:T(8,128)(2,1)} %broadcast_in_dim.22), calls=%async_computation | async-start | bytes 1572864 | tf_op jit(solution)/shard_map/all_to_all | solution.py:25
  35.6 1.8 iota_compare_fusion
  37.4 1.6 fusion.14
  39.0 4.3 %collective-permute-start = (bf16[128,768]{0,1:T(8,128)(2,1)}, bf16[128,768]{0,1:T(8,128)(2,1)}, u32[]{:S(2)}, u32[]{:S(2)}) collective-permute-start(bf16[128,768]{0,1:T(8,128)(2,1)} %fusion.14), channel_id=1, source_target_pairs={{0,1},{1,0},{2,3},{3,2},{4,5},{5,4},{6,7},{7,6},{8,9},{9,8},{10,11... | collective-permute-start | bytes 589832 | tf_op jit(solution)/shard_map/ppermute | solution.py:29
  43.3 0.9 fusion.13
  44.2 22.9 %collective-permute-done = bf16[128,768]{0,1:T(8,128)(2,1)} collective-permute-done((bf16[128,768]{0,1:T(8,128)(2,1)}, bf16[128,768]{0,1:T(8,128)(2,1)}, u32[]{:S(2)}, u32[]{:S(2)}) %collective-permute-start) | collective-permute-done | bytes 196640 | tf_op jit(solution)/shard_map/ppermute | solution.py:29
  67.0 1.2 convolution_convert_fusion.2
  68.3 1.9 collective-permute-start.1
  70.9 8.0 %collective-permute-done.1 = bf16[128,512]{1,0:T(8,128)(2,1)S(1)} collective-permute-done((bf16[128,512]{1,0:T(8,128)(2,1)S(1)}, bf16[128,512]{1,0:T(8,128)(2,1)S(1)}, u32[]{:S(2)}, u32[]{:S(2)}) %collective-permute-start.1) | collective-permute-done | bytes 131104 | tf_op jit(solution)/shard_map/ppermute | solution.py:29
  78.8 5.2 %collective-permute-start.6 = (bf16[128,512]{1,0:T(8,128)(2,1)}, bf16[128,512]{1,0:T(8,128)(2,1)S(1)}, u32[]{:S(2)}, u32[]{:S(2)}) collective-permute-start(bf16[128,512]{1,0:T(8,128)(2,1)} %fusion.16.refs_0_), channel_id=1, source_target_pairs={{0,12},{4,16},{8,20},{12,24},{16,28},{20,0},{24,4},{28,8},{1,13},{... | collective-permute-start | bytes 393224 | tf_op jit(solution)/shard_map/ppermute | solution.py:37
  84.0 0.4 multiply_reduce_fusion.1
  84.4 0.1 multiply_convert_fusion
  84.5 0.0 collective-permute-done.2.refs_1_
  84.5 5.5 %collective-permute-start.7 = (bf16[128,512]{1,0:T(8,128)(2,1)}, bf16[128,512]{1,0:T(8,128)(2,1)S(1)}, u32[]{:S(2)}, u32[]{:S(2)}) collective-permute-start(bf16[128,512]{1,0:T(8,128)(2,1)} %fusion.16.refs_0_), channel_id=1, source_target_pairs={{0,8},{4,12},{8,16},{12,20},{16,24},{20,28},{24,0},{28,4},{1,9},{5... | collective-permute-start | bytes 393224 | tf_op jit(solution)/shard_map/ppermute | solution.py:37
  90.1 1.9 collective-permute-start.8
  92.0 19.1 %all_gather.3.images = bf16[512,512]{1,0:T(8,128)(2,1)} all-gather(bf16[128,512]{1,0:T(8,128)(2,1)S(1)} %multiply_convert_fusion), channel_id=1, replica_groups=mesh['rep'=16,'dp_y'=8,'dp_zh'=2,'dp_pair'=2] {'dp_zh','dp_pair'}, dimensions={0}, use_global_device_ids=true | all-gather | bytes 655360 | tf_op jit(solution)/shard_map/all_gather | solution.py:122
  111.1 0.0 collective-permute-done.4.refs_3_
  111.1 0.0 collective-permute-done.5.refs_4_
  111.1 0.0 collective-permute-done.7.refs_6_
  111.2 0.0 collective-permute-done.8.refs_7_
  111.2 0.6 copy-done.8
  111.8 0.1 copy-done.9
  111.9 0.0 copy-done.10
  111.9 4.4 %exps.1 = (f32[512,1024]{1,0:T(8,128)}, bf16[1024,512]{1,0:T(8,128)(2,1)}, f32[512,128]{1,0:T(8,128)}, f32[8,128]{1,0:T(8,128)}) custom-call(s32[1]{0:T(128)} %bitcast.3.place, f32[1]{0:T(128)} %copy.17.scale, bf16[512,512]{1,0:T(8,128)(2,1)} %all_gather.3.images, bf16[128,512]{1,0:T(8,128)(2,1)} %fusion.16.refs_0_, ...), custom_call_target="tpu_custom_call" | custom-call | tf_op jit(solution)/shard_map/exps/pallas_call | solution.py:63
  116.3 1.4 broadcast_in_dim.23
  117.7 3.8 %all-to-all-start.1 = ((f32[8,8,128]{2,1,0:T(8,128)}), f32[8,8,128]{2,1,0:T(8,128)S(1)}, u32[]{:S(2)}, u32[]{:S(2)}) async-start(f32[8,8,128]{2,1,0:T(8,128)} %broadcast_in_dim.23), calls=%async_computation.1 | async-start | bytes 65536 | tf_op jit(solution)/shard_map/all_to_all | solution.py:25
  121.5 1.1 reduce_sum.74
  122.6 8.6 %psum.7 = f32[512]{0:T(512)S(1)} all-reduce(f32[512]{0:T(512)S(1)} %reduce_sum.74), channel_id=1, replica_groups=mesh['rep'=16,'dp_y'=8,'dp_zh'=2,'dp_pair'=2] {'dp_zh','dp_pair'}, use_global_device_ids=true, to_apply=%region_3.4 | all-reduce | flops 512 | bytes 4096 | tf_op jit(solution)/shard_map/psum | solution.py:127
  131.3 2.1 subtract_convert_fusion
  133.4 2.4 %fusion.40 = (bf16[1024,512]{1,0:T(8,128)(2,1)}, f32[1024,512]{1,0:T(8,128)}) fusion(bf16[512,1024]{1,0:T(8,128)(2,1)S(1)} %subtract_convert_fusion, bf16[512,512]{1,0:T(8,128)(2,1)S(1)} %copy-done.1), kind=kOutput, calls=%fused_computation.82 | convolution fusion | flops 537395200 | bytes 4718592 | tf_op jit(solution)/shard_map/dot_general | solution.py:18
  135.9 7.2 %all-to-all-start.2 = ((bf16[8,128,512]{2,1,0:T(8,128)(2,1)}), bf16[8,128,512]{2,1,0:T(8,128)(2,1)S(1)}, u32[]{:S(2)}, u32[]{:S(2)}) async-start(bf16[8,128,512]{2,1,0:T(8,128)(2,1)} %bitcast.37), calls=%async_computation.2 | async-start | bytes 2097152 | tf_op jit(solution)/shard_map/all_to_all | solution.py:137
  143.1 1.9 fusion.41
  145.0 1.0 copy-done.5
  146.0 5.0 %collective-permute-start.11 = (bf16[128,512]{1,0:T(8,128)(2,1)S(1)}, bf16[128,512]{1,0:T(8,128)(2,1)S(1)}, u32[]{:S(2)}, u32[]{:S(2)}) collective-permute-start(bf16[128,512]{1,0:T(8,128)(2,1)S(1)} %get-tuple-element.17), channel_id=1, source_target_pairs={{0,1},{1,2},{2,3},{3,0},{4,5},{5,6},{6,7},{7,4},{8,9},{9,10},{10,1... | collective-permute-start | bytes 393224 | tf_op jit(solution)/shard_map/ppermute | solution.py:33
  151.0 4.9 %collective-permute-start.10 = (bf16[128,512]{1,0:T(8,128)(2,1)S(1)}, bf16[128,512]{1,0:T(8,128)(2,1)S(1)}, u32[]{:S(2)}, u32[]{:S(2)}) collective-permute-start(bf16[128,512]{1,0:T(8,128)(2,1)S(1)} %get-tuple-element.16), channel_id=1, source_target_pairs={{0,2},{1,3},{2,0},{3,1},{4,6},{5,7},{6,4},{7,5},{8,10},{9,11},{10,... | collective-permute-start | bytes 393224 | tf_op jit(solution)/shard_map/ppermute | solution.py:33
  155.9 3.4 %collective-permute-start.9 = (bf16[128,512]{1,0:T(8,128)(2,1)S(1)}, bf16[128,512]{1,0:T(8,128)(2,1)S(1)}, u32[]{:S(2)}, u32[]{:S(2)}) collective-permute-start(bf16[128,512]{1,0:T(8,128)(2,1)S(1)} %get-tuple-element.15), channel_id=1, source_target_pairs={{0,3},{1,0},{2,1},{3,2},{4,7},{5,4},{6,5},{7,6},{8,11},{9,8},{10,9... | collective-permute-start | bytes 393224 | tf_op jit(solution)/shard_map/ppermute | solution.py:33
  159.3 0.0 collective-permute-done.11
  159.3 3.8 %collective-permute-done.10 = bf16[128,512]{1,0:T(8,128)(2,1)S(1)} collective-permute-done((bf16[128,512]{1,0:T(8,128)(2,1)S(1)}, bf16[128,512]{1,0:T(8,128)(2,1)S(1)}, u32[]{:S(2)}, u32[]{:S(2)}) %collective-permute-start.10) | collective-permute-done | bytes 131104 | tf_op jit(solution)/shard_map/ppermute | solution.py:33
  163.2 4.4 %collective-permute-done.9 = bf16[128,512]{1,0:T(8,128)(2,1)S(1)} collective-permute-done((bf16[128,512]{1,0:T(8,128)(2,1)S(1)}, bf16[128,512]{1,0:T(8,128)(2,1)S(1)}, u32[]{:S(2)}, u32[]{:S(2)}) %collective-permute-start.9) | collective-permute-done | bytes 131104 | tf_op jit(solution)/shard_map/ppermute | solution.py:33
  167.6 1.2 multiply_reduce_fusion
  168.8 1.1 subtract_convert_fusion.1
  169.9 1.9 collective-permute-start.12
  171.9 0.3 fusion.42
  172.2 6.6 %collective-permute-done.12 = bf16[128,512]{1,0:T(8,128)(2,1)S(1)} collective-permute-done((bf16[128,512]{1,0:T(8,128)(2,1)S(1)}, bf16[128,512]{1,0:T(8,128)(2,1)S(1)}, u32[]{:S(2)}, u32[]{:S(2)}) %collective-permute-start.12) | collective-permute-done | bytes 131104 | tf_op jit(solution)/shard_map/ppermute | solution.py:29
  178.8 2.2 add_convert_fusion
  181.0 8.7 %all-to-all-start.3 = ((bf16[16,48,512]{2,1,0:T(8,128)(2,1)}), bf16[16,48,512]{2,1,0:T(8,128)(2,1)S(1)}, u32[]{:S(2)}, u32[]{:S(2)}) async-start(bf16[16,48,512]{2,1,0:T(8,128)(2,1)} %bitcast.38), calls=%async_computation.3 | async-start | bytes 1572864 | tf_op jit(solution)/shard_map/all_to_all | solution.py:153
  189.7 1.1 convolution_convert_fusion
  190.8 1.9 collective-permute-start.13
  192.7 3.1 %fusion.2 = f32[128,1408]{1,0:T(8,128)} fusion(pred[1408,1536]{1,0:T(32,128)(4,1)} %copy-done.2, bf16[128,512]{1,0:T(8,128)(2,1)S(1)} %subtract_convert_fusion.1, bf16[768,512]{1,0:T(8,128)(2,1)S(1)} %bitcast.36), kind=kOutput, calls=%fused_computation.4 | convolution fusion | flops 377585664 | bytes 2719744 | tf_op jit(solution)/shard_map/dot_general | solution.py:18
  195.8 16.1 %collective-permute-done.13 = bf16[128,768]{1,0:T(8,128)(2,1)} collective-permute-done((bf16[128,768]{1,0:T(8,128)(2,1)}, bf16[128,768]{1,0:T(8,128)(2,1)}, u32[]{:S(2)}, u32[]{:S(2)}) %collective-permute-start.13) | collective-permute-done | bytes 196640 | tf_op jit(solution)/shard_map/ppermute | solution.py:29
  211.9 3.1 %fusion.7 = bf16[128,1408]{1,0:T(8,128)(2,1)} fusion(f32[128,1408]{1,0:T(8,128)} %fusion.2, bf16[128,768]{1,0:T(8,128)(2,1)} %collective-permute-done.13, pred[1408,1536]{1,0:T(32,128)(4,1)} %copy-done.2), kind=kOutput, calls=%fused_computation.8 | convolution fusion | flops 277184512 | bytes 2359296 | tf_op jit(solution)/shard_map/dot_general | solution.py:18
  215.1 0.3 select_reduce_fusion
  215.4 1.1 fusion.20
  216.4 1.7 fusion.19
  218.2 0.8 convert_reduce_fusion
  (34 shorter events, 0.2 us)
Async XLA Ops:
  0.6 36.8 %copy-start = (bf16[128,1408]{1,0:T(8,128)(2,1)S(1)}, bf16[128,1408]{1,0:T(8,128)(2,1)}, u32[]{:S(2)}) copy-start(bf16[128,1408]{1,0:T(8,128)(2,1)} %param.4) | copy-start | bytes 1081348
  3.4 81.2 %collective-permute-start.2 = (bf16[128,512]{1,0:T(8,128)(2,1)}, bf16[128,512]{1,0:T(8,128)(2,1)}, u32[]{:S(2)}, u32[]{:S(2)}) collective-permute-start(bf16[128,512]{1,0:T(8,128)(2,1)} %fusion.16.refs_0_), channel_id=1, source_target_pairs={{0,28},{4,0},{8,4},{12,8},{16,12},{20,16},{24,20},{28,24},{1,29},{... | collective-permute-start | bytes 393224 | tf_op jit(solution)/shard_map/ppermute | solution.py:37
  8.8 81.3 %collective-permute-start.3 = (bf16[128,512]{1,0:T(8,128)(2,1)}, bf16[128,512]{1,0:T(8,128)(2,1)}, u32[]{:S(2)}, u32[]{:S(2)}) collective-permute-start(bf16[128,512]{1,0:T(8,128)(2,1)} %fusion.16.refs_0_), channel_id=1, source_target_pairs={{0,24},{4,28},{8,0},{12,4},{16,8},{20,12},{24,16},{28,20},{1,25},{... | collective-permute-start | bytes 393224 | tf_op jit(solution)/shard_map/ppermute | solution.py:37
  12.8 98.3 %collective-permute-start.4 = (bf16[128,512]{1,0:T(8,128)(2,1)}, bf16[128,512]{1,0:T(8,128)(2,1)}, u32[]{:S(2)}, u32[]{:S(2)}) collective-permute-start(bf16[128,512]{1,0:T(8,128)(2,1)} %fusion.16.refs_0_), channel_id=1, source_target_pairs={{0,20},{4,24},{8,28},{12,0},{16,4},{20,8},{24,12},{28,16},{1,21},{... | collective-permute-start | bytes 393224 | tf_op jit(solution)/shard_map/ppermute | solution.py:37
  15.8 95.3 %collective-permute-start.5 = (bf16[128,512]{1,0:T(8,128)(2,1)}, bf16[128,512]{1,0:T(8,128)(2,1)}, u32[]{:S(2)}, u32[]{:S(2)}) collective-permute-start(bf16[128,512]{1,0:T(8,128)(2,1)} %fusion.16.refs_0_), channel_id=1, source_target_pairs={{0,16},{4,20},{8,24},{12,28},{16,0},{20,4},{24,8},{28,12},{1,17},{... | collective-permute-start | bytes 393224 | tf_op jit(solution)/shard_map/ppermute | solution.py:37
  23.6 43.5 %all-to-all-start = ((bf16[16,48,512]{2,1,0:T(8,128)(2,1)}), bf16[16,48,512]{2,1,0:T(8,128)(2,1)S(1)}, u32[]{:S(2)}, u32[]{:S(2)}) async-start(bf16[16,48,512]{2,1,0:T(8,128)(2,1)} %broadcast_in_dim.22), calls=%async_computation | async-start | bytes 1572864 | tf_op jit(solution)/shard_map/all_to_all | solution.py:25
  37.4 5.9 %copy-start.2 = (pred[1408,1536]{1,0:T(32,128)(4,1)}, pred[1408,1536]{1,0:T(32,128)(4,1)S(1)}, u32[]{:S(2)}) copy-start(pred[1408,1536]{1,0:T(32,128)(4,1)S(1)} %iota_compare_fusion) | copy-start | bytes 6488068
  39.0 28.1 %collective-permute-start = (bf16[128,768]{0,1:T(8,128)(2,1)}, bf16[128,768]{0,1:T(8,128)(2,1)}, u32[]{:S(2)}, u32[]{:S(2)}) collective-permute-start(bf16[128,768]{0,1:T(8,128)(2,1)} %fusion.14), channel_id=1, source_target_pairs={{0,1},{1,0},{2,3},{3,2},{4,5},{5,4},{6,7},{7,6},{8,9},{9,8},{10,11... | collective-permute-start | bytes 589832 | tf_op jit(solution)/shard_map/ppermute | solution.py:29
  44.2 72.2 %copy-start.6 = (bf16[768,128]{1,0:T(8,128)(2,1)}, bf16[768,128]{1,0:T(8,128)(2,1)S(1)}, u32[]{:S(2)}) copy-start(bf16[768,128]{1,0:T(8,128)(2,1)S(1)} %fusion.13) | copy-start | bytes 589828
  68.3 10.6 %collective-permute-start.1 = (bf16[128,512]{1,0:T(8,128)(2,1)S(1)}, bf16[128,512]{1,0:T(8,128)(2,1)S(1)}, u32[]{:S(2)}, u32[]{:S(2)}) collective-permute-start(bf16[128,512]{1,0:T(8,128)(2,1)S(1)} %convolution_convert_fusion.2), channel_id=1, source_target_pairs={{0,1},{1,0},{2,3},{3,2},{4,5},{5,4},{6,7},{7,6},{8,9},{9,8},{10,11... | collective-permute-start | bytes 393224 | tf_op jit(solution)/shard_map/ppermute | solution.py:29
  78.8 32.3 %copy-start.3 = (bf16[128,512]{1,0:T(8,128)(2,1)}, bf16[128,512]{1,0:T(8,128)(2,1)S(1)}, u32[]{:S(2)}) copy-start(bf16[128,512]{1,0:T(8,128)(2,1)S(1)} %collective-permute-done.1) | copy-start | bytes 393220
  78.8 32.3 %collective-permute-start.6 = (bf16[128,512]{1,0:T(8,128)(2,1)}, bf16[128,512]{1,0:T(8,128)(2,1)S(1)}, u32[]{:S(2)}, u32[]{:S(2)}) collective-permute-start(bf16[128,512]{1,0:T(8,128)(2,1)} %fusion.16.refs_0_), channel_id=1, source_target_pairs={{0,12},{4,16},{8,20},{12,24},{16,28},{20,0},{24,4},{28,8},{1,13},{... | collective-permute-start | bytes 393224 | tf_op jit(solution)/shard_map/ppermute | solution.py:37
  84.5 26.6 %collective-permute-start.7 = (bf16[128,512]{1,0:T(8,128)(2,1)}, bf16[128,512]{1,0:T(8,128)(2,1)S(1)}, u32[]{:S(2)}, u32[]{:S(2)}) collective-permute-start(bf16[128,512]{1,0:T(8,128)(2,1)} %fusion.16.refs_0_), channel_id=1, source_target_pairs={{0,8},{4,12},{8,16},{12,20},{16,24},{20,28},{24,0},{28,4},{1,9},{5... | collective-permute-start | bytes 393224 | tf_op jit(solution)/shard_map/ppermute | solution.py:37
  90.1 21.1 %collective-permute-start.8 = (bf16[128,512]{1,0:T(8,128)(2,1)}, bf16[128,512]{1,0:T(8,128)(2,1)S(1)}, u32[]{:S(2)}, u32[]{:S(2)}) collective-permute-start(bf16[128,512]{1,0:T(8,128)(2,1)} %fusion.16.refs_0_), channel_id=1, source_target_pairs={{0,4},{4,8},{8,12},{12,16},{16,20},{20,24},{24,28},{28,0},{1,5},{5... | collective-permute-start | bytes 393224 | tf_op jit(solution)/shard_map/ppermute | solution.py:37
  111.1 0.7 copy-start.8
  111.1 0.7 copy-start.9
  111.2 0.7 copy-start.10
  116.3 17.1 %copy-start.1 = (bf16[512,512]{1,0:T(8,128)(2,1)S(1)}, bf16[512,512]{1,0:T(8,128)(2,1)}, u32[]{:S(2)}) copy-start(bf16[512,512]{1,0:T(8,128)(2,1)} %all_gather.3.images) | copy-start | bytes 1572868
  117.7 13.6 %all-to-all-start.1 = ((f32[8,8,128]{2,1,0:T(8,128)}), f32[8,8,128]{2,1,0:T(8,128)S(1)}, u32[]{:S(2)}, u32[]{:S(2)}) async-start(f32[8,8,128]{2,1,0:T(8,128)} %broadcast_in_dim.23), calls=%async_computation.1 | async-start | bytes 65536 | tf_op jit(solution)/shard_map/all_to_all | solution.py:25
  135.9 45.1 %all-to-all-start.2 = ((bf16[8,128,512]{2,1,0:T(8,128)(2,1)}), bf16[8,128,512]{2,1,0:T(8,128)(2,1)S(1)}, u32[]{:S(2)}, u32[]{:S(2)}) async-start(bf16[8,128,512]{2,1,0:T(8,128)(2,1)} %bitcast.37), calls=%async_computation.2 | async-start | bytes 2097152 | tf_op jit(solution)/shard_map/all_to_all | solution.py:137
  145.0 1.0 copy-start.5
  146.0 25.9 %copy-start.7 = (bf16[768,128]{1,0:T(8,128)(2,1)S(1)}, bf16[768,128]{1,0:T(8,128)(2,1)}, u32[]{:S(2)}) copy-start(bf16[768,128]{1,0:T(8,128)(2,1)} %copy-done.6) | copy-start | bytes 589828
  146.0 13.3 %collective-permute-start.11 = (bf16[128,512]{1,0:T(8,128)(2,1)S(1)}, bf16[128,512]{1,0:T(8,128)(2,1)S(1)}, u32[]{:S(2)}, u32[]{:S(2)}) collective-permute-start(bf16[128,512]{1,0:T(8,128)(2,1)S(1)} %get-tuple-element.17), channel_id=1, source_target_pairs={{0,1},{1,2},{2,3},{3,0},{4,5},{5,6},{6,7},{7,4},{8,9},{9,10},{10,1... | collective-permute-start | bytes 393224 | tf_op jit(solution)/shard_map/ppermute | solution.py:33
  151.0 12.2 %collective-permute-start.10 = (bf16[128,512]{1,0:T(8,128)(2,1)S(1)}, bf16[128,512]{1,0:T(8,128)(2,1)S(1)}, u32[]{:S(2)}, u32[]{:S(2)}) collective-permute-start(bf16[128,512]{1,0:T(8,128)(2,1)S(1)} %get-tuple-element.16), channel_id=1, source_target_pairs={{0,2},{1,3},{2,0},{3,1},{4,6},{5,7},{6,4},{7,5},{8,10},{9,11},{10,... | collective-permute-start | bytes 393224 | tf_op jit(solution)/shard_map/ppermute | solution.py:33
  155.9 11.7 %collective-permute-start.9 = (bf16[128,512]{1,0:T(8,128)(2,1)S(1)}, bf16[128,512]{1,0:T(8,128)(2,1)S(1)}, u32[]{:S(2)}, u32[]{:S(2)}) collective-permute-start(bf16[128,512]{1,0:T(8,128)(2,1)S(1)} %get-tuple-element.15), channel_id=1, source_target_pairs={{0,3},{1,0},{2,1},{3,2},{4,7},{5,4},{6,5},{7,6},{8,11},{9,8},{10,9... | collective-permute-start | bytes 393224 | tf_op jit(solution)/shard_map/ppermute | solution.py:33
  169.9 8.9 %collective-permute-start.12 = (bf16[128,512]{1,0:T(8,128)(2,1)S(1)}, bf16[128,512]{1,0:T(8,128)(2,1)S(1)}, u32[]{:S(2)}, u32[]{:S(2)}) collective-permute-start(bf16[128,512]{1,0:T(8,128)(2,1)S(1)} %subtract_convert_fusion.1), channel_id=1, source_target_pairs={{0,1},{1,0},{2,3},{3,2},{4,5},{5,4},{6,7},{7,6},{8,9},{9,8},{10,11... | collective-permute-start | bytes 393224 | tf_op jit(solution)/shard_map/ppermute | solution.py:29
  181.0 37.2 %all-to-all-start.3 = ((bf16[16,48,512]{2,1,0:T(8,128)(2,1)}), bf16[16,48,512]{2,1,0:T(8,128)(2,1)S(1)}, u32[]{:S(2)}, u32[]{:S(2)}) async-start(bf16[16,48,512]{2,1,0:T(8,128)(2,1)} %bitcast.38), calls=%async_computation.3 | async-start | bytes 1572864 | tf_op jit(solution)/shard_map/all_to_all | solution.py:153
  190.8 21.2 %collective-permute-start.13 = (bf16[128,768]{1,0:T(8,128)(2,1)}, bf16[128,768]{1,0:T(8,128)(2,1)}, u32[]{:S(2)}, u32[]{:S(2)}) collective-permute-start(bf16[128,768]{1,0:T(8,128)(2,1)} %convolution_convert_fusion), channel_id=1, source_target_pairs={{0,1},{1,0},{2,3},{3,2},{4,5},{5,4},{6,7},{7,6},{8,9},{9,8},{10,11... | collective-permute-start | bytes 589832 | tf_op jit(solution)/shard_map/ppermute | solution.py:29
  195.8 19.5 %copy-start.4 = (bf16[128,512]{1,0:T(8,128)(2,1)S(1)}, bf16[128,512]{1,0:T(8,128)(2,1)}, u32[]{:S(2)}) copy-start(bf16[128,512]{1,0:T(8,128)(2,1)} %param.5) | copy-start | bytes 393220

commit v4 on v1

--- a/solution.py
+++ b/solution.py
@@ -25,10 +25,6 @@
 
 def swapped(array):
     return lax.ppermute(array, PAIR, [(0, 1), (1, 0)])
-
-
-def shifted(array, distance):
-    return lax.ppermute(array, Z, [(k, (k + distance) % NZ) for k in range(NZ)])
 
 
 def inv_norm(embedding):
@@ -72,6 +68,7 @@
     txt_unit = (txt_emb * txt_inv).astype(jnp.bfloat16)
     texts = lax.all_gather(txt_unit, Y, axis=0, tiled=True)
     returned = swapped(partner_part)
+    other_head = swapped(head)
 
     img_emb = matmul(kept, head) + returned.astype(jnp.float32)
     img_inv = inv_norm(img_emb)
@@ -82,7 +79,8 @@
     row_part = jnp.sum(exps, axis=1)
     col_part = jnp.sum(exps, axis=0)
 
-    col_sum = jnp.sum(to_all(col_part.reshape(NY, rows), Y, NY), axis=0).reshape(NY * rows)
+    col_parts = to_all(col_part.reshape(NY, rows), Y, NY)
+    col_sum = jnp.sum(col_parts, axis=0).reshape(NY * rows)
     row_sum = lax.psum(row_part, Z)
 
     i = lax.broadcasted_iota(jnp.int32, exps.shape, 0) - b * rows
@@ -97,13 +95,14 @@
         txt_part.astype(jnp.bfloat16), Y, scatter_dimension=0, tiled=True
     )
     origin = jnp.uint32(0)
-    img_sum = lax.dynamic_slice(
-        img_part, (b.astype(jnp.uint32) * rows, origin), (rows, emb_width)
+    img_grads = lax.all_to_all(
+        img_part.astype(jnp.bfloat16).reshape(NZ, rows, emb_width), Z, 0, 0, tiled=True
     )
-    for k in range(1, NZ):
-        start = ((b + NZ - k) & (NZ - 1)).astype(jnp.uint32) * rows
-        piece = lax.dynamic_slice(img_part, (start, origin), (rows, emb_width))
-        img_sum = img_sum + shifted(piece.astype(jnp.bfloat16), -k).astype(jnp.float32)
+    img_own = lax.dynamic_slice(
+        img_part, (b.astype(jnp.uint32) * rows, jnp.uint32(0)), (rows, emb_width)
+    )
+    ids = jnp.arange(NZ, dtype=jnp.int32)[:, None, None]
+    img_sum = img_own + jnp.sum(jnp.where(ids == b, 0.0, img_grads.astype(jnp.float32)), axis=0)
     img_emb_grad = norm_backward(img_emb, img_inv, scale * img_sum)
     partner_grad = swapped(img_emb_grad)
 
@@ -112,7 +111,7 @@
         head_part.astype(jnp.bfloat16).reshape(NQ * NZ, padded, emb_width), SAME, 0, 0, tiled=True
     )
     kept_grad = matmul(img_emb_grad, head, 1, 1).astype(jnp.bfloat16)
-    given_grad = swapped(matmul(partner_grad, head, 1, 1).astype(jnp.bfloat16))
+    given_grad = matmul(img_emb_grad, other_head, 1, 1).astype(jnp.bfloat16)
     image_features_grad = (
         matmul(kept_grad, choice[:, :half], 1, 1) + matmul(given_grad, choice[:, half:], 1, 1)
     ).astype(jnp.bfloat16)

time: 184 us -> 178 us (0.967); the launches traced: 183 us -> 174 us
  starting transfers between devices: 55.3 us -> 47.1 us
    reduce_scatter x1, waiting for transfers between devices: 0.01 us -> 18.3 us  [local(): lax.psum_scatter(txt_part.astype(jnp.bfloat16), Y, scatter_dimension=0, t...]
    ppermute x4, waiting for transfers between devices: 39.1 us -> 24.2 us  [swapped(): return lax.ppermute(array, PAIR, [(0, 1), (1, 0)])]
    ppermute x3 -> x0, starting transfers between devices: 11.9 us -> none  [shifted(): return lax.ppermute(array, Z, [(k, (k + distance) % NZ) for k in range(NZ)])]
    all_to_all x0 -> x1, waiting for transfers between devices: none -> 4.88 us  [local(): lax.all_to_all(img_part.astype(jnp.bfloat16).reshape(NZ, rows, emb_width)...]
    all_to_all x0 -> x1, starting transfers between devices: none -> 4.16 us  [local(): lax.all_to_all(img_part.astype(jnp.bfloat16).reshape(NZ, rows, emb_width)...]
    ppermute x3 -> x0, waiting for transfers between devices: 3.84 us -> none  [shifted(): return lax.ppermute(array, Z, [(k, (k + distance) % NZ) for k in range(NZ)])]
    all_to_all x1, waiting for transfers between devices: 2.55 us -> 0.01 us  [local(): lax.all_to_all(head_part.astype(jnp.bfloat16).reshape(NQ * NZ, padded, em...]
    dot_general x12 -> x11, matrix products: 21.8 us -> 21 us  [matmul(): lax.dot_general(left, right, (((left_dim,), (right_dim,)), ((), ())), pre...]
  transfers between devices with their start and end apart: 12 -> 10, of which waited for: 8 -> 6; matrix products, arithmetic and copies ran while one was open for 12% -> 13% of each run, Pallas kernels for 0% -> 0%
where the time goes in v4:
time: 178 us; the launch traced here: 174 us
  waiting for transfers between devices  51 us (29%)
  starting transfers between devices  47.1 us (26%)
  blocking collectives  26.8 us (15%)
  matrix products  21 us (12%)
  between operations  15 us (8%)
  other arithmetic  10.9 us (6%)
  local copies, waits for them, and re-layouts  2.51 us (1%)
    ppermute x4, waiting for transfers between devices, swapped(): return lax.ppermute(array, PAIR, [(0, 1), (1, 0)])  24.2 us
    all_to_all x2, starting transfers between devices, to_all(): return lax.all_to_all(copies, axes, 0, 0, tiled=True)  21.9 us
    dot_general x11, matrix products, matmul(): lax.dot_general(left, right, (((left_dim,), (right_dim,)), ((), ())), pre...  21 us
    reduce_scatter x1, waiting for transfers between devices, local(): lax.psum_scatter(txt_part.astype(jnp.bfloat16), Y, scatter_dimension=0, t...  18.3 us
    all_gather x1, blocking collectives, local(): images = lax.all_gather(img_unit, Z, axis=0, tiled=True)  16.2 us
    ppermute x4, starting transfers between devices, swapped(): return lax.ppermute(array, PAIR, [(0, 1), (1, 0)])  12 us
    psum x1, blocking collectives, local(): row_sum = lax.psum(row_part, Z)  10.6 us
    all_to_all x1, starting transfers between devices, local(): lax.all_to_all(head_part.astype(jnp.bfloat16).reshape(NQ * NZ, padded, em...  8.99 us
  transfers between devices with their start and end apart: 10, of which 6 were waited for; matrix products, arithmetic and copies ran while one was open for 13% of the time, Pallas kernels for 0%

profile of v4, /device:TPU:6, one launch (start us, length us, event | category | flops | bytes accessed | tf_op | source)
XLA Modules:
  0.0 174.4 jit_solution(224766303005962860)
XLA Ops:
  7.2 0.0 copy-start
  7.2 0.0 copy-start.2
  7.2 0.9 pad.4
  8.1 1.0 broadcast_in_dim.42
  9.0 15.7 %all-to-all-start = ((bf16[16,48,512]{2,1,0:T(8,128)(2,1)}), bf16[16,48,512]{2,1,0:T(8,128)(2,1)S(1)}, u32[]{:S(2)}, u32[]{:S(2)}) async-start(bf16[16,48,512]{2,1,0:T(8,128)(2,1)} %broadcast_in_dim.42), calls=%async_computation | async-start | bytes 1572864 | tf_op jit(solution)/shard_map/all_to_all | solution.py:23
  24.7 0.0 all-gather.2.cloned.1.call-start
  24.8 0.0 copy-done.2
  24.8 0.1 fusion.15
  24.9 0.8 fusion.16
  25.7 0.0 all-gather.2.cloned.1.call-update
  25.7 1.8 %iota_compare_fusion = pred[1408,1536]{1,0:T(32,128)(4,1)S(1)} fusion(s32[1536]{0:T(1024)S(1)} %fusion.28), kind=kLoop, calls=%fused_computation | loop fusion | flops 2162688 | bytes 2168832 | tf_op jit(solution)/shard_map/eq | solution.py:46
  27.5 0.0 copy-done
  27.5 0.0 copy-start.1
  27.6 1.6 fusion.14
  29.1 2.6 %collective-permute-start = (bf16[128,768]{0,1:T(8,128)(2,1)}, bf16[128,768]{0,1:T(8,128)(2,1)}, u32[]{:S(2)}, u32[]{:S(2)}) collective-permute-start(bf16[128,768]{0,1:T(8,128)(2,1)} %fusion.14), channel_id=1, source_target_pairs={{0,4},{4,0},{1,5},{5,1},{2,6},{6,2},{3,7},{7,3},{8,12},{12,8},{9,1... | collective-permute-start | bytes 589832 | tf_op jit(solution)/shard_map/ppermute | solution.py:27
  31.7 0.0 copy-done.1
  31.7 0.9 fusion.13
  32.6 0.0 copy-start.6
  32.6 16.1 %collective-permute-done = bf16[128,768]{0,1:T(8,128)(2,1)} collective-permute-done((bf16[128,768]{0,1:T(8,128)(2,1)}, bf16[128,768]{0,1:T(8,128)(2,1)}, u32[]{:S(2)}, u32[]{:S(2)}) %collective-permute-start) | collective-permute-done | bytes 196640 | tf_op jit(solution)/shard_map/ppermute | solution.py:27
  48.7 3.7 %all-to-all-done = bf16[16,48,512]{2,1,0:T(8,128)(2,1)S(1)} async-done(((bf16[16,48,512]{2,1,0:T(8,128)(2,1)}), bf16[16,48,512]{2,1,0:T(8,128)(2,1)S(1)}, u32[]{:S(2)}, u32[]{:S(2)}) %all-to-all-start) | async-done | bytes 786464 | tf_op jit(solution)/shard_map/all_to_all | solution.py:23
  52.4 1.2 convolution_convert_fusion.3
  53.6 1.9 %collective-permute-start.1 = (bf16[128,512]{1,0:T(8,128)(2,1)S(1)}, bf16[128,512]{1,0:T(8,128)(2,1)S(1)}, u32[]{:S(2)}, u32[]{:S(2)}) collective-permute-start(bf16[128,512]{1,0:T(8,128)(2,1)S(1)} %convolution_convert_fusion.3), channel_id=1, source_target_pairs={{0,4},{4,0},{1,5},{5,1},{2,6},{6,2},{3,7},{7,3},{8,12},{12,8},{9,1... | collective-permute-start | bytes 393224 | tf_op jit(solution)/shard_map/ppermute | solution.py:27
  56.2 5.1 %collective-permute-done.1 = bf16[128,512]{1,0:T(8,128)(2,1)S(1)} collective-permute-done((bf16[128,512]{1,0:T(8,128)(2,1)S(1)}, bf16[128,512]{1,0:T(8,128)(2,1)S(1)}, u32[]{:S(2)}, u32[]{:S(2)}) %collective-permute-start.1) | collective-permute-done | bytes 131104 | tf_op jit(solution)/shard_map/ppermute | solution.py:27
  61.4 0.0 copy-start.4
  61.4 0.4 multiply_reduce_fusion.1
  61.8 0.1 multiply_convert_fusion
  61.9 16.2 %all_gather.6 = bf16[512,512]{1,0:T(8,128)(2,1)S(1)} all-gather(bf16[128,512]{1,0:T(8,128)(2,1)S(1)} %multiply_convert_fusion), channel_id=1, replica_groups=mesh['rep'=16,'dp_q'=4,'dp_pair'=2,'dp_z'=4] {'dp_z'}, dimensions={0}, use_global_device_ids=true | all-gather | bytes 655360 | tf_op jit(solution)/shard_map/all_gather | solution.py:76
  78.1 0.0 copy-start.8
  78.1 3.5 %fusion.46 = (f32[512]{0:T(512)S(1)}, f32[1024]{0:T(1024)S(1)}, f32[512,1024]{1,0:T(8,128)}) fusion(bf16[512,512]{1,0:T(8,128)(2,1)S(1)} %all_gather.6, bf16[1024,512]{1,0:T(8,128)(2,1)} %all-gather.2.cloned.1.call-done, f32[]{:T(128)} %bitcast.31), kind=kOutput, calls=%fused_computation.93 | convolution fusion | flops 538442240 | bytes 3676164 | tf_op jit(solution)/shard_map/dot_general | solution.py:16
  81.6 0.0 copy-done.6
  81.6 0.0 copy-done.4
  81.6 0.0 copy-done.8
  81.6 0.6 broadcast_in_dim.44
  82.3 6.2 %all-to-all-start.1 = ((f32[8,8,128]{2,1,0:T(8,128)}), f32[8,8,128]{2,1,0:T(8,128)S(1)}, u32[]{:S(2)}, u32[]{:S(2)}) async-start(f32[8,8,128]{2,1,0:T(8,128)} %broadcast_in_dim.44), calls=%async_computation.1 | async-start | bytes 65536 | tf_op jit(solution)/shard_map/all_to_all | solution.py:23
  88.5 10.6 %psum.7 = f32[512]{0:T(512)S(1)} all-reduce(f32[512]{0:T(512)S(1)} %get-tuple-element.3), channel_id=1, replica_groups=mesh['rep'=16,'dp_q'=4,'dp_pair'=2,'dp_z'=4] {'dp_z'}, use_global_device_ids=true, to_apply=%region_3.4 | all-reduce | flops 512 | bytes 4096 | tf_op jit(solution)/shard_map/psum | solution.py:84
  99.1 0.0 all-to-all-done.1
  99.1 2.1 %subtract_convert_fusion = bf16[512,1024]{1,0:T(8,128)(2,1)S(1)} fusion(f32[512,1024]{1,0:T(8,128)} %get-tuple-element.11, s32[1024]{0:T(1024)S(1)} %iota_subtract_fusion, f32[1024]{0:T(1024)S(1)} %divide_bitcast_fusion, f32[512]{0:T(512)S(1)} %broadcast_divide_fusion, s32[512]{0:T(512)S(1)} %iota_subtract_fusion.1, pred[512]{0:T(512)(128)(4,1)S(1)} %get-tuple-element.14, ...), kind=kLoop, calls=%fused_computation.11 | loop fusion | flops 4194304 | bytes 3159040 | tf_op jit(solution)/shard_map/convert_element_type | solution.py:90
  101.2 2.7 %fusion.47 = (bf16[512,512]{1,0:T(8,128)(2,1)}, f32[512,512]{1,0:T(8,128)S(1)}) fusion(bf16[512,1024]{1,0:T(8,128)(2,1)S(1)} %subtract_convert_fusion, bf16[1024,512]{1,0:T(8,128)(2,1)} %all-gather.2.cloned.1.call-done), kind=kOutput, calls=%fused_computation.94 | convolution fusion | flops 537133056 | bytes 3670016 | tf_op jit(solution)/shard_map/dot_general | solution.py:16
  104.0 4.2 %all-to-all-start.2 = ((bf16[4,128,512]{2,1,0:T(8,128)(2,1)}), bf16[4,128,512]{2,1,0:T(8,128)(2,1)}, u32[]{:S(2)}, u32[]{:S(2)}) async-start(bf16[4,128,512]{2,1,0:T(8,128)(2,1)} %bitcast.39), calls=%async_computation.2 | async-start | bytes 1048576 | tf_op jit(solution)/shard_map/all_to_all | solution.py:98
  108.1 0.0 reduce-scatter.2.cloned.1.call-start
  108.2 3.9 %collective-permute-start.2 = (bf16[768,512]{1,0:T(8,128)(2,1)S(1)}, bf16[768,512]{1,0:T(8,128)(2,1)}, u32[]{:S(2)}, u32[]{:S(2)}) collective-permute-start(bf16[768,512]{1,0:T(8,128)(2,1)S(1)} %bitcast.37), channel_id=1, source_target_pairs={{0,4},{4,0},{1,5},{5,1},{2,6},{6,2},{3,7},{7,3},{8,12},{12,8},{9,1... | collective-permute-start | bytes 2359304 | tf_op jit(solution)/shard_map/ppermute | solution.py:27
  112.1 2.8 %convolution_convert_fusion = bf16[1024,512]{1,0:T(8,128)(2,1)} fusion(bf16[512,1024]{1,0:T(8,128)(2,1)S(1)} %subtract_convert_fusion, bf16[512,512]{1,0:T(8,128)(2,1)} %copy-done.8), kind=kOutput, calls=%fused_computation.15 | convolution fusion | flops 537395200 | bytes 2621440 | tf_op jit(solution)/shard_map/dot_general | solution.py:16
  114.9 0.0 reduce-scatter.2.cloned.1.call-update
  114.9 4.9 %all-to-all-done.2 = bf16[4,128,512]{2,1,0:T(8,128)(2,1)} async-done(((bf16[4,128,512]{2,1,0:T(8,128)(2,1)}), bf16[4,128,512]{2,1,0:T(8,128)(2,1)}, u32[]{:S(2)}, u32[]{:S(2)}) %all-to-all-start.2) | async-done | bytes 524320 | tf_op jit(solution)/shard_map/all_to_all | solution.py:98
  119.8 1.2 select_reduce_fusion
  121.1 1.1 multiply_reduce_fusion
  122.1 0.0 copy-done.5
  122.1 0.1 subtract_convert_fusion.1
  122.3 3.6 %collective-permute-start.3 = (bf16[128,512]{1,0:T(8,128)(2,1)S(1)}, bf16[128,512]{1,0:T(8,128)(2,1)S(1)}, u32[]{:S(2)}, u32[]{:S(2)}) collective-permute-start(bf16[128,512]{1,0:T(8,128)(2,1)S(1)} %subtract_convert_fusion.1), channel_id=1, source_target_pairs={{0,4},{4,0},{1,5},{5,1},{2,6},{6,2},{3,7},{7,3},{8,12},{12,8},{9,1... | collective-permute-start | bytes 393224 | tf_op jit(solution)/shard_map/ppermute | solution.py:27
  125.8 0.0 copy-done.7
  125.9 0.3 fusion.48
  126.2 2.9 %collective-permute-done.3 = bf16[128,512]{1,0:T(8,128)(2,1)S(1)} collective-permute-done((bf16[128,512]{1,0:T(8,128)(2,1)S(1)}, bf16[128,512]{1,0:T(8,128)(2,1)S(1)}, u32[]{:S(2)}, u32[]{:S(2)}) %collective-permute-start.3) | collective-permute-done | bytes 131104 | tf_op jit(solution)/shard_map/ppermute | solution.py:27
  129.1 2.2 %add_convert_fusion = bf16[768,512]{1,0:T(8,128)(2,1)} fusion(f32[768,512]{1,0:T(8,128)S(1)} %fusion.48, bf16[128,768]{0,1:T(8,128)(2,1)} %collective-permute-done, bf16[128,512]{1,0:T(8,128)(2,1)S(1)} %collective-permute-done.3), kind=kOutput, calls=%fused_computation.14 | convolution fusion | flops 101449728 | bytes 2686976 | tf_op jit(solution)/shard_map/dot_general | solution.py:16
  131.3 9.0 %all-to-all-start.3 = ((bf16[16,48,512]{2,1,0:T(8,128)(2,1)}), bf16[16,48,512]{2,1,0:T(8,128)(2,1)S(1)}, u32[]{:S(2)}, u32[]{:S(2)}) async-start(bf16[16,48,512]{2,1,0:T(8,128)(2,1)} %bitcast.6), calls=%async_computation.4 | async-start | bytes 1572864 | tf_op jit(solution)/shard_map/all_to_all | solution.py:110
  140.3 0.0 collective-permute-done.2
  140.3 2.4 %fusion = f32[128,1408]{1,0:T(8,128)S(1)} fusion(pred[1408,1536]{1,0:T(32,128)(4,1)} %copy-done.1, bf16[128,512]{1,0:T(8,128)(2,1)S(1)} %subtract_convert_fusion.1, bf16[768,512]{1,0:T(8,128)(2,1)} %collective-permute-done.2), kind=kOutput, calls=%fused_computation.1 | convolution fusion | flops 377585664 | bytes 2719744 | tf_op jit(solution)/shard_map/dot_general | solution.py:16
  142.8 0.0 copy-start.3
  142.8 3.0 %fusion.7 = bf16[128,1408]{1,0:T(8,128)(2,1)} fusion(f32[128,1408]{1,0:T(8,128)S(1)} %fusion, pred[1408,1536]{1,0:T(32,128)(4,1)} %copy-done.1, bf16[128,512]{1,0:T(8,128)(2,1)S(1)} %subtract_convert_fusion.1, bf16[768,512]{1,0:T(8,128)(2,1)S(1)} %bitcast.38), kind=kOutput, calls=%fused_computation.8 | convolution fusion | flops 377946112 | bytes 3080192 | tf_op jit(solution)/shard_map/dot_general | solution.py:16
  145.8 18.3 %reduce-scatter.2.cloned.1.call-done = bf16[128,512]{1,0:T(8,128)(2,1)} async-done(((bf16[1024,512]{1,0:T(8,128)(2,1)}), bf16[128,512]{1,0:T(8,128)(2,1)}) %reduce-scatter.2.cloned.1.call-update) | async-done | bytes 131088 | tf_op jit(solution)/shard_map/reduce_scatter | solution.py:94
  164.0 0.0 copy-done.3
  164.0 1.0 fusion.20
  165.1 1.7 fusion.19
  166.8 0.0 all-to-all-done.3
  166.8 0.8 convert_reduce_fusion
  (13 shorter events, 0.1 us)
Async XLA Ops:
  7.2 20.4 %copy-start = (bf16[128,1408]{1,0:T(8,128)(2,1)S(1)}, bf16[128,1408]{1,0:T(8,128)(2,1)}, u32[]{:S(2)}) copy-start(bf16[128,1408]{1,0:T(8,128)(2,1)} %param.4) | copy-start | bytes 1081348
  7.2 17.6 %copy-start.2 = (bf16[128,512]{1,0:T(8,128)(2,1)S(1)}, bf16[128,512]{1,0:T(8,128)(2,1)}, u32[]{:S(2)}) copy-start(bf16[128,512]{1,0:T(8,128)(2,1)} %param.5) | copy-start | bytes 393220
  9.0 43.4 %all-to-all-start = ((bf16[16,48,512]{2,1,0:T(8,128)(2,1)}), bf16[16,48,512]{2,1,0:T(8,128)(2,1)S(1)}, u32[]{:S(2)}, u32[]{:S(2)}) async-start(bf16[16,48,512]{2,1,0:T(8,128)(2,1)} %broadcast_in_dim.42), calls=%async_computation | async-start | bytes 1572864 | tf_op jit(solution)/shard_map/all_to_all | solution.py:23
  24.7 53.4 %all-gather.2.cloned.1.call-start = ((), (), s32[]{:S(2)}) async-start(), calls=%async_computation.5 | async-start | bytes 1179648 | tf_op jit(solution)/shard_map/all_gather | solution.py:69
  27.5 4.2 %copy-start.1 = (pred[1408,1536]{1,0:T(32,128)(4,1)}, pred[1408,1536]{1,0:T(32,128)(4,1)S(1)}, u32[]{:S(2)}) copy-start(pred[1408,1536]{1,0:T(32,128)(4,1)S(1)} %iota_compare_fusion) | copy-start | bytes 6488068
  29.1 19.6 %collective-permute-start = (bf16[128,768]{0,1:T(8,128)(2,1)}, bf16[128,768]{0,1:T(8,128)(2,1)}, u32[]{:S(2)}, u32[]{:S(2)}) collective-permute-start(bf16[128,768]{0,1:T(8,128)(2,1)} %fusion.14), channel_id=1, source_target_pairs={{0,4},{4,0},{1,5},{5,1},{2,6},{6,2},{3,7},{7,3},{8,12},{12,8},{9,1... | collective-permute-start | bytes 589832 | tf_op jit(solution)/shard_map/ppermute | solution.py:27
  32.6 49.0 %copy-start.6 = (bf16[768,128]{1,0:T(8,128)(2,1)}, bf16[768,128]{1,0:T(8,128)(2,1)S(1)}, u32[]{:S(2)}) copy-start(bf16[768,128]{1,0:T(8,128)(2,1)S(1)} %fusion.13) | copy-start | bytes 589828
  53.6 7.8 %collective-permute-start.1 = (bf16[128,512]{1,0:T(8,128)(2,1)S(1)}, bf16[128,512]{1,0:T(8,128)(2,1)S(1)}, u32[]{:S(2)}, u32[]{:S(2)}) collective-permute-start(bf16[128,512]{1,0:T(8,128)(2,1)S(1)} %convolution_convert_fusion.3), channel_id=1, source_target_pairs={{0,4},{4,0},{1,5},{5,1},{2,6},{6,2},{3,7},{7,3},{8,12},{12,8},{9,1... | collective-permute-start | bytes 393224 | tf_op jit(solution)/shard_map/ppermute | solution.py:27
  61.4 20.3 %copy-start.4 = (bf16[128,512]{1,0:T(8,128)(2,1)}, bf16[128,512]{1,0:T(8,128)(2,1)S(1)}, u32[]{:S(2)}) copy-start(bf16[128,512]{1,0:T(8,128)(2,1)S(1)} %collective-permute-done.1) | copy-start | bytes 393220
  78.1 3.5 %copy-start.8 = (bf16[512,512]{1,0:T(8,128)(2,1)}, bf16[512,512]{1,0:T(8,128)(2,1)S(1)}, u32[]{:S(2)}) copy-start(bf16[512,512]{1,0:T(8,128)(2,1)S(1)} %all_gather.6) | copy-start | bytes 1572868
  82.3 16.8 %all-to-all-start.1 = ((f32[8,8,128]{2,1,0:T(8,128)}), f32[8,8,128]{2,1,0:T(8,128)S(1)}, u32[]{:S(2)}, u32[]{:S(2)}) async-start(f32[8,8,128]{2,1,0:T(8,128)} %broadcast_in_dim.44), calls=%async_computation.1 | async-start | bytes 65536 | tf_op jit(solution)/shard_map/all_to_all | solution.py:23
  104.0 15.8 %all-to-all-start.2 = ((bf16[4,128,512]{2,1,0:T(8,128)(2,1)}), bf16[4,128,512]{2,1,0:T(8,128)(2,1)}, u32[]{:S(2)}, u32[]{:S(2)}) async-start(bf16[4,128,512]{2,1,0:T(8,128)(2,1)} %bitcast.39), calls=%async_computation.2 | async-start | bytes 1048576 | tf_op jit(solution)/shard_map/all_to_all | solution.py:98
  108.1 55.9 %reduce-scatter.2.cloned.1.call-start = ((), (), s32[]{:S(2)}) async-start(), calls=%async_computation.6 | async-start | bytes 1179648 | tf_op jit(solution)/shard_map/reduce_scatter | solution.py:94
  108.2 32.1 %collective-permute-start.2 = (bf16[768,512]{1,0:T(8,128)(2,1)S(1)}, bf16[768,512]{1,0:T(8,128)(2,1)}, u32[]{:S(2)}, u32[]{:S(2)}) collective-permute-start(bf16[768,512]{1,0:T(8,128)(2,1)S(1)} %bitcast.37), channel_id=1, source_target_pairs={{0,4},{4,0},{1,5},{5,1},{2,6},{6,2},{3,7},{7,3},{8,12},{12,8},{9,1... | collective-permute-start | bytes 2359304 | tf_op jit(solution)/shard_map/ppermute | solution.py:27
  114.9 7.2 %copy-start.5 = (bf16[128,512]{1,0:T(8,128)(2,1)S(1)}, bf16[128,512]{1,0:T(8,128)(2,1)}, u32[]{:S(2)}) copy-start(bf16[128,512]{1,0:T(8,128)(2,1)} %copy-done.4) | copy-start | bytes 393220
  114.9 10.9 %copy-start.7 = (bf16[768,128]{1,0:T(8,128)(2,1)S(1)}, bf16[768,128]{1,0:T(8,128)(2,1)}, u32[]{:S(2)}) copy-start(bf16[768,128]{1,0:T(8,128)(2,1)} %copy-done.6) | copy-start | bytes 589828
  122.3 6.9 %collective-permute-start.3 = (bf16[128,512]{1,0:T(8,128)(2,1)S(1)}, bf16[128,512]{1,0:T(8,128)(2,1)S(1)}, u32[]{:S(2)}, u32[]{:S(2)}) collective-permute-start(bf16[128,512]{1,0:T(8,128)(2,1)S(1)} %subtract_convert_fusion.1), channel_id=1, source_target_pairs={{0,4},{4,0},{1,5},{5,1},{2,6},{6,2},{3,7},{7,3},{8,12},{12,8},{9,1... | collective-permute-start | bytes 393224 | tf_op jit(solution)/shard_map/ppermute | solution.py:27
  131.3 35.5 %all-to-all-start.3 = ((bf16[16,48,512]{2,1,0:T(8,128)(2,1)}), bf16[16,48,512]{2,1,0:T(8,128)(2,1)S(1)}, u32[]{:S(2)}, u32[]{:S(2)}) async-start(bf16[16,48,512]{2,1,0:T(8,128)(2,1)} %bitcast.6), calls=%async_computation.4 | async-start | bytes 1572864 | tf_op jit(solution)/shard_map/all_to_all | solution.py:110
  142.8 21.3 %copy-start.3 = (bf16[128,512]{1,0:T(8,128)(2,1)S(1)}, bf16[128,512]{1,0:T(8,128)(2,1)}, u32[]{:S(2)}) copy-start(bf16[128,512]{1,0:T(8,128)(2,1)} %param.5) | copy-start | bytes 393220
Sparse Core Ops, SparseCore 0:
  28.2 42.0 all-gather.1
  115.1 48.9 reduce-scatter.1

commit v5 on v4

--- a/solution.py
+++ b/solution.py
@@ -1,6 +1,8 @@
 import jax
 import jax.numpy as jnp
 from jax import lax
+from jax.experimental import pallas as pl
+from jax.experimental.pallas import tpu as pltpu
 from jax.sharding import Mesh
 from jax.sharding import PartitionSpec as P
 
@@ -25,6 +27,49 @@
 
 def swapped(array):
     return lax.ppermute(array, PAIR, [(0, 1), (1, 0)])
+
+
+def coef_kernel(place, exps, row_inv, col_inv, images, texts, img_sent, img_own, txt_sent, coef, img_part):
+    a, b = place[0], place[1]
+    rows = img_own.shape[0]
+    eye = lax.broadcasted_iota(jnp.int32, (rows, rows), 0) == lax.broadcasted_iota(
+        jnp.int32, (rows, rows), 1
+    )
+    for r in range(NZ):
+        at_row = slice(r * rows, (r + 1) * rows)
+        inverse = row_inv[at_row, :]
+        for c in range(NY):
+            at = (at_row, slice(c * rows, (c + 1) * rows))
+            label = jnp.where(eye, jnp.where((a == c) & (b == r), 2.0, 0.0), 0.0)
+            coef[at] = (exps[at] * (inverse + col_inv[c : c + 1, :]) - label).astype(jnp.bfloat16)
+    img_part[...] = jnp.dot(coef[...], texts[...], preferred_element_type=jnp.float32)
+    img_sent[...] = img_part[...].astype(jnp.bfloat16)
+    img_own[...] = img_part[pl.ds(pl.multiple_of(b * rows, rows), rows), :]
+    txt_sent[...] = lax.dot_general(
+        coef[...], images[...], (((0,), (0,)), ((), ())), preferred_element_type=jnp.float32
+    ).astype(jnp.bfloat16)
+
+
+def coef_products(place, exps, row_inv, col_inv, images, texts):
+    rows = row_inv.shape[1]
+    smem = pl.BlockSpec(memory_space=pltpu.SMEM)
+    vmem = pl.BlockSpec(memory_space=pltpu.VMEM)
+    width = images.shape[1]
+    return pl.pallas_call(
+        coef_kernel,
+        in_specs=[smem] + [vmem] * 5,
+        out_specs=[vmem] * 3,
+        out_shape=[
+            jax.ShapeDtypeStruct(images.shape, jnp.bfloat16),
+            jax.ShapeDtypeStruct((rows, width), jnp.float32),
+            jax.ShapeDtypeStruct(texts.shape, jnp.bfloat16),
+        ],
+        scratch_shapes=[
+            pltpu.VMEM(exps.shape, jnp.bfloat16),
+            pltpu.VMEM(images.shape, jnp.float32),
+        ],
+        name="coef_products",
+    )(place, exps, row_inv, col_inv, images, texts)
 
 
 def inv_norm(embedding):
@@ -58,8 +103,8 @@
     head = to_all(jnp.pad(image_head, ((0, padded - block), (0, 0))), SAME, NQ * NZ)
     head = head.reshape(half, emb_width)
     choice = column_choice(width, padded, block, p)
-    kept = matmul(image_features, choice[:, :half]).astype(jnp.bfloat16)
-    given = matmul(image_features, choice[:, half:]).astype(jnp.bfloat16)
+    own_features = matmul(image_features, choice).astype(jnp.bfloat16)
+    kept, given = own_features[:, :half], own_features[:, half:]
     taken = swapped(given)
     partner_part = matmul(taken, head).astype(jnp.bfloat16)
 
@@ -80,27 +125,15 @@
     col_part = jnp.sum(exps, axis=0)
 
     col_parts = to_all(col_part.reshape(NY, rows), Y, NY)
-    col_sum = jnp.sum(col_parts, axis=0).reshape(NY * rows)
+    col_inv = 1.0 / jnp.sum(col_parts, axis=0)
     row_sum = lax.psum(row_part, Z)
+    row_inv = jnp.broadcast_to((1.0 / row_sum)[:, None], (NZ * rows, rows))
 
-    i = lax.broadcasted_iota(jnp.int32, exps.shape, 0) - b * rows
-    j = lax.broadcasted_iota(jnp.int32, exps.shape, 1) - a * rows
-    label = jnp.where((i == j) & (i >= 0) & (i < rows), 2.0, 0.0)
-    coef = exps * ((1.0 / row_sum)[:, None] + (1.0 / col_sum)[None, :])
-    coef = (coef - label).astype(jnp.bfloat16)
-
-    img_part = matmul(coef, texts)
-    txt_part = matmul(coef, images, 0, 0)
-    txt_sum = lax.psum_scatter(
-        txt_part.astype(jnp.bfloat16), Y, scatter_dimension=0, tiled=True
+    img_sent, img_own, txt_sent = coef_products(
+        jnp.stack([a, b]), exps, row_inv, col_inv, images, texts
     )
-    origin = jnp.uint32(0)
-    img_grads = lax.all_to_all(
-        img_part.astype(jnp.bfloat16).reshape(NZ, rows, emb_width), Z, 0, 0, tiled=True
-    )
-    img_own = lax.dynamic_slice(
-        img_part, (b.astype(jnp.uint32) * rows, jnp.uint32(0)), (rows, emb_width)
-    )
+    txt_sum = lax.psum_scatter(txt_sent, Y, scatter_dimension=0, tiled=True)
+    img_grads = lax.all_to_all(img_sent.reshape(NZ, rows, emb_width), Z, 0, 0, tiled=True)
     ids = jnp.arange(NZ, dtype=jnp.int32)[:, None, None]
     img_sum = img_own + jnp.sum(jnp.where(ids == b, 0.0, img_grads.astype(jnp.float32)), axis=0)
     img_emb_grad = norm_backward(img_emb, img_inv, scale * img_sum)
@@ -112,9 +145,8 @@
     )
     kept_grad = matmul(img_emb_grad, head, 1, 1).astype(jnp.bfloat16)
     given_grad = matmul(img_emb_grad, other_head, 1, 1).astype(jnp.bfloat16)
-    image_features_grad = (
-        matmul(kept_grad, choice[:, :half], 1, 1) + matmul(given_grad, choice[:, half:], 1, 1)
-    ).astype(jnp.bfloat16)
+    feat_grad = jnp.concatenate([kept_grad, given_grad], axis=1)
+    image_features_grad = matmul(feat_grad, choice, 1, 1).astype(jnp.bfloat16)
 
     txt_unit_grad = scale * txt_sum.astype(jnp.float32)
     text_embed_grad = norm_backward(txt_emb, txt_inv, txt_unit_grad)

time: 178 us -> 176 us (0.989); the launches traced: 174 us -> 175 us
  waiting for transfers between devices: 51 us -> 67.3 us
  matrix products: 21 us -> 11.7 us
  starting transfers between devices: 47.1 us -> 42 us
  other arithmetic: 10.9 us -> 6.15 us
  Pallas kernels: 0 us -> 4.44 us
    dot_general x11 -> x9, matrix products: 21 us -> 11.7 us  [matmul(): lax.dot_general(left, right, (((left_dim,), (right_dim,)), ((), ())), pre...]
    all_to_all x2, waiting for transfers between devices: 3.7 us -> 11.8 us  [to_all(): return lax.all_to_all(copies, axes, 0, 0, tiled=True)]
    all_to_all x1, waiting for transfers between devices: 4.88 us -> 9.36 us  [local(): lax.all_to_all(img_sent.reshape(NZ, rows, emb_width), Z, 0, 0, tiled=True)]
    pallas_call x0 -> x1, Pallas kernels: none -> 4.44 us  [coef_products(): pl.pallas_call(coef_kernel, in_specs=[smem] + [vmem] * 5, out_specs=[vmem...]
    ppermute x4, waiting for transfers between devices: 24.2 us -> 28 us  [swapped(): return lax.ppermute(array, PAIR, [(0, 1), (1, 0)])]
    ppermute x4, starting transfers between devices: 12 us -> 9.48 us  [swapped(): return lax.ppermute(array, PAIR, [(0, 1), (1, 0)])]
    all_to_all x1, starting transfers between devices: 8.99 us -> 6.83 us  [local(): lax.all_to_all(head_part.astype(jnp.bfloat16).reshape(NQ * NZ, padded, em...]
    convert_element_type x1 -> x0, other arithmetic: 2.12 us -> none  [local(): coef = (coef - label).astype(jnp.bfloat16)]
  transfers between devices with their start and end apart: 10 -> 10, of which waited for: 6 -> 7; matrix products, arithmetic and copies ran while one was open for 13% -> 7% of each run, Pallas kernels for 0% -> 0%
where the time goes in v5:
time: 176 us; the launch traced here: 175 us
  waiting for transfers between devices  67.3 us (38%)
  starting transfers between devices  42 us (24%)
  blocking collectives  25.2 us (14%)
  between operations  14.9 us (8%)
  matrix products  11.7 us (7%)
  other arithmetic  6.15 us (3%)
  Pallas kernels  4.44 us (3%)
  local copies, waits for them, and re-layouts  3.32 us (2%)
    ppermute x4, waiting for transfers between devices, swapped(): return lax.ppermute(array, PAIR, [(0, 1), (1, 0)])  28 us
    all_to_all x2, starting transfers between devices, to_all(): return lax.all_to_all(copies, axes, 0, 0, tiled=True)  21.9 us
    reduce_scatter x1, waiting for transfers between devices, local(): txt_sum = lax.psum_scatter(txt_sent, Y, scatter_dimension=0, tiled=True)  18 us
    all_gather x1, blocking collectives, local(): images = lax.all_gather(img_unit, Z, axis=0, tiled=True)  16.4 us
    all_to_all x2, waiting for transfers between devices, to_all(): return lax.all_to_all(copies, axes, 0, 0, tiled=True)  11.8 us
    dot_general x9, matrix products, matmul(): lax.dot_general(left, right, (((left_dim,), (right_dim,)), ((), ())), pre...  11.7 us
    ppermute x4, starting transfers between devices, swapped(): return lax.ppermute(array, PAIR, [(0, 1), (1, 0)])  9.48 us
    all_to_all x1, waiting for transfers between devices, local(): lax.all_to_all(img_sent.reshape(NZ, rows, emb_width), Z, 0, 0, tiled=True)  9.36 us
  transfers between devices with their start and end apart: 10, of which 7 were waited for; matrix products, arithmetic and copies ran while one was open for 7% of the time, Pallas kernels for 0%

profile of v5, /device:TPU:6, one launch (start us, length us, event | category | flops | bytes accessed | tf_op | source)
XLA Modules:
  0.0 174.9 jit_solution(6642869333707626407)
XLA Ops:
  7.2 0.0 copy-start
  7.2 0.0 copy-start.2
  7.2 0.9 pad.4
  8.1 1.0 broadcast_in_dim.18
  9.0 15.7 %all-to-all-start = ((bf16[16,48,512]{2,1,0:T(8,128)(2,1)}), bf16[16,48,512]{2,1,0:T(8,128)(2,1)S(1)}, u32[]{:S(2)}, u32[]{:S(2)}) async-start(bf16[16,48,512]{2,1,0:T(8,128)(2,1)} %broadcast_in_dim.18), calls=%async_computation | async-start | bytes 1572864 | tf_op jit(solution)/shard_map/all_to_all | solution.py:25
  24.7 0.0 all-gather.2.cloned.1.call-start
  24.8 0.0 copy-done.2
  24.8 0.1 fusion.16
  24.9 0.8 fusion.17
  25.6 0.0 all-gather.2.cloned.1.call-update
  25.7 0.0 copy-done
  25.7 1.4 fusion.10
  27.1 2.6 %collective-permute-start = (bf16[128,768]{0,1:T(8,128)(2,1)S(1)}, bf16[128,768]{0,1:T(8,128)(2,1)S(1)}, u32[]{:S(2)}, u32[]{:S(2)}) collective-permute-start(bf16[128,768]{0,1:T(8,128)(2,1)S(1)} %slice.13), channel_id=1, source_target_pairs={{0,4},{4,0},{1,5},{5,1},{2,6},{6,2},{3,7},{7,3},{8,12},{12,8},{9,1... | collective-permute-start | bytes 589832 | tf_op jit(solution)/shard_map/ppermute | solution.py:29
  29.7 18.9 %collective-permute-done = bf16[128,768]{0,1:T(8,128)(2,1)S(1)} collective-permute-done((bf16[128,768]{0,1:T(8,128)(2,1)S(1)}, bf16[128,768]{0,1:T(8,128)(2,1)S(1)}, u32[]{:S(2)}, u32[]{:S(2)}) %collective-permute-start) | collective-permute-done | bytes 196640 | tf_op jit(solution)/shard_map/ppermute | solution.py:29
  48.6 3.8 %all-to-all-done = bf16[16,48,512]{2,1,0:T(8,128)(2,1)S(1)} async-done(((bf16[16,48,512]{2,1,0:T(8,128)(2,1)}), bf16[16,48,512]{2,1,0:T(8,128)(2,1)S(1)}, u32[]{:S(2)}, u32[]{:S(2)}) %all-to-all-start) | async-done | bytes 786464 | tf_op jit(solution)/shard_map/all_to_all | solution.py:25
  52.4 0.3 convolution_convert_fusion.2
  52.7 1.9 %collective-permute-start.1 = (bf16[128,512]{1,0:T(8,128)(2,1)S(1)}, bf16[128,512]{1,0:T(8,128)(2,1)S(1)}, u32[]{:S(2)}, u32[]{:S(2)}) collective-permute-start(bf16[128,512]{1,0:T(8,128)(2,1)S(1)} %convolution_convert_fusion.2), channel_id=1, source_target_pairs={{0,4},{4,0},{1,5},{5,1},{2,6},{6,2},{3,7},{7,3},{8,12},{12,8},{9,1... | collective-permute-start | bytes 393224 | tf_op jit(solution)/shard_map/ppermute | solution.py:29
  55.3 0.6 pad_add_fusion.place
  55.9 4.7 %collective-permute-done.1 = bf16[128,512]{1,0:T(8,128)(2,1)S(1)} collective-permute-done((bf16[128,512]{1,0:T(8,128)(2,1)S(1)}, bf16[128,512]{1,0:T(8,128)(2,1)S(1)}, u32[]{:S(2)}, u32[]{:S(2)}) %collective-permute-start.1) | collective-permute-done | bytes 131104 | tf_op jit(solution)/shard_map/ppermute | solution.py:29
  60.6 0.4 multiply_reduce_fusion.1
  61.0 0.1 multiply_convert_fusion
  61.1 16.4 %all_gather.6.images = bf16[512,512]{1,0:T(8,128)(2,1)S(1)} all-gather(bf16[128,512]{1,0:T(8,128)(2,1)S(1)} %multiply_convert_fusion), channel_id=1, replica_groups=mesh['rep'=16,'dp_q'=4,'dp_pair'=2,'dp_z'=4] {'dp_z'}, dimensions={0}, use_global_device_ids=true | all-gather | bytes 655360 | tf_op jit(solution)/shard_map/all_gather | solution.py:121
  77.5 0.0 copy-start.1
  77.5 0.0 all-gather.2.cloned.1.call-done.texts
  77.5 3.6 %fusion.50 = (f32[1024]{0:T(1024)S(1)}, f32[512]{0:T(512)S(1)}, f32[512,1024]{1,0:T(8,128)}) fusion(bf16[512,512]{1,0:T(8,128)(2,1)S(1)} %all_gather.6.images, bf16[1024,512]{1,0:T(8,128)(2,1)} %all-gather.2.cloned.1.call-done.texts, f32[]{:T(128)} %bitcast.24), kind=kOutput, calls=%fused_computation.91 | convolution fusion | flops 538442240 | bytes 3676164 | tf_op jit(solution)/shard_map/dot_general | solution.py:18
  81.0 0.0 copy-done.1
  81.0 8.8 %psum.7 = f32[512]{0:T(512)S(1)} all-reduce(f32[512]{0:T(512)S(1)} %get-tuple-element.10), channel_id=1, replica_groups=mesh['rep'=16,'dp_q'=4,'dp_pair'=2,'dp_z'=4] {'dp_z'}, use_global_device_ids=true, to_apply=%region_3.4 | all-reduce | flops 512 | bytes 4096 | tf_op jit(solution)/shard_map/psum | solution.py:129
  89.8 0.6 broadcast_in_dim.25
  90.4 6.2 %all-to-all-start.1 = ((f32[8,8,128]{2,1,0:T(8,128)}), f32[8,8,128]{2,1,0:T(8,128)S(1)}, u32[]{:S(2)}, u32[]{:S(2)}) async-start(f32[8,8,128]{2,1,0:T(8,128)} %broadcast_in_dim.25), calls=%async_computation.1 | async-start | bytes 65536 | tf_op jit(solution)/shard_map/all_to_all | solution.py:25
  96.7 8.0 %all-to-all-done.1 = f32[8,8,128]{2,1,0:T(8,128)S(1)} async-done(((f32[8,8,128]{2,1,0:T(8,128)}), f32[8,8,128]{2,1,0:T(8,128)S(1)}, u32[]{:S(2)}, u32[]{:S(2)}) %all-to-all-start.1) | async-done | bytes 32800 | tf_op jit(solution)/shard_map/all_to_all | solution.py:25
  104.7 0.6 broadcast_divide_fusion.col_inv
  105.3 0.8 broadcast_in_dim.19.row_inv
  106.1 4.4 %coef_products.1 = (bf16[512,512]{1,0:T(8,128)(2,1)}, f32[128,512]{1,0:T(8,128)}, bf16[1024,512]{1,0:T(8,128)(2,1)}) custom-call(s32[2]{0:T(128)} %pad_add_fusion.place, f32[512,1024]{1,0:T(8,128)} %get-tuple-element.17.exps, f32[512,128]{1,0:T(8,128)} %broadcast_in_dim.19.row_inv, f32[8,128]{1,0:T(8,128)} %broadcast_divide_fusion.col_inv, ...), custom_call_target="tpu_custom_call" | custom-call | tf_op jit(solution)/shard_map/coef_products/pallas_call | solution.py:58
  110.6 0.0 copy-start.3
  110.6 3.8 %all-to-all-start.2 = ((bf16[4,128,512]{2,1,0:T(8,128)(2,1)}), bf16[4,128,512]{2,1,0:T(8,128)(2,1)S(1)}, u32[]{:S(2)}, u32[]{:S(2)}) async-start(bf16[4,128,512]{2,1,0:T(8,128)(2,1)} %bitcast.32), calls=%async_computation.2 | async-start | bytes 1048576 | tf_op jit(solution)/shard_map/all_to_all | solution.py:136
  114.3 0.0 reduce-scatter.2.cloned.1.call-start
  114.3 2.5 %collective-permute-start.2 = (bf16[768,512]{1,0:T(8,128)(2,1)S(1)}, bf16[768,512]{1,0:T(8,128)(2,1)}, u32[]{:S(2)}, u32[]{:S(2)}) collective-permute-start(bf16[768,512]{1,0:T(8,128)(2,1)S(1)} %bitcast.30), channel_id=1, source_target_pairs={{0,4},{4,0},{1,5},{5,1},{2,6},{6,2},{3,7},{7,3},{8,12},{12,8},{9,1... | collective-permute-start | bytes 2359304 | tf_op jit(solution)/shard_map/ppermute | solution.py:29
  116.8 0.0 reduce-scatter.2.cloned.1.call-update
  116.9 9.4 %all-to-all-done.2 = bf16[4,128,512]{2,1,0:T(8,128)(2,1)S(1)} async-done(((bf16[4,128,512]{2,1,0:T(8,128)(2,1)}), bf16[4,128,512]{2,1,0:T(8,128)(2,1)S(1)}, u32[]{:S(2)}, u32[]{:S(2)}) %all-to-all-start.2) | async-done | bytes 524320 | tf_op jit(solution)/shard_map/all_to_all | solution.py:136
  126.2 0.2 select_reduce_fusion
  126.4 0.0 copy-done.3
  126.4 0.1 multiply_reduce_fusion
  126.6 0.1 subtract_convert_fusion
  126.7 2.5 %collective-permute-start.3 = (bf16[128,512]{1,0:T(8,128)(2,1)S(1)}, bf16[128,512]{1,0:T(8,128)(2,1)S(1)}, u32[]{:S(2)}, u32[]{:S(2)}) collective-permute-start(bf16[128,512]{1,0:T(8,128)(2,1)S(1)} %subtract_convert_fusion), channel_id=1, source_target_pairs={{0,4},{4,0},{1,5},{5,1},{2,6},{6,2},{3,7},{7,3},{8,12},{12,8},{9,1... | collective-permute-start | bytes 393224 | tf_op jit(solution)/shard_map/ppermute | solution.py:29
  129.2 0.3 fusion.22
  129.6 4.4 %collective-permute-done.3 = bf16[128,512]{1,0:T(8,128)(2,1)S(1)} collective-permute-done((bf16[128,512]{1,0:T(8,128)(2,1)S(1)}, bf16[128,512]{1,0:T(8,128)(2,1)S(1)}, u32[]{:S(2)}, u32[]{:S(2)}) %collective-permute-start.3) | collective-permute-done | bytes 131104 | tf_op jit(solution)/shard_map/ppermute | solution.py:29
  134.0 1.3 add_convert_fusion
  135.2 6.8 %all-to-all-start.3 = ((bf16[16,48,512]{2,1,0:T(8,128)(2,1)}), bf16[16,48,512]{2,1,0:T(8,128)(2,1)S(1)}, u32[]{:S(2)}, u32[]{:S(2)}) async-start(bf16[16,48,512]{2,1,0:T(8,128)(2,1)} %bitcast.7), calls=%async_computation.4 | async-start | bytes 1572864 | tf_op jit(solution)/shard_map/all_to_all | solution.py:143
  142.1 0.4 convolution_convert_fusion.1
  142.5 0.0 collective-permute-done.2
  142.5 1.5 convolution_convert_fusion
  144.0 2.6 %fusion.9 = bf16[128,1408]{1,0:T(8,128)(2,1)} fusion(s32[1536]{0:T(1024)S(1)} %fusion.33, bf16[128,768]{1,0:T(8,128)(2,1)S(1)} %convolution_convert_fusion, bf16[128,768]{1,0:T(8,128)(2,1)S(1)} %convolution_convert_fusion.1), kind=kOutput, calls=%fused_computation.7 | convolution fusion | flops 556777472 | bytes 759808 | tf_op jit(solution)/shard_map/dot_general | solution.py:18
  146.6 18.0 %reduce-scatter.2.cloned.1.call-done = bf16[128,512]{1,0:T(8,128)(2,1)} async-done(((bf16[1024,512]{1,0:T(8,128)(2,1)}), bf16[128,512]{1,0:T(8,128)(2,1)}) %reduce-scatter.2.cloned.1.call-update) | async-done | bytes 131088 | tf_op jit(solution)/shard_map/reduce_scatter | solution.py:135
  164.6 1.0 fusion.21
  165.6 1.7 fusion.20
  167.3 0.0 all-to-all-done.3
  167.3 0.8 convert_reduce_fusion
  (7 shorter events, 0.1 us)
Async XLA Ops:
  7.2 18.5 %copy-start = (bf16[128,1408]{1,0:T(8,128)(2,1)S(1)}, bf16[128,1408]{1,0:T(8,128)(2,1)}, u32[]{:S(2)}) copy-start(bf16[128,1408]{1,0:T(8,128)(2,1)} %param.4) | copy-start | bytes 1081348
  7.2 17.6 %copy-start.2 = (bf16[128,512]{1,0:T(8,128)(2,1)S(1)}, bf16[128,512]{1,0:T(8,128)(2,1)}, u32[]{:S(2)}) copy-start(bf16[128,512]{1,0:T(8,128)(2,1)} %param.5) | copy-start | bytes 393220
  9.0 43.4 %all-to-all-start = ((bf16[16,48,512]{2,1,0:T(8,128)(2,1)}), bf16[16,48,512]{2,1,0:T(8,128)(2,1)S(1)}, u32[]{:S(2)}, u32[]{:S(2)}) async-start(bf16[16,48,512]{2,1,0:T(8,128)(2,1)} %broadcast_in_dim.18), calls=%async_computation | async-start | bytes 1572864 | tf_op jit(solution)/shard_map/all_to_all | solution.py:25
  24.7 52.8 %all-gather.2.cloned.1.call-start = ((), (), s32[]{:S(2)}) async-start(), calls=%async_computation.5 | async-start | bytes 1179648 | tf_op jit(solution)/shard_map/all_gather | solution.py:114
  27.1 21.5 %collective-permute-start = (bf16[128,768]{0,1:T(8,128)(2,1)S(1)}, bf16[128,768]{0,1:T(8,128)(2,1)S(1)}, u32[]{:S(2)}, u32[]{:S(2)}) collective-permute-start(bf16[128,768]{0,1:T(8,128)(2,1)S(1)} %slice.13), channel_id=1, source_target_pairs={{0,4},{4,0},{1,5},{5,1},{2,6},{6,2},{3,7},{7,3},{8,12},{12,8},{9,1... | collective-permute-start | bytes 589832 | tf_op jit(solution)/shard_map/ppermute | solution.py:29
  52.7 7.9 %collective-permute-start.1 = (bf16[128,512]{1,0:T(8,128)(2,1)S(1)}, bf16[128,512]{1,0:T(8,128)(2,1)S(1)}, u32[]{:S(2)}, u32[]{:S(2)}) collective-permute-start(bf16[128,512]{1,0:T(8,128)(2,1)S(1)} %convolution_convert_fusion.2), channel_id=1, source_target_pairs={{0,4},{4,0},{1,5},{5,1},{2,6},{6,2},{3,7},{7,3},{8,12},{12,8},{9,1... | collective-permute-start | bytes 393224 | tf_op jit(solution)/shard_map/ppermute | solution.py:29
  77.5 3.6 %copy-start.1 = (bf16[512,512]{1,0:T(8,128)(2,1)}, bf16[512,512]{1,0:T(8,128)(2,1)S(1)}, u32[]{:S(2)}) copy-start(bf16[512,512]{1,0:T(8,128)(2,1)S(1)} %all_gather.6.images) | copy-start | bytes 1572868
  90.4 14.2 %all-to-all-start.1 = ((f32[8,8,128]{2,1,0:T(8,128)}), f32[8,8,128]{2,1,0:T(8,128)S(1)}, u32[]{:S(2)}, u32[]{:S(2)}) async-start(f32[8,8,128]{2,1,0:T(8,128)} %broadcast_in_dim.25), calls=%async_computation.1 | async-start | bytes 65536 | tf_op jit(solution)/shard_map/all_to_all | solution.py:25
  110.6 15.8 %copy-start.3 = (f32[128,512]{1,0:T(8,128)S(1)}, f32[128,512]{1,0:T(8,128)}, u32[]{:S(2)}) copy-start(f32[128,512]{1,0:T(8,128)} %get-tuple-element.6) | copy-start | bytes 786436
  110.6 15.6 %all-to-all-start.2 = ((bf16[4,128,512]{2,1,0:T(8,128)(2,1)}), bf16[4,128,512]{2,1,0:T(8,128)(2,1)S(1)}, u32[]{:S(2)}, u32[]{:S(2)}) async-start(bf16[4,128,512]{2,1,0:T(8,128)(2,1)} %bitcast.32), calls=%async_computation.2 | async-start | bytes 1048576 | tf_op jit(solution)/shard_map/all_to_all | solution.py:136
  114.3 50.3 %reduce-scatter.2.cloned.1.call-start = ((), (), s32[]{:S(2)}) async-start(), calls=%async_computation.6 | async-start | bytes 1179648 | tf_op jit(solution)/shard_map/reduce_scatter | solution.py:135
  114.3 28.1 %collective-permute-start.2 = (bf16[768,512]{1,0:T(8,128)(2,1)S(1)}, bf16[768,512]{1,0:T(8,128)(2,1)}, u32[]{:S(2)}, u32[]{:S(2)}) collective-permute-start(bf16[768,512]{1,0:T(8,128)(2,1)S(1)} %bitcast.30), channel_id=1, source_target_pairs={{0,4},{4,0},{1,5},{5,1},{2,6},{6,2},{3,7},{7,3},{8,12},{12,8},{9,1... | collective-permute-start | bytes 2359304 | tf_op jit(solution)/shard_map/ppermute | solution.py:29
  126.7 7.3 %collective-permute-start.3 = (bf16[128,512]{1,0:T(8,128)(2,1)S(1)}, bf16[128,512]{1,0:T(8,128)(2,1)S(1)}, u32[]{:S(2)}, u32[]{:S(2)}) collective-permute-start(bf16[128,512]{1,0:T(8,128)(2,1)S(1)} %subtract_convert_fusion), channel_id=1, source_target_pairs={{0,4},{4,0},{1,5},{5,1},{2,6},{6,2},{3,7},{7,3},{8,12},{12,8},{9,1... | collective-permute-start | bytes 393224 | tf_op jit(solution)/shard_map/ppermute | solution.py:29
  135.2 32.1 %all-to-all-start.3 = ((bf16[16,48,512]{2,1,0:T(8,128)(2,1)}), bf16[16,48,512]{2,1,0:T(8,128)(2,1)S(1)}, u32[]{:S(2)}, u32[]{:S(2)}) async-start(bf16[16,48,512]{2,1,0:T(8,128)(2,1)} %bitcast.7), calls=%async_computation.4 | async-start | bytes 1572864 | tf_op jit(solution)/shard_map/all_to_all | solution.py:143
Sparse Core Ops, SparseCore 0:
  28.2 42.2 all-gather.1
  118.0 46.6 reduce-scatter.1

commit v6 on v5

--- a/solution.py
+++ b/solution.py
@@ -20,24 +20,93 @@
     )
 
 
-def to_all(array, axes, devices):
-    copies = jnp.broadcast_to(array[None], (devices, *array.shape))
-    return lax.all_to_all(copies, axes, 0, 0, tiled=True)
-
-
 def swapped(array):
     return lax.ppermute(array, PAIR, [(0, 1), (1, 0)])
 
 
-def coef_kernel(place, exps, row_inv, col_inv, images, texts, img_sent, img_own, txt_sent, coef, img_part):
+def copies_kernel(block, copies):
+    height = block.shape[0]
+    for k in range(copies.shape[0]):
+        copies[k, :height, :] = block[...]
+        copies[k, height:, :] = jnp.zeros((copies.shape[1] - height, block.shape[1]), block.dtype)
+
+
+def padded_copies(block, count, height):
+    vmem = pl.BlockSpec(memory_space=pltpu.VMEM)
+    return pl.pallas_call(
+        copies_kernel,
+        in_specs=[vmem],
+        out_specs=vmem,
+        out_shape=jax.ShapeDtypeStruct((count, height, block.shape[1]), block.dtype),
+        name="padded_copies",
+    )(block)
+
+
+def exps_kernel(scale, images, texts, exps, row_part, col_copies, col_part):
+    r = pl.program_id(0)
+    rows = images.shape[0]
+    product = lax.dot_general(
+        images[...], texts[...], (((1,), (1,)), ((), ())), preferred_element_type=jnp.float32
+    )
+    values = jnp.exp(scale[0] * product)
+    exps[...] = values
+
+    @pl.when(r == 0)
+    def _():
+        col_part[...] = jnp.zeros(col_part.shape, jnp.float32)
+
+    total = jnp.zeros((rows, rows), jnp.float32)
+    for c in range(NY):
+        tile = values[:, c * rows : (c + 1) * rows]
+        total = total + tile
+        col_part[c : c + 1, :] += jnp.sum(tile, axis=0, keepdims=True)
+    row_part[pl.ds(r, 1), :] = jnp.sum(total.T, axis=0, keepdims=True)
+
+    @pl.when(r == NZ - 1)
+    def _():
+        for k in range(NY):
+            col_copies[k] = col_part[...]
+
+
+def exps_and_sums(scale, images, texts):
+    rows, width = images.shape[0] // NZ, images.shape[1]
+    return pl.pallas_call(
+        exps_kernel,
+        grid=(NZ,),
+        in_specs=[
+            pl.BlockSpec(memory_space=pltpu.SMEM),
+            pl.BlockSpec((rows, width), lambda r: (r, 0)),
+            pl.BlockSpec(texts.shape, lambda r: (0, 0)),
+        ],
+        out_specs=[
+            pl.BlockSpec((rows, NY * rows), lambda r: (r, 0)),
+            pl.BlockSpec((NZ, rows), lambda r: (0, 0)),
+            pl.BlockSpec((NY, NY, rows), lambda r: (0, 0, 0)),
+        ],
+        out_shape=[
+            jax.ShapeDtypeStruct((NZ * rows, NY * rows), jnp.float32),
+            jax.ShapeDtypeStruct((NZ, rows), jnp.float32),
+            jax.ShapeDtypeStruct((NY, NY, rows), jnp.float32),
+        ],
+        scratch_shapes=[pltpu.VMEM((NY, rows), jnp.float32)],
+        name="exps",
+    )(scale, images, texts)
+
+
+def coef_kernel(place, exps, row_sum, col_parts, images, texts, img_sent, img_own, txt_sent, coef, img_part):
     a, b = place[0], place[1]
     rows = img_own.shape[0]
+    col_sum = col_parts[0]
+    for k in range(1, NY):
+        col_sum = col_sum + col_parts[k]
+    col_inv = 1.0 / col_sum
+    row_inv = 1.0 / row_sum[...]
     eye = lax.broadcasted_iota(jnp.int32, (rows, rows), 0) == lax.broadcasted_iota(
         jnp.int32, (rows, rows), 1
     )
     for r in range(NZ):
         at_row = slice(r * rows, (r + 1) * rows)
-        inverse = row_inv[at_row, :]
+        inverse = jnp.broadcast_to(row_inv[r : r + 1, :], (rows, rows)).T
         for c in range(NY):
             at = (at_row, slice(c * rows, (c + 1) * rows))
             label = jnp.where(eye, jnp.where((a == c) & (b == r), 2.0, 0.0), 0.0)
@@ -50,8 +119,8 @@
     ).astype(jnp.bfloat16)
 
 
-def coef_products(place, exps, row_inv, col_inv, images, texts):
-    rows = row_inv.shape[1]
+def coef_products(place, exps, row_sum, col_parts, images, texts):
+    rows = row_sum.shape[1]
     smem = pl.BlockSpec(memory_space=pltpu.SMEM)
     vmem = pl.BlockSpec(memory_space=pltpu.VMEM)
     width = images.shape[1]
@@ -69,7 +138,7 @@
             pltpu.VMEM(images.shape, jnp.float32),
         ],
         name="coef_products",
-    )(place, exps, row_inv, col_inv, images, texts)
+    )(place, exps, row_sum, col_parts, images, texts)
 
 
 def inv_norm(embedding):
@@ -100,7 +169,7 @@
     p, b = lax.axis_index(PAIR), lax.axis_index(Z)
     a = lax.axis_index(Y)
 
-    head = to_all(jnp.pad(image_head, ((0, padded - block), (0, 0))), SAME, NQ * NZ)
+    head = lax.all_to_all(padded_copies(image_head, NQ * NZ, padded), SAME, 0, 0, tiled=True)
     head = head.reshape(half, emb_width)
     choice = column_choice(width, padded, block, p)
     own_features = matmul(image_features, choice).astype(jnp.bfloat16)
@@ -120,17 +189,11 @@
     img_unit = (img_emb * img_inv).astype(jnp.bfloat16)
     images = lax.all_gather(img_unit, Z, axis=0, tiled=True)
 
-    exps = jnp.exp(scale * matmul(images, texts, 1, 1))
-    row_part = jnp.sum(exps, axis=1)
-    col_part = jnp.sum(exps, axis=0)
-
-    col_parts = to_all(col_part.reshape(NY, rows), Y, NY)
-    col_inv = 1.0 / jnp.sum(col_parts, axis=0)
+    exps, row_part, col_copies = exps_and_sums(logit_scale, images, texts)
+    col_parts = lax.all_to_all(col_copies, Y, 0, 0, tiled=True)
     row_sum = lax.psum(row_part, Z)
-    row_inv = jnp.broadcast_to((1.0 / row_sum)[:, None], (NZ * rows, rows))
-
     img_sent, img_own, txt_sent = coef_products(
-        jnp.stack([a, b]), exps, row_inv, col_inv, images, texts
+        jnp.stack([a, b]), exps, row_sum, col_parts, images, texts
     )
     txt_sum = lax.psum_scatter(txt_sent, Y, scatter_dimension=0, tiled=True)
     img_grads = lax.all_to_all(img_sent.reshape(NZ, rows, emb_width), Z, 0, 0, tiled=True)

time: 176 us -> 176 us (level)
  waiting for transfers between devices: 67.3 us -> 58.2 us
  Pallas kernels: 4.44 us -> 11.6 us
  starting transfers between devices: 42 us -> 48.4 us
  matrix products: 11.7 us -> 8.08 us
  local copies, waits for them, and re-layouts: 3.32 us -> 0.65 us
  blocking collectives: 25.2 us -> 27.8 us
    all_to_all x2, waiting for transfers between devices: 11.8 us -> 3.81 us  [the longest x1 3.8 us: local(): lax.all_to_all(padded_copies(image_head, NQ * NZ, padded), SAME, 0, 0, ti...]
    pallas_call x0 -> x2, Pallas kernels: none -> 6.92 us  [the longest x1 5.11 us: exps_and_sums(): pl.pallas_call(exps_kernel, grid=(NZ,), in_specs=[pl.BlockSpec(memory_spa...]
    all_to_all x1, starting transfers between devices: 6.83 us -> 11.8 us  [local(): lax.all_to_all(head_part.astype(jnp.bfloat16).reshape(NQ * NZ, padded, em...]
    dot_general x9 -> x8, matrix products: 11.7 us -> 8.08 us  [matmul(): lax.dot_general(left, right, (((left_dim,), (right_dim,)), ((), ())), pre...]
    ppermute x4, starting transfers between devices: 9.48 us -> 12.5 us  [swapped(): return lax.ppermute(array, PAIR, [(0, 1), (1, 0)])]
    broadcast_in_dim x3 -> x0, local copies, waits for them, and re-layouts: 2.41 us -> none  [the longest x2 1.57 us: to_all(): copies = jnp.broadcast_to(array[None], (devices, *array.shape))]
    psum x1, blocking collectives: 8.79 us -> 10.8 us  [local(): row_sum = lax.psum(row_part, Z)]
    all_to_all x1, waiting for transfers between devices: 9.36 us -> 7.37 us  [local(): lax.all_to_all(img_sent.reshape(NZ, rows, emb_width), Z, 0, 0, tiled=True)]
where the time goes in v6:
time: 176 us; the launch traced here: 175 us
  waiting for transfers between devices  58.2 us (33%)
  starting transfers between devices  48.4 us (28%)
  blocking collectives  27.8 us (16%)
  between operations  14.9 us (8%)
  Pallas kernels  11.6 us (7%)
  matrix products  8.08 us (5%)
  other arithmetic  5.53 us (3%)
    ppermute x4, waiting for transfers between devices, swapped(): return lax.ppermute(array, PAIR, [(0, 1), (1, 0)])  27.6 us
    reduce_scatter x1, waiting for transfers between devices, local(): txt_sum = lax.psum_scatter(txt_sent, Y, scatter_dimension=0, tiled=True)  19 us
    all_gather x1, blocking collectives, local(): images = lax.all_gather(img_unit, Z, axis=0, tiled=True)  17 us
    all_to_all x1, starting transfers between devices, local(): lax.all_to_all(padded_copies(image_head, NQ * NZ, padded), SAME, 0, 0, ti...  15.7 us
    ppermute x4, starting transfers between devices, swapped(): return lax.ppermute(array, PAIR, [(0, 1), (1, 0)])  12.5 us
    all_to_all x1, starting transfers between devices, local(): lax.all_to_all(head_part.astype(jnp.bfloat16).reshape(NQ * NZ, padded, em...  11.8 us
    psum x1, blocking collectives, local(): row_sum = lax.psum(row_part, Z)  10.8 us
    dot_general x8, matrix products, matmul(): lax.dot_general(left, right, (((left_dim,), (right_dim,)), ((), ())), pre...  8.08 us
  transfers between devices with their start and end apart: 10, of which 7 were waited for; matrix products, arithmetic and copies ran while one was open for 7% of the time, Pallas kernels for 0%

profile of v6, /device:TPU:6, one launch (start us, length us, event | category | flops | bytes accessed | tf_op | source)
XLA Modules:
  0.0 175.1 jit_solution(3885842363051312343)
XLA Ops:
  7.2 0.0 copy-start
  7.2 0.0 copy-start.1
  7.2 1.8 %padded_copies.1 = bf16[16,48,512]{2,1,0:T(8,128)(2,1)} custom-call(bf16[44,512]{1,0:T(8,128)(2,1)} %block.1), custom_call_target="tpu_custom_call" | custom-call | tf_op jit(solution)/shard_map/padded_copies/pallas_call | solution.py:36
  9.0 15.7 %all-to-all-start = ((bf16[16,48,512]{2,1,0:T(8,128)(2,1)}), bf16[16,48,512]{2,1,0:T(8,128)(2,1)S(1)}, u32[]{:S(2)}, u32[]{:S(2)}) async-start(bf16[16,48,512]{2,1,0:T(8,128)(2,1)} %padded_copies.1), calls=%async_computation | async-start | bytes 1572864 | tf_op jit(solution)/shard_map/all_to_all | solution.py:172
  24.7 0.0 all-gather.2.cloned.1.call-start
  24.7 0.0 copy-done.1
  24.7 0.1 fusion.16
  24.9 0.8 fusion.17
  25.6 0.0 all-gather.2.cloned.1.call-update
  25.7 0.0 copy-done
  25.7 1.3 fusion.10
  27.1 2.6 %collective-permute-start = (bf16[128,768]{0,1:T(8,128)(2,1)S(1)}, bf16[128,768]{0,1:T(8,128)(2,1)S(1)}, u32[]{:S(2)}, u32[]{:S(2)}) collective-permute-start(bf16[128,768]{0,1:T(8,128)(2,1)S(1)} %slice.13), channel_id=1, source_target_pairs={{0,4},{4,0},{1,5},{5,1},{2,6},{6,2},{3,7},{7,3},{8,12},{12,8},{9,1... | collective-permute-start | bytes 589832 | tf_op jit(solution)/shard_map/ppermute | solution.py:24
  29.7 18.9 %collective-permute-done = bf16[128,768]{0,1:T(8,128)(2,1)S(1)} collective-permute-done((bf16[128,768]{0,1:T(8,128)(2,1)S(1)}, bf16[128,768]{0,1:T(8,128)(2,1)S(1)}, u32[]{:S(2)}, u32[]{:S(2)}) %collective-permute-start) | collective-permute-done | bytes 196640 | tf_op jit(solution)/shard_map/ppermute | solution.py:24
  48.6 3.8 %all-to-all-done = bf16[16,48,512]{2,1,0:T(8,128)(2,1)S(1)} async-done(((bf16[16,48,512]{2,1,0:T(8,128)(2,1)}), bf16[16,48,512]{2,1,0:T(8,128)(2,1)S(1)}, u32[]{:S(2)}, u32[]{:S(2)}) %all-to-all-start) | async-done | bytes 786464 | tf_op jit(solution)/shard_map/all_to_all | solution.py:172
  52.4 0.3 convolution_convert_fusion.2
  52.7 1.9 %collective-permute-start.1 = (bf16[128,512]{1,0:T(8,128)(2,1)S(1)}, bf16[128,512]{1,0:T(8,128)(2,1)S(1)}, u32[]{:S(2)}, u32[]{:S(2)}) collective-permute-start(bf16[128,512]{1,0:T(8,128)(2,1)S(1)} %convolution_convert_fusion.2), channel_id=1, source_target_pairs={{0,4},{4,0},{1,5},{5,1},{2,6},{6,2},{3,7},{7,3},{8,12},{12,8},{9,1... | collective-permute-start | bytes 393224 | tf_op jit(solution)/shard_map/ppermute | solution.py:24
  55.3 5.3 %collective-permute-done.1 = bf16[128,512]{1,0:T(8,128)(2,1)S(1)} collective-permute-done((bf16[128,512]{1,0:T(8,128)(2,1)S(1)}, bf16[128,512]{1,0:T(8,128)(2,1)S(1)}, u32[]{:S(2)}, u32[]{:S(2)}) %collective-permute-start.1) | collective-permute-done | bytes 131104 | tf_op jit(solution)/shard_map/ppermute | solution.py:24
  60.6 0.4 multiply_reduce_fusion.1
  61.0 0.1 multiply_convert_fusion
  61.1 17.0 %all_gather.6.images = bf16[512,512]{1,0:T(8,128)(2,1)} all-gather(bf16[128,512]{1,0:T(8,128)(2,1)S(1)} %multiply_convert_fusion), channel_id=1, replica_groups=mesh['rep'=16,'dp_q'=4,'dp_pair'=2,'dp_z'=4] {'dp_z'}, dimensions={0}, use_global_device_ids=true | all-gather | bytes 655360 | tf_op jit(solution)/shard_map/all_gather | solution.py:190
  78.1 0.0 all-gather.2.cloned.1.call-done.texts
  78.1 5.1 %exps.1 = (f32[512,1024]{1,0:T(8,128)}, f32[4,128]{1,0:T(4,128)}, f32[8,8,128]{2,1,0:T(8,128)}) custom-call(f32[1]{0:T(128)} %copy.7.scale, bf16[512,512]{1,0:T(8,128)(2,1)} %all_gather.6.images, bf16[1024,512]{1,0:T(8,128)(2,1)} %all-gather.2.cloned.1.call-done.texts), custom_call_target="tpu_custom_call" | custom-call | tf_op jit(solution)/shard_map/exps/pallas_call | solution.py:73
  83.2 4.6 %all-to-all-start.1 = ((f32[8,8,128]{2,1,0:T(8,128)}), f32[8,8,128]{2,1,0:T(8,128)S(1)}, u32[]{:S(2)}, u32[]{:S(2)}) async-start(f32[8,8,128]{2,1,0:T(8,128)} %get-tuple-element.11), calls=%async_computation.1 | async-start | bytes 65536 | tf_op jit(solution)/shard_map/all_to_all | solution.py:193
  87.8 0.6 pad_add_fusion.place
  88.4 10.8 %psum.7.row_sum = f32[4,128]{1,0:T(4,128)} all-reduce(f32[4,128]{1,0:T(4,128)} %get-tuple-element.10), channel_id=1, replica_groups=mesh['rep'=16,'dp_q'=4,'dp_pair'=2,'dp_z'=4] {'dp_z'}, use_global_device_ids=true, to_apply=%region_2.3 | all-reduce | flops 512 | bytes 4096 | tf_op jit(solution)/shard_map/psum | solution.py:194
  99.2 0.0 all-to-all-done.1.col_parts
  99.2 0.0 copy-start.3
  99.2 0.6 copy-done.3
  99.8 4.6 %coef_products.1 = (bf16[512,512]{1,0:T(8,128)(2,1)}, f32[128,512]{1,0:T(8,128)}, bf16[1024,512]{1,0:T(8,128)(2,1)}) custom-call(s32[2]{0:T(128)} %pad_add_fusion.place, f32[512,1024]{1,0:T(8,128)} %get-tuple-element.9.exps, f32[4,128]{1,0:T(4,128)} %psum.7.row_sum, f32[8,8,128]{2,1,0:T(8,128)} %copy-done.3, bf16[512,512]{1,0:T(8,128)(2,1)} %all_gather.6.images, ...), custom_call_target="tpu_custom_call" | custom-call | tf_op jit(solution)/shard_map/coef_products/pallas_call | solution.py:127
  104.5 0.0 copy-start.2
  104.5 3.8 %all-to-all-start.2 = ((bf16[4,128,512]{2,1,0:T(8,128)(2,1)}), bf16[4,128,512]{2,1,0:T(8,128)(2,1)S(1)}, u32[]{:S(2)}, u32[]{:S(2)}) async-start(bf16[4,128,512]{2,1,0:T(8,128)(2,1)} %bitcast.28), calls=%async_computation.2 | async-start | bytes 1048576 | tf_op jit(solution)/shard_map/all_to_all | solution.py:199
  108.2 0.0 reduce-scatter.2.cloned.1.call-start
  108.2 3.9 %collective-permute-start.2 = (bf16[768,512]{1,0:T(8,128)(2,1)S(1)}, bf16[768,512]{1,0:T(8,128)(2,1)}, u32[]{:S(2)}, u32[]{:S(2)}) collective-permute-start(bf16[768,512]{1,0:T(8,128)(2,1)S(1)} %bitcast.26), channel_id=1, source_target_pairs={{0,4},{4,0},{1,5},{5,1},{2,6},{6,2},{3,7},{7,3},{8,12},{12,8},{9,1... | collective-permute-start | bytes 2359304 | tf_op jit(solution)/shard_map/ppermute | solution.py:24
  112.2 0.0 reduce-scatter.2.cloned.1.call-update
  112.2 7.4 %all-to-all-done.2 = bf16[4,128,512]{2,1,0:T(8,128)(2,1)S(1)} async-done(((bf16[4,128,512]{2,1,0:T(8,128)(2,1)}), bf16[4,128,512]{2,1,0:T(8,128)(2,1)S(1)}, u32[]{:S(2)}, u32[]{:S(2)}) %all-to-all-start.2) | async-done | bytes 524320 | tf_op jit(solution)/shard_map/all_to_all | solution.py:199
  119.6 0.2 select_reduce_fusion
  119.8 0.0 copy-done.2
  119.8 0.1 multiply_reduce_fusion
  119.9 0.1 subtract_convert_fusion
  120.1 4.0 %collective-permute-start.3 = (bf16[128,512]{1,0:T(8,128)(2,1)S(1)}, bf16[128,512]{1,0:T(8,128)(2,1)S(1)}, u32[]{:S(2)}, u32[]{:S(2)}) collective-permute-start(bf16[128,512]{1,0:T(8,128)(2,1)S(1)} %subtract_convert_fusion), channel_id=1, source_target_pairs={{0,4},{4,0},{1,5},{5,1},{2,6},{6,2},{3,7},{7,3},{8,12},{12,8},{9,1... | collective-permute-start | bytes 393224 | tf_op jit(solution)/shard_map/ppermute | solution.py:24
  124.1 0.3 fusion.22
  124.4 3.4 %collective-permute-done.3 = bf16[128,512]{1,0:T(8,128)(2,1)S(1)} collective-permute-done((bf16[128,512]{1,0:T(8,128)(2,1)S(1)}, bf16[128,512]{1,0:T(8,128)(2,1)S(1)}, u32[]{:S(2)}, u32[]{:S(2)}) %collective-permute-start.3) | collective-permute-done | bytes 131104 | tf_op jit(solution)/shard_map/ppermute | solution.py:24
  127.8 1.2 add_convert_fusion
  129.1 11.8 %all-to-all-start.3 = ((bf16[16,48,512]{2,1,0:T(8,128)(2,1)}), bf16[16,48,512]{2,1,0:T(8,128)(2,1)S(1)}, u32[]{:S(2)}, u32[]{:S(2)}) async-start(bf16[16,48,512]{2,1,0:T(8,128)(2,1)} %bitcast.6), calls=%async_computation.4 | async-start | bytes 1572864 | tf_op jit(solution)/shard_map/all_to_all | solution.py:206
  140.9 0.4 convolution_convert_fusion.1
  141.3 0.0 collective-permute-done.2
  141.3 1.5 convolution_convert_fusion
  142.8 2.6 %fusion.9 = bf16[128,1408]{1,0:T(8,128)(2,1)} fusion(s32[1536]{0:T(1024)S(1)} %fusion.33, bf16[128,768]{1,0:T(8,128)(2,1)S(1)} %convolution_convert_fusion, bf16[128,768]{1,0:T(8,128)(2,1)S(1)} %convolution_convert_fusion.1), kind=kOutput, calls=%fused_computation.7 | convolution fusion | flops 556777472 | bytes 759808 | tf_op jit(solution)/shard_map/dot_general | solution.py:18
  145.4 19.0 %reduce-scatter.2.cloned.1.call-done = bf16[128,512]{1,0:T(8,128)(2,1)} async-done(((bf16[1024,512]{1,0:T(8,128)(2,1)}), bf16[128,512]{1,0:T(8,128)(2,1)}) %reduce-scatter.2.cloned.1.call-update) | async-done | bytes 131088 | tf_op jit(solution)/shard_map/reduce_scatter | solution.py:198
  164.4 1.0 fusion.21
  165.4 1.7 fusion.20
  167.1 0.4 all-to-all-done.3
  167.5 0.8 convert_reduce_fusion
  (5 shorter events, 0.1 us)
Async XLA Ops:
  7.2 18.5 %copy-start = (bf16[128,1408]{1,0:T(8,128)(2,1)S(1)}, bf16[128,1408]{1,0:T(8,128)(2,1)}, u32[]{:S(2)}) copy-start(bf16[128,1408]{1,0:T(8,128)(2,1)} %param.4) | copy-start | bytes 1081348
  7.2 17.6 %copy-start.1 = (bf16[128,512]{1,0:T(8,128)(2,1)S(1)}, bf16[128,512]{1,0:T(8,128)(2,1)}, u32[]{:S(2)}) copy-start(bf16[128,512]{1,0:T(8,128)(2,1)} %param.5) | copy-start | bytes 393220
  9.0 43.4 %all-to-all-start = ((bf16[16,48,512]{2,1,0:T(8,128)(2,1)}), bf16[16,48,512]{2,1,0:T(8,128)(2,1)S(1)}, u32[]{:S(2)}, u32[]{:S(2)}) async-start(bf16[16,48,512]{2,1,0:T(8,128)(2,1)} %padded_copies.1), calls=%async_computation | async-start | bytes 1572864 | tf_op jit(solution)/shard_map/all_to_all | solution.py:172
  24.7 53.4 %all-gather.2.cloned.1.call-start = ((), (), s32[]{:S(2)}) async-start(), calls=%async_computation.5 | async-start | bytes 1179648 | tf_op jit(solution)/shard_map/all_gather | solution.py:183
  27.1 21.5 %collective-permute-start = (bf16[128,768]{0,1:T(8,128)(2,1)S(1)}, bf16[128,768]{0,1:T(8,128)(2,1)S(1)}, u32[]{:S(2)}, u32[]{:S(2)}) collective-permute-start(bf16[128,768]{0,1:T(8,128)(2,1)S(1)} %slice.13), channel_id=1, source_target_pairs={{0,4},{4,0},{1,5},{5,1},{2,6},{6,2},{3,7},{7,3},{8,12},{12,8},{9,1... | collective-permute-start | bytes 589832 | tf_op jit(solution)/shard_map/ppermute | solution.py:24
  52.7 7.9 %collective-permute-start.1 = (bf16[128,512]{1,0:T(8,128)(2,1)S(1)}, bf16[128,512]{1,0:T(8,128)(2,1)S(1)}, u32[]{:S(2)}, u32[]{:S(2)}) collective-permute-start(bf16[128,512]{1,0:T(8,128)(2,1)S(1)} %convolution_convert_fusion.2), channel_id=1, source_target_pairs={{0,4},{4,0},{1,5},{5,1},{2,6},{6,2},{3,7},{7,3},{8,12},{12,8},{9,1... | collective-permute-start | bytes 393224 | tf_op jit(solution)/shard_map/ppermute | solution.py:24
  83.2 16.0 %all-to-all-start.1 = ((f32[8,8,128]{2,1,0:T(8,128)}), f32[8,8,128]{2,1,0:T(8,128)S(1)}, u32[]{:S(2)}, u32[]{:S(2)}) async-start(f32[8,8,128]{2,1,0:T(8,128)} %get-tuple-element.11), calls=%async_computation.1 | async-start | bytes 65536 | tf_op jit(solution)/shard_map/all_to_all | solution.py:193
  99.2 0.6 copy-start.3
  104.5 15.3 %copy-start.2 = (f32[128,512]{1,0:T(8,128)S(1)}, f32[128,512]{1,0:T(8,128)}, u32[]{:S(2)}) copy-start(f32[128,512]{1,0:T(8,128)} %get-tuple-element.12) | copy-start | bytes 786436
  104.5 15.1 %all-to-all-start.2 = ((bf16[4,128,512]{2,1,0:T(8,128)(2,1)}), bf16[4,128,512]{2,1,0:T(8,128)(2,1)S(1)}, u32[]{:S(2)}, u32[]{:S(2)}) async-start(bf16[4,128,512]{2,1,0:T(8,128)(2,1)} %bitcast.28), calls=%async_computation.2 | async-start | bytes 1048576 | tf_op jit(solution)/shard_map/all_to_all | solution.py:199
  108.2 56.1 %reduce-scatter.2.cloned.1.call-start = ((), (), s32[]{:S(2)}) async-start(), calls=%async_computation.6 | async-start | bytes 1179648 | tf_op jit(solution)/shard_map/reduce_scatter | solution.py:198
  108.2 33.0 %collective-permute-start.2 = (bf16[768,512]{1,0:T(8,128)(2,1)S(1)}, bf16[768,512]{1,0:T(8,128)(2,1)}, u32[]{:S(2)}, u32[]{:S(2)}) collective-permute-start(bf16[768,512]{1,0:T(8,128)(2,1)S(1)} %bitcast.26), channel_id=1, source_target_pairs={{0,4},{4,0},{1,5},{5,1},{2,6},{6,2},{3,7},{7,3},{8,12},{12,8},{9,1... | collective-permute-start | bytes 2359304 | tf_op jit(solution)/shard_map/ppermute | solution.py:24
  120.1 7.8 %collective-permute-start.3 = (bf16[128,512]{1,0:T(8,128)(2,1)S(1)}, bf16[128,512]{1,0:T(8,128)(2,1)S(1)}, u32[]{:S(2)}, u32[]{:S(2)}) collective-permute-start(bf16[128,512]{1,0:T(8,128)(2,1)S(1)} %subtract_convert_fusion), channel_id=1, source_target_pairs={{0,4},{4,0},{1,5},{5,1},{2,6},{6,2},{3,7},{7,3},{8,12},{12,8},{9,1... | collective-permute-start | bytes 393224 | tf_op jit(solution)/shard_map/ppermute | solution.py:24
  129.1 38.4 %all-to-all-start.3 = ((bf16[16,48,512]{2,1,0:T(8,128)(2,1)}), bf16[16,48,512]{2,1,0:T(8,128)(2,1)S(1)}, u32[]{:S(2)}, u32[]{:S(2)}) async-start(bf16[16,48,512]{2,1,0:T(8,128)(2,1)} %bitcast.6), calls=%async_computation.4 | async-start | bytes 1572864 | tf_op jit(solution)/shard_map/all_to_all | solution.py:206
Sparse Core Ops, SparseCore 0:
  28.1 42.2 all-gather.1
  112.3 51.9 reduce-scatter.1

commit v7 on v5

--- a/solution.py
+++ b/solution.py
@@ -29,15 +29,22 @@
     return lax.ppermute(array, PAIR, [(0, 1), (1, 0)])
 
 
-def coef_kernel(place, exps, row_inv, col_inv, images, texts, img_sent, img_own, txt_sent, coef, img_part):
-    a, b = place[0], place[1]
+def coef_kernel(
+    at_y, at_z, exps, row_sum, col_parts, images, texts, img_sent, img_own, txt_sent, coef, img_part
+):
+    a, b = at_y[0], at_z[0]
     rows = img_own.shape[0]
+    col_sum = col_parts[0]
+    for k in range(1, NY):
+        col_sum = col_sum + col_parts[k]
+    col_inv = 1.0 / col_sum
+    row_inv = 1.0 / row_sum[...]
     eye = lax.broadcasted_iota(jnp.int32, (rows, rows), 0) == lax.broadcasted_iota(
         jnp.int32, (rows, rows), 1
     )
     for r in range(NZ):
         at_row = slice(r * rows, (r + 1) * rows)
-        inverse = row_inv[at_row, :]
+        inverse = jnp.broadcast_to(row_inv[r : r + 1, :], (rows, rows)).T
         for c in range(NY):
             at = (at_row, slice(c * rows, (c + 1) * rows))
             label = jnp.where(eye, jnp.where((a == c) & (b == r), 2.0, 0.0), 0.0)
@@ -50,14 +57,14 @@
     ).astype(jnp.bfloat16)
 
 
-def coef_products(place, exps, row_inv, col_inv, images, texts):
-    rows = row_inv.shape[1]
+def coef_products(at_y, at_z, exps, row_sum, col_parts, images, texts):
+    rows = row_sum.shape[1]
     smem = pl.BlockSpec(memory_space=pltpu.SMEM)
     vmem = pl.BlockSpec(memory_space=pltpu.VMEM)
     width = images.shape[1]
     return pl.pallas_call(
         coef_kernel,
-        in_specs=[smem] + [vmem] * 5,
+        in_specs=[smem] * 2 + [vmem] * 5,
         out_specs=[vmem] * 3,
         out_shape=[
             jax.ShapeDtypeStruct(images.shape, jnp.bfloat16),
@@ -69,7 +76,7 @@
             pltpu.VMEM(images.shape, jnp.float32),
         ],
         name="coef_products",
-    )(place, exps, row_inv, col_inv, images, texts)
+    )(at_y.reshape(1), at_z.reshape(1), exps, row_sum, col_parts, images, texts)
 
 
 def inv_norm(embedding):
@@ -125,12 +132,10 @@
     col_part = jnp.sum(exps, axis=0)
 
     col_parts = to_all(col_part.reshape(NY, rows), Y, NY)
-    col_inv = 1.0 / jnp.sum(col_parts, axis=0)
-    row_sum = lax.psum(row_part, Z)
-    row_inv = jnp.broadcast_to((1.0 / row_sum)[:, None], (NZ * rows, rows))
-
+    row_sum = lax.optimization_barrier(lax.psum(row_part, Z))
+    row_sum = row_sum.reshape(NZ, rows)
     img_sent, img_own, txt_sent = coef_products(
-        jnp.stack([a, b]), exps, row_inv, col_inv, images, texts
+        a, b, exps, row_sum, col_parts, images, texts
     )
     txt_sum = lax.psum_scatter(txt_sent, Y, scatter_dimension=0, tiled=True)
     img_grads = lax.all_to_all(img_sent.reshape(NZ, rows, emb_width), Z, 0, 0, tiled=True)

time: 176 us -> 173 us (0.983)
  waiting for transfers between devices: 67.3 us -> 57.5 us
  starting transfers between devices: 42 us -> 48.3 us
  blocking collectives: 25.2 us -> 27.4 us
    all_to_all x2, waiting for transfers between devices: 11.8 us -> 3.81 us  [to_all(): return lax.all_to_all(copies, axes, 0, 0, tiled=True)]
    all_to_all x1, starting transfers between devices: 6.83 us -> 11.9 us  [local(): lax.all_to_all(head_part.astype(jnp.bfloat16).reshape(NQ * NZ, padded, em...]
    ppermute x4, starting transfers between devices: 9.48 us -> 12.4 us  [swapped(): return lax.ppermute(array, PAIR, [(0, 1), (1, 0)])]
    psum x1, blocking collectives: 8.79 us -> 11.1 us  [local(): row_sum = lax.optimization_barrier(lax.psum(row_part, Z))]
    all_to_all x1, waiting for transfers between devices: 9.36 us -> 7.4 us  [local(): lax.all_to_all(img_sent.reshape(NZ, rows, emb_width), Z, 0, 0, tiled=True)]
where the time goes in v7:
time: 173 us; the launch traced here: 172 us
  waiting for transfers between devices  57.5 us (33%)
  starting transfers between devices  48.3 us (28%)
  blocking collectives  27.4 us (16%)
  between operations  14.9 us (9%)
  matrix products  11.6 us (7%)
  other arithmetic  4.94 us (3%)
  Pallas kernels  4.62 us (3%)
  local copies, waits for them, and re-layouts  3.1 us (2%)
    ppermute x4, waiting for transfers between devices, swapped(): return lax.ppermute(array, PAIR, [(0, 1), (1, 0)])  27.5 us
    all_to_all x2, starting transfers between devices, to_all(): return lax.all_to_all(copies, axes, 0, 0, tiled=True)  20.2 us
    reduce_scatter x1, waiting for transfers between devices, local(): txt_sum = lax.psum_scatter(txt_sent, Y, scatter_dimension=0, tiled=True)  18.4 us
    all_gather x1, blocking collectives, local(): images = lax.all_gather(img_unit, Z, axis=0, tiled=True)  16.4 us
    ppermute x4, starting transfers between devices, swapped(): return lax.ppermute(array, PAIR, [(0, 1), (1, 0)])  12.4 us
    all_to_all x1, starting transfers between devices, local(): lax.all_to_all(head_part.astype(jnp.bfloat16).reshape(NQ * NZ, padded, em...  11.9 us
    dot_general x9, matrix products, matmul(): lax.dot_general(left, right, (((left_dim,), (right_dim,)), ((), ())), pre...  11.6 us
    psum x1, blocking collectives, local(): row_sum = lax.optimization_barrier(lax.psum(row_part, Z))  11.1 us
  transfers between devices with their start and end apart: 10, of which 7 were waited for; matrix products, arithmetic and copies ran while one was open for 7% of the time, Pallas kernels for 0%

profile of v7, /device:TPU:6, one launch (start us, length us, event | category | flops | bytes accessed | tf_op | source)
XLA Modules:
  0.0 172.4 jit_solution(10184618388497039643)
XLA Ops:
  7.2 0.0 copy-start
  7.2 0.0 copy-start.1
  7.2 0.9 pad.4
  8.1 1.0 broadcast_in_dim.20
  9.0 15.7 %all-to-all-start = ((bf16[16,48,512]{2,1,0:T(8,128)(2,1)}), bf16[16,48,512]{2,1,0:T(8,128)(2,1)S(1)}, u32[]{:S(2)}, u32[]{:S(2)}) async-start(bf16[16,48,512]{2,1,0:T(8,128)(2,1)} %broadcast_in_dim.20), calls=%async_computation | async-start | bytes 1572864 | tf_op jit(solution)/shard_map/all_to_all | solution.py:25
  24.7 0.0 all-gather.2.cloned.1.call-start
  24.8 0.0 copy-done.1
  24.8 0.1 fusion.16
  24.9 0.8 fusion.17
  25.6 0.0 all-gather.2.cloned.1.call-update
  25.7 0.0 copy-done
  25.7 1.4 fusion.10
  27.1 2.6 %collective-permute-start = (bf16[128,768]{0,1:T(8,128)(2,1)S(1)}, bf16[128,768]{0,1:T(8,128)(2,1)S(1)}, u32[]{:S(2)}, u32[]{:S(2)}) collective-permute-start(bf16[128,768]{0,1:T(8,128)(2,1)S(1)} %slice.13), channel_id=1, source_target_pairs={{0,4},{4,0},{1,5},{5,1},{2,6},{6,2},{3,7},{7,3},{8,12},{12,8},{9,1... | collective-permute-start | bytes 589832 | tf_op jit(solution)/shard_map/ppermute | solution.py:29
  29.7 18.9 %collective-permute-done = bf16[128,768]{0,1:T(8,128)(2,1)S(1)} collective-permute-done((bf16[128,768]{0,1:T(8,128)(2,1)S(1)}, bf16[128,768]{0,1:T(8,128)(2,1)S(1)}, u32[]{:S(2)}, u32[]{:S(2)}) %collective-permute-start) | collective-permute-done | bytes 196640 | tf_op jit(solution)/shard_map/ppermute | solution.py:29
  48.6 3.8 %all-to-all-done = bf16[16,48,512]{2,1,0:T(8,128)(2,1)S(1)} async-done(((bf16[16,48,512]{2,1,0:T(8,128)(2,1)}), bf16[16,48,512]{2,1,0:T(8,128)(2,1)S(1)}, u32[]{:S(2)}, u32[]{:S(2)}) %all-to-all-start) | async-done | bytes 786464 | tf_op jit(solution)/shard_map/all_to_all | solution.py:25
  52.4 0.3 convolution_convert_fusion.2
  52.7 1.9 %collective-permute-start.1 = (bf16[128,512]{1,0:T(8,128)(2,1)S(1)}, bf16[128,512]{1,0:T(8,128)(2,1)S(1)}, u32[]{:S(2)}, u32[]{:S(2)}) collective-permute-start(bf16[128,512]{1,0:T(8,128)(2,1)S(1)} %convolution_convert_fusion.2), channel_id=1, source_target_pairs={{0,4},{4,0},{1,5},{5,1},{2,6},{6,2},{3,7},{7,3},{8,12},{12,8},{9,1... | collective-permute-start | bytes 393224 | tf_op jit(solution)/shard_map/ppermute | solution.py:29
  55.3 5.3 %collective-permute-done.1 = bf16[128,512]{1,0:T(8,128)(2,1)S(1)} collective-permute-done((bf16[128,512]{1,0:T(8,128)(2,1)S(1)}, bf16[128,512]{1,0:T(8,128)(2,1)S(1)}, u32[]{:S(2)}, u32[]{:S(2)}) %collective-permute-start.1) | collective-permute-done | bytes 131104 | tf_op jit(solution)/shard_map/ppermute | solution.py:29
  60.6 0.4 multiply_reduce_fusion.1
  61.0 0.1 multiply_convert_fusion
  61.1 16.4 %all_gather.6.images = bf16[512,512]{1,0:T(8,128)(2,1)S(1)} all-gather(bf16[128,512]{1,0:T(8,128)(2,1)S(1)} %multiply_convert_fusion), channel_id=1, replica_groups=mesh['rep'=16,'dp_q'=4,'dp_pair'=2,'dp_z'=4] {'dp_z'}, dimensions={0}, use_global_device_ids=true | all-gather | bytes 655360 | tf_op jit(solution)/shard_map/all_gather | solution.py:128
  77.5 0.0 copy-start.2
  77.5 0.0 all-gather.2.cloned.1.call-done.texts
  77.5 3.6 %fusion.50 = (f32[1024]{0:T(1024)S(1)}, f32[512]{0:T(512)S(1)}, f32[512,1024]{1,0:T(8,128)}) fusion(bf16[512,512]{1,0:T(8,128)(2,1)S(1)} %all_gather.6.images, bf16[1024,512]{1,0:T(8,128)(2,1)} %all-gather.2.cloned.1.call-done.texts, f32[]{:T(128)} %bitcast.25), kind=kOutput, calls=%fused_computation.88 | convolution fusion | flops 538442240 | bytes 3676164 | tf_op jit(solution)/shard_map/dot_general | solution.py:18
  81.0 0.0 copy-done.2
  81.0 0.6 broadcast_in_dim.34
  81.7 4.5 %all-to-all-start.1 = ((f32[8,8,128]{2,1,0:T(8,128)}), f32[8,8,128]{2,1,0:T(8,128)S(1)}, u32[]{:S(2)}, u32[]{:S(2)}) async-start(f32[8,8,128]{2,1,0:T(8,128)} %broadcast_in_dim.34), calls=%async_computation.1 | async-start | bytes 65536 | tf_op jit(solution)/shard_map/all_to_all | solution.py:25
  86.2 11.1 %psum.7 = f32[512]{0:T(512)} all-reduce(f32[512]{0:T(512)S(1)} %get-tuple-element.10), channel_id=1, replica_groups=mesh['rep'=16,'dp_q'=4,'dp_pair'=2,'dp_z'=4] {'dp_z'}, use_global_device_ids=true, to_apply=%region_3.4 | all-reduce | flops 512 | bytes 4096 | tf_op jit(solution)/shard_map/psum | solution.py:135
  97.3 0.0 all-to-all-done.1.col_parts
  97.3 0.0 copy-start.4
  97.3 0.6 copy-done.4
  97.9 4.6 %coef_products.1 = (bf16[512,512]{1,0:T(8,128)(2,1)}, f32[128,512]{1,0:T(8,128)}, bf16[1024,512]{1,0:T(8,128)(2,1)}) custom-call(s32[1]{0:T(128)} %bitcast.3.at_y, s32[1]{0:T(128)} %bitcast.4.at_z, f32[512,1024]{1,0:T(8,128)} %get-tuple-element.17.exps, f32[4,128]{1,0:T(4,128)} %bitcast.35, f32[8,8,128]{2,1,0:T(8,128)} %copy-done.4, ...), custom_call_target="tpu_custom_call" | custom-call | tf_op jit(solution)/shard_map/coef_products/pallas_call | solution.py:65
  102.5 0.0 copy-start.3
  102.5 3.8 %all-to-all-start.2 = ((bf16[4,128,512]{2,1,0:T(8,128)(2,1)}), bf16[4,128,512]{2,1,0:T(8,128)(2,1)S(1)}, u32[]{:S(2)}, u32[]{:S(2)}) async-start(bf16[4,128,512]{2,1,0:T(8,128)(2,1)} %bitcast.33), calls=%async_computation.2 | async-start | bytes 1048576 | tf_op jit(solution)/shard_map/all_to_all | solution.py:141
  106.3 0.0 reduce-scatter.2.cloned.1.call-start
  106.3 3.9 %collective-permute-start.2 = (bf16[768,512]{1,0:T(8,128)(2,1)S(1)}, bf16[768,512]{1,0:T(8,128)(2,1)}, u32[]{:S(2)}, u32[]{:S(2)}) collective-permute-start(bf16[768,512]{1,0:T(8,128)(2,1)S(1)} %bitcast.31), channel_id=1, source_target_pairs={{0,4},{4,0},{1,5},{5,1},{2,6},{6,2},{3,7},{7,3},{8,12},{12,8},{9,1... | collective-permute-start | bytes 2359304 | tf_op jit(solution)/shard_map/ppermute | solution.py:29
  110.2 0.0 reduce-scatter.2.cloned.1.call-update
  110.2 7.4 %all-to-all-done.2 = bf16[4,128,512]{2,1,0:T(8,128)(2,1)S(1)} async-done(((bf16[4,128,512]{2,1,0:T(8,128)(2,1)}), bf16[4,128,512]{2,1,0:T(8,128)(2,1)S(1)}, u32[]{:S(2)}, u32[]{:S(2)}) %all-to-all-start.2) | async-done | bytes 524320 | tf_op jit(solution)/shard_map/all_to_all | solution.py:141
  117.6 0.2 select_reduce_fusion
  117.8 0.0 copy-done.3
  117.8 0.1 multiply_reduce_fusion
  117.9 0.1 subtract_convert_fusion
  118.1 4.0 %collective-permute-start.3 = (bf16[128,512]{1,0:T(8,128)(2,1)S(1)}, bf16[128,512]{1,0:T(8,128)(2,1)S(1)}, u32[]{:S(2)}, u32[]{:S(2)}) collective-permute-start(bf16[128,512]{1,0:T(8,128)(2,1)S(1)} %subtract_convert_fusion), channel_id=1, source_target_pairs={{0,4},{4,0},{1,5},{5,1},{2,6},{6,2},{3,7},{7,3},{8,12},{12,8},{9,1... | collective-permute-start | bytes 393224 | tf_op jit(solution)/shard_map/ppermute | solution.py:29
  122.1 0.3 fusion.22
  122.4 3.3 %collective-permute-done.3 = bf16[128,512]{1,0:T(8,128)(2,1)S(1)} collective-permute-done((bf16[128,512]{1,0:T(8,128)(2,1)S(1)}, bf16[128,512]{1,0:T(8,128)(2,1)S(1)}, u32[]{:S(2)}, u32[]{:S(2)}) %collective-permute-start.3) | collective-permute-done | bytes 131104 | tf_op jit(solution)/shard_map/ppermute | solution.py:29
  125.7 1.2 add_convert_fusion
  126.9 11.9 %all-to-all-start.3 = ((bf16[16,48,512]{2,1,0:T(8,128)(2,1)}), bf16[16,48,512]{2,1,0:T(8,128)(2,1)S(1)}, u32[]{:S(2)}, u32[]{:S(2)}) async-start(bf16[16,48,512]{2,1,0:T(8,128)(2,1)} %bitcast.8), calls=%async_computation.4 | async-start | bytes 1572864 | tf_op jit(solution)/shard_map/all_to_all | solution.py:148
  138.8 0.4 convolution_convert_fusion.1
  139.2 0.0 collective-permute-done.2
  139.2 1.5 convolution_convert_fusion
  140.7 2.6 %fusion.9 = bf16[128,1408]{1,0:T(8,128)(2,1)} fusion(s32[1536]{0:T(1024)S(1)} %fusion.33, bf16[128,768]{1,0:T(8,128)(2,1)S(1)} %convolution_convert_fusion, bf16[128,768]{1,0:T(8,128)(2,1)S(1)} %convolution_convert_fusion.1), kind=kOutput, calls=%fused_computation.7 | convolution fusion | flops 556777472 | bytes 759808 | tf_op jit(solution)/shard_map/dot_general | solution.py:18
  143.3 18.4 %reduce-scatter.2.cloned.1.call-done = bf16[128,512]{1,0:T(8,128)(2,1)} async-done(((bf16[1024,512]{1,0:T(8,128)(2,1)}), bf16[128,512]{1,0:T(8,128)(2,1)}) %reduce-scatter.2.cloned.1.call-update) | async-done | bytes 131088 | tf_op jit(solution)/shard_map/reduce_scatter | solution.py:140
  161.8 1.0 fusion.21
  162.8 1.7 fusion.20
  164.5 0.3 all-to-all-done.3
  164.8 0.8 convert_reduce_fusion
  (5 shorter events, 0.1 us)
Async XLA Ops:
  7.2 18.5 %copy-start = (bf16[128,1408]{1,0:T(8,128)(2,1)S(1)}, bf16[128,1408]{1,0:T(8,128)(2,1)}, u32[]{:S(2)}) copy-start(bf16[128,1408]{1,0:T(8,128)(2,1)} %param.4) | copy-start | bytes 1081348
  7.2 17.6 %copy-start.1 = (bf16[128,512]{1,0:T(8,128)(2,1)S(1)}, bf16[128,512]{1,0:T(8,128)(2,1)}, u32[]{:S(2)}) copy-start(bf16[128,512]{1,0:T(8,128)(2,1)} %param.5) | copy-start | bytes 393220
  9.0 43.4 %all-to-all-start = ((bf16[16,48,512]{2,1,0:T(8,128)(2,1)}), bf16[16,48,512]{2,1,0:T(8,128)(2,1)S(1)}, u32[]{:S(2)}, u32[]{:S(2)}) async-start(bf16[16,48,512]{2,1,0:T(8,128)(2,1)} %broadcast_in_dim.20), calls=%async_computation | async-start | bytes 1572864 | tf_op jit(solution)/shard_map/all_to_all | solution.py:25
  24.7 52.8 %all-gather.2.cloned.1.call-start = ((), (), s32[]{:S(2)}) async-start(), calls=%async_computation.5 | async-start | bytes 1179648 | tf_op jit(solution)/shard_map/all_gather | solution.py:121
  27.1 21.5 %collective-permute-start = (bf16[128,768]{0,1:T(8,128)(2,1)S(1)}, bf16[128,768]{0,1:T(8,128)(2,1)S(1)}, u32[]{:S(2)}, u32[]{:S(2)}) collective-permute-start(bf16[128,768]{0,1:T(8,128)(2,1)S(1)} %slice.13), channel_id=1, source_target_pairs={{0,4},{4,0},{1,5},{5,1},{2,6},{6,2},{3,7},{7,3},{8,12},{12,8},{9,1... | collective-permute-start | bytes 589832 | tf_op jit(solution)/shard_map/ppermute | solution.py:29
  52.7 7.9 %collective-permute-start.1 = (bf16[128,512]{1,0:T(8,128)(2,1)S(1)}, bf16[128,512]{1,0:T(8,128)(2,1)S(1)}, u32[]{:S(2)}, u32[]{:S(2)}) collective-permute-start(bf16[128,512]{1,0:T(8,128)(2,1)S(1)} %convolution_convert_fusion.2), channel_id=1, source_target_pairs={{0,4},{4,0},{1,5},{5,1},{2,6},{6,2},{3,7},{7,3},{8,12},{12,8},{9,1... | collective-permute-start | bytes 393224 | tf_op jit(solution)/shard_map/ppermute | solution.py:29
  77.5 3.6 %copy-start.2 = (bf16[512,512]{1,0:T(8,128)(2,1)}, bf16[512,512]{1,0:T(8,128)(2,1)S(1)}, u32[]{:S(2)}) copy-start(bf16[512,512]{1,0:T(8,128)(2,1)S(1)} %all_gather.6.images) | copy-start | bytes 1572868
  81.7 15.6 %all-to-all-start.1 = ((f32[8,8,128]{2,1,0:T(8,128)}), f32[8,8,128]{2,1,0:T(8,128)S(1)}, u32[]{:S(2)}, u32[]{:S(2)}) async-start(f32[8,8,128]{2,1,0:T(8,128)} %broadcast_in_dim.34), calls=%async_computation.1 | async-start | bytes 65536 | tf_op jit(solution)/shard_map/all_to_all | solution.py:25
  97.3 0.6 copy-start.4
  102.5 15.3 %copy-start.3 = (f32[128,512]{1,0:T(8,128)S(1)}, f32[128,512]{1,0:T(8,128)}, u32[]{:S(2)}) copy-start(f32[128,512]{1,0:T(8,128)} %get-tuple-element.6) | copy-start | bytes 786436
  102.5 15.1 %all-to-all-start.2 = ((bf16[4,128,512]{2,1,0:T(8,128)(2,1)}), bf16[4,128,512]{2,1,0:T(8,128)(2,1)S(1)}, u32[]{:S(2)}, u32[]{:S(2)}) async-start(bf16[4,128,512]{2,1,0:T(8,128)(2,1)} %bitcast.33), calls=%async_computation.2 | async-start | bytes 1048576 | tf_op jit(solution)/shard_map/all_to_all | solution.py:141
  106.3 55.5 %reduce-scatter.2.cloned.1.call-start = ((), (), s32[]{:S(2)}) async-start(), calls=%async_computation.6 | async-start | bytes 1179648 | tf_op jit(solution)/shard_map/reduce_scatter | solution.py:140
  106.3 32.9 %collective-permute-start.2 = (bf16[768,512]{1,0:T(8,128)(2,1)S(1)}, bf16[768,512]{1,0:T(8,128)(2,1)}, u32[]{:S(2)}, u32[]{:S(2)}) collective-permute-start(bf16[768,512]{1,0:T(8,128)(2,1)S(1)} %bitcast.31), channel_id=1, source_target_pairs={{0,4},{4,0},{1,5},{5,1},{2,6},{6,2},{3,7},{7,3},{8,12},{12,8},{9,1... | collective-permute-start | bytes 2359304 | tf_op jit(solution)/shard_map/ppermute | solution.py:29
  118.1 7.6 %collective-permute-start.3 = (bf16[128,512]{1,0:T(8,128)(2,1)S(1)}, bf16[128,512]{1,0:T(8,128)(2,1)S(1)}, u32[]{:S(2)}, u32[]{:S(2)}) collective-permute-start(bf16[128,512]{1,0:T(8,128)(2,1)S(1)} %subtract_convert_fusion), channel_id=1, source_target_pairs={{0,4},{4,0},{1,5},{5,1},{2,6},{6,2},{3,7},{7,3},{8,12},{12,8},{9,1... | collective-permute-start | bytes 393224 | tf_op jit(solution)/shard_map/ppermute | solution.py:29
  126.9 37.8 %all-to-all-start.3 = ((bf16[16,48,512]{2,1,0:T(8,128)(2,1)}), bf16[16,48,512]{2,1,0:T(8,128)(2,1)S(1)}, u32[]{:S(2)}, u32[]{:S(2)}) async-start(bf16[16,48,512]{2,1,0:T(8,128)(2,1)} %bitcast.8), calls=%async_computation.4 | async-start | bytes 1572864 | tf_op jit(solution)/shard_map/all_to_all | solution.py:148
Sparse Core Ops, SparseCore 0:
  28.2 42.2 all-gather.1
  110.3 51.3 reduce-scatter.1

commit v8 on v7

--- a/solution.py
+++ b/solution.py
@@ -120,7 +120,6 @@
     txt_unit = (txt_emb * txt_inv).astype(jnp.bfloat16)
     texts = lax.all_gather(txt_unit, Y, axis=0, tiled=True)
     returned = swapped(partner_part)
-    other_head = swapped(head)
 
     img_emb = matmul(kept, head) + returned.astype(jnp.float32)
     img_inv = inv_norm(img_emb)
@@ -132,8 +131,7 @@
     col_part = jnp.sum(exps, axis=0)
 
     col_parts = to_all(col_part.reshape(NY, rows), Y, NY)
-    row_sum = lax.optimization_barrier(lax.psum(row_part, Z))
-    row_sum = row_sum.reshape(NZ, rows)
+    row_sum = lax.psum(row_part.reshape(NZ, rows), Z)
     img_sent, img_own, txt_sent = coef_products(
         a, b, exps, row_sum, col_parts, images, texts
     )
@@ -149,7 +147,7 @@
         head_part.astype(jnp.bfloat16).reshape(NQ * NZ, padded, emb_width), SAME, 0, 0, tiled=True
     )
     kept_grad = matmul(img_emb_grad, head, 1, 1).astype(jnp.bfloat16)
-    given_grad = matmul(img_emb_grad, other_head, 1, 1).astype(jnp.bfloat16)
+    given_grad = swapped(matmul(partner_grad, head, 1, 1).astype(jnp.bfloat16))
     feat_grad = jnp.concatenate([kept_grad, given_grad], axis=1)
     image_features_grad = matmul(feat_grad, choice, 1, 1).astype(jnp.bfloat16)
 

time: 173 us -> 173 us (level)
  waiting for transfers between devices: 57.5 us -> 63.1 us
  starting transfers between devices: 48.3 us -> 43.7 us
    ppermute x4, waiting for transfers between devices: 27.5 us -> 47.9 us  [swapped(): return lax.ppermute(array, PAIR, [(0, 1), (1, 0)])]
    reduce_scatter x1, waiting for transfers between devices: 18.4 us -> 0.01 us  [local(): txt_sum = lax.psum_scatter(txt_sent, Y, scatter_dimension=0, tiled=True)]
    all_to_all x1, waiting for transfers between devices: 7.4 us -> 10.6 us  [local(): lax.all_to_all(img_sent.reshape(NZ, rows, emb_width), Z, 0, 0, tiled=True)]
    all_to_all x1, starting transfers between devices: 11.9 us -> 9.17 us  [local(): lax.all_to_all(head_part.astype(jnp.bfloat16).reshape(NQ * NZ, padded, em...]
    ppermute x4, starting transfers between devices: 12.4 us -> 10.5 us  [swapped(): return lax.ppermute(array, PAIR, [(0, 1), (1, 0)])]
  transfers between devices with their start and end apart: 10 -> 10, of which waited for: 7 -> 6; matrix products, arithmetic and copies ran while one was open for 7% -> 6% of each run, Pallas kernels for 0% -> 0%
where the time goes in v8:
time: 173 us; the launch traced here: 172 us
  waiting for transfers between devices  63.1 us (36%)
  starting transfers between devices  43.7 us (25%)
  blocking collectives  27.4 us (16%)
  between operations  14.9 us (9%)
  matrix products  10.5 us (6%)
  other arithmetic  4.94 us (3%)
  Pallas kernels  4.62 us (3%)
  local copies, waits for them, and re-layouts  3.1 us (2%)
    ppermute x4, waiting for transfers between devices, swapped(): return lax.ppermute(array, PAIR, [(0, 1), (1, 0)])  47.9 us
    all_to_all x2, starting transfers between devices, to_all(): return lax.all_to_all(copies, axes, 0, 0, tiled=True)  20.2 us
    all_gather x1, blocking collectives, local(): images = lax.all_gather(img_unit, Z, axis=0, tiled=True)  16.4 us
    psum x1, blocking collectives, local(): row_sum = lax.psum(row_part.reshape(NZ, rows), Z)  11.1 us
    all_to_all x1, waiting for transfers between devices, local(): lax.all_to_all(img_sent.reshape(NZ, rows, emb_width), Z, 0, 0, tiled=True)  10.6 us
    ppermute x4, starting transfers between devices, swapped(): return lax.ppermute(array, PAIR, [(0, 1), (1, 0)])  10.5 us
    dot_general x9, matrix products, matmul(): lax.dot_general(left, right, (((left_dim,), (right_dim,)), ((), ())), pre...  10.5 us
    all_to_all x1, starting transfers between devices, local(): lax.all_to_all(head_part.astype(jnp.bfloat16).reshape(NQ * NZ, padded, em...  9.17 us
  transfers between devices with their start and end apart: 10, of which 6 were waited for; matrix products, arithmetic and copies ran while one was open for 6% of the time, Pallas kernels for 0%

profile of v8, /device:TPU:6, one launch (start us, length us, event | category | flops | bytes accessed | tf_op | source)
XLA Modules:
  0.0 172.2 jit_solution(15564075644385151912)
XLA Ops:
  7.2 0.0 copy-start
  7.2 0.0 copy-start.1
  7.2 0.9 pad.4
  8.1 1.0 broadcast_in_dim.20
  9.0 15.7 %all-to-all-start = ((bf16[16,48,512]{2,1,0:T(8,128)(2,1)}), bf16[16,48,512]{2,1,0:T(8,128)(2,1)S(1)}, u32[]{:S(2)}, u32[]{:S(2)}) async-start(bf16[16,48,512]{2,1,0:T(8,128)(2,1)} %broadcast_in_dim.20), calls=%async_computation | async-start | bytes 1572864 | tf_op jit(solution)/shard_map/all_to_all | solution.py:25
  24.7 0.0 all-gather.2.cloned.1.call-start
  24.8 0.0 copy-done.1
  24.8 0.1 fusion.16
  24.9 0.8 fusion.17
  25.6 0.0 all-gather.2.cloned.1.call-update
  25.7 0.0 copy-done
  25.7 1.4 fusion.10
  27.1 2.6 %collective-permute-start = (bf16[128,768]{0,1:T(8,128)(2,1)S(1)}, bf16[128,768]{0,1:T(8,128)(2,1)S(1)}, u32[]{:S(2)}, u32[]{:S(2)}) collective-permute-start(bf16[128,768]{0,1:T(8,128)(2,1)S(1)} %slice.13), channel_id=1, source_target_pairs={{0,4},{4,0},{1,5},{5,1},{2,6},{6,2},{3,7},{7,3},{8,12},{12,8},{9,1... | collective-permute-start | bytes 589832 | tf_op jit(solution)/shard_map/ppermute | solution.py:29
  29.7 18.9 %collective-permute-done = bf16[128,768]{0,1:T(8,128)(2,1)S(1)} collective-permute-done((bf16[128,768]{0,1:T(8,128)(2,1)S(1)}, bf16[128,768]{0,1:T(8,128)(2,1)S(1)}, u32[]{:S(2)}, u32[]{:S(2)}) %collective-permute-start) | collective-permute-done | bytes 196640 | tf_op jit(solution)/shard_map/ppermute | solution.py:29
  48.6 3.8 %all-to-all-done = bf16[16,48,512]{2,1,0:T(8,128)(2,1)S(1)} async-done(((bf16[16,48,512]{2,1,0:T(8,128)(2,1)}), bf16[16,48,512]{2,1,0:T(8,128)(2,1)S(1)}, u32[]{:S(2)}, u32[]{:S(2)}) %all-to-all-start) | async-done | bytes 786464 | tf_op jit(solution)/shard_map/all_to_all | solution.py:25
  52.4 0.3 convolution_convert_fusion.2
  52.7 1.9 %collective-permute-start.1 = (bf16[128,512]{1,0:T(8,128)(2,1)S(1)}, bf16[128,512]{1,0:T(8,128)(2,1)S(1)}, u32[]{:S(2)}, u32[]{:S(2)}) collective-permute-start(bf16[128,512]{1,0:T(8,128)(2,1)S(1)} %convolution_convert_fusion.2), channel_id=1, source_target_pairs={{0,4},{4,0},{1,5},{5,1},{2,6},{6,2},{3,7},{7,3},{8,12},{12,8},{9,1... | collective-permute-start | bytes 393224 | tf_op jit(solution)/shard_map/ppermute | solution.py:29
  55.3 5.3 %collective-permute-done.1 = bf16[128,512]{1,0:T(8,128)(2,1)S(1)} collective-permute-done((bf16[128,512]{1,0:T(8,128)(2,1)S(1)}, bf16[128,512]{1,0:T(8,128)(2,1)S(1)}, u32[]{:S(2)}, u32[]{:S(2)}) %collective-permute-start.1) | collective-permute-done | bytes 131104 | tf_op jit(solution)/shard_map/ppermute | solution.py:29
  60.6 0.4 multiply_reduce_fusion.1
  61.0 0.1 multiply_convert_fusion
  61.1 16.4 %all_gather.6.images = bf16[512,512]{1,0:T(8,128)(2,1)S(1)} all-gather(bf16[128,512]{1,0:T(8,128)(2,1)S(1)} %multiply_convert_fusion), channel_id=1, replica_groups=mesh['rep'=16,'dp_q'=4,'dp_pair'=2,'dp_z'=4] {'dp_z'}, dimensions={0}, use_global_device_ids=true | all-gather | bytes 655360 | tf_op jit(solution)/shard_map/all_gather | solution.py:127
  77.5 0.0 copy-start.2
  77.5 0.0 all-gather.2.cloned.1.call-done.texts
  77.5 3.6 %fusion.50 = (f32[1024]{0:T(1024)S(1)}, f32[512]{0:T(512)S(1)}, f32[512,1024]{1,0:T(8,128)}) fusion(bf16[512,512]{1,0:T(8,128)(2,1)S(1)} %all_gather.6.images, bf16[1024,512]{1,0:T(8,128)(2,1)} %all-gather.2.cloned.1.call-done.texts, f32[]{:T(128)} %bitcast.25), kind=kOutput, calls=%fused_computation.88 | convolution fusion | flops 538442240 | bytes 3676164 | tf_op jit(solution)/shard_map/dot_general | solution.py:18
  81.0 0.0 copy-done.2
  81.0 0.6 broadcast_in_dim.34
  81.7 4.5 %all-to-all-start.1 = ((f32[8,8,128]{2,1,0:T(8,128)}), f32[8,8,128]{2,1,0:T(8,128)S(1)}, u32[]{:S(2)}, u32[]{:S(2)}) async-start(f32[8,8,128]{2,1,0:T(8,128)} %broadcast_in_dim.34), calls=%async_computation.1 | async-start | bytes 65536 | tf_op jit(solution)/shard_map/all_to_all | solution.py:25
  86.2 11.1 %psum.7.row_sum = f32[4,128]{1,0:T(4,128)} all-reduce(f32[4,128]{1,0:T(4,128)S(1)} %bitcast.36), channel_id=1, replica_groups=mesh['rep'=16,'dp_q'=4,'dp_pair'=2,'dp_z'=4] {'dp_z'}, use_global_device_ids=true, to_apply=%region_3.4 | all-reduce | flops 512 | bytes 4096 | tf_op jit(solution)/shard_map/psum | solution.py:134
  97.3 0.0 all-to-all-done.1.col_parts
  97.3 0.0 copy-start.4
  97.3 0.6 copy-done.4
  97.9 4.6 %coef_products.1 = (bf16[512,512]{1,0:T(8,128)(2,1)}, f32[128,512]{1,0:T(8,128)}, bf16[1024,512]{1,0:T(8,128)(2,1)}) custom-call(s32[1]{0:T(128)} %bitcast.3.at_y, s32[1]{0:T(128)} %bitcast.4.at_z, f32[512,1024]{1,0:T(8,128)} %get-tuple-element.17.exps, f32[4,128]{1,0:T(4,128)} %psum.7.row_sum, f32[8,8,128]{2,1,0:T(8,128)} %copy-done.4, ...), custom_call_target="tpu_custom_call" | custom-call | tf_op jit(solution)/shard_map/coef_products/pallas_call | solution.py:65
  102.5 0.0 copy-start.3
  102.5 3.8 %all-to-all-start.2 = ((bf16[4,128,512]{2,1,0:T(8,128)(2,1)}), bf16[4,128,512]{2,1,0:T(8,128)(2,1)S(1)}, u32[]{:S(2)}, u32[]{:S(2)}) async-start(bf16[4,128,512]{2,1,0:T(8,128)(2,1)} %bitcast.33), calls=%async_computation.2 | async-start | bytes 1048576 | tf_op jit(solution)/shard_map/all_to_all | solution.py:139
  106.2 0.0 reduce-scatter.2.cloned.1.call-start
  106.3 0.7 reduce-scatter.2.cloned.1.call-update
  107.0 10.6 %all-to-all-done.2 = bf16[4,128,512]{2,1,0:T(8,128)(2,1)S(1)} async-done(((bf16[4,128,512]{2,1,0:T(8,128)(2,1)}), bf16[4,128,512]{2,1,0:T(8,128)(2,1)S(1)}, u32[]{:S(2)}, u32[]{:S(2)}) %all-to-all-start.2) | async-done | bytes 524320 | tf_op jit(solution)/shard_map/all_to_all | solution.py:139
  117.6 0.2 select_reduce_fusion
  117.8 0.0 copy-done.3
  117.8 0.1 multiply_reduce_fusion
  117.9 0.1 subtract_convert_fusion
  118.1 4.0 %collective-permute-start.2 = (bf16[128,512]{1,0:T(8,128)(2,1)S(1)}, bf16[128,512]{1,0:T(8,128)(2,1)S(1)}, u32[]{:S(2)}, u32[]{:S(2)}) collective-permute-start(bf16[128,512]{1,0:T(8,128)(2,1)S(1)} %subtract_convert_fusion), channel_id=1, source_target_pairs={{0,4},{4,0},{1,5},{5,1},{2,6},{6,2},{3,7},{7,3},{8,12},{12,8},{9,1... | collective-permute-start | bytes 393224 | tf_op jit(solution)/shard_map/ppermute | solution.py:29
  122.1 0.3 fusion.22
  122.4 2.6 %collective-permute-done.2 = bf16[128,512]{1,0:T(8,128)(2,1)S(1)} collective-permute-done((bf16[128,512]{1,0:T(8,128)(2,1)S(1)}, bf16[128,512]{1,0:T(8,128)(2,1)S(1)}, u32[]{:S(2)}, u32[]{:S(2)}) %collective-permute-start.2) | collective-permute-done | bytes 131104 | tf_op jit(solution)/shard_map/ppermute | solution.py:29
  125.0 1.2 add_convert_fusion
  126.2 9.2 %all-to-all-start.3 = ((bf16[16,48,512]{2,1,0:T(8,128)(2,1)}), bf16[16,48,512]{2,1,0:T(8,128)(2,1)S(1)}, u32[]{:S(2)}, u32[]{:S(2)}) async-start(bf16[16,48,512]{2,1,0:T(8,128)(2,1)} %bitcast.8), calls=%async_computation.4 | async-start | bytes 1572864 | tf_op jit(solution)/shard_map/all_to_all | solution.py:146
  135.4 0.4 convolution_convert_fusion
  135.8 2.0 %collective-permute-start.3 = (bf16[128,768]{1,0:T(8,128)(2,1)S(1)}, bf16[128,768]{1,0:T(8,128)(2,1)S(1)}, u32[]{:S(2)}, u32[]{:S(2)}) collective-permute-start(bf16[128,768]{1,0:T(8,128)(2,1)S(1)} %convolution_convert_fusion), channel_id=1, source_target_pairs={{0,4},{4,0},{1,5},{5,1},{2,6},{6,2},{3,7},{7,3},{8,12},{12,8},{9,1... | collective-permute-start | bytes 589832 | tf_op jit(solution)/shard_map/ppermute | solution.py:29
  137.8 0.4 convolution_convert_fusion.1
  138.2 21.1 %collective-permute-done.3 = bf16[128,768]{1,0:T(8,128)(2,1)S(1)} collective-permute-done((bf16[128,768]{1,0:T(8,128)(2,1)S(1)}, bf16[128,768]{1,0:T(8,128)(2,1)S(1)}, u32[]{:S(2)}, u32[]{:S(2)}) %collective-permute-start.3) | collective-permute-done | bytes 196640 | tf_op jit(solution)/shard_map/ppermute | solution.py:29
  159.3 2.6 %fusion.9 = bf16[128,1408]{1,0:T(8,128)(2,1)} fusion(s32[1536]{0:T(1024)S(1)} %fusion.33, bf16[128,768]{1,0:T(8,128)(2,1)S(1)} %collective-permute-done.3, bf16[128,768]{1,0:T(8,128)(2,1)S(1)} %convolution_convert_fusion.1), kind=kOutput, calls=%fused_computation.7 | convolution fusion | flops 556777472 | bytes 759808 | tf_op jit(solution)/shard_map/dot_general | solution.py:18
  161.9 0.0 reduce-scatter.2.cloned.1.call-done
  161.9 1.0 fusion.21
  162.9 1.7 fusion.20
  164.6 0.0 all-to-all-done.3
  164.6 0.8 convert_reduce_fusion
  (5 shorter events, 0.1 us)
Async XLA Ops:
  7.2 18.5 %copy-start = (bf16[128,1408]{1,0:T(8,128)(2,1)S(1)}, bf16[128,1408]{1,0:T(8,128)(2,1)}, u32[]{:S(2)}) copy-start(bf16[128,1408]{1,0:T(8,128)(2,1)} %param.4) | copy-start | bytes 1081348
  7.2 17.6 %copy-start.1 = (bf16[128,512]{1,0:T(8,128)(2,1)S(1)}, bf16[128,512]{1,0:T(8,128)(2,1)}, u32[]{:S(2)}) copy-start(bf16[128,512]{1,0:T(8,128)(2,1)} %param.5) | copy-start | bytes 393220
  9.0 43.4 %all-to-all-start = ((bf16[16,48,512]{2,1,0:T(8,128)(2,1)}), bf16[16,48,512]{2,1,0:T(8,128)(2,1)S(1)}, u32[]{:S(2)}, u32[]{:S(2)}) async-start(bf16[16,48,512]{2,1,0:T(8,128)(2,1)} %broadcast_in_dim.20), calls=%async_computation | async-start | bytes 1572864 | tf_op jit(solution)/shard_map/all_to_all | solution.py:25
  24.7 52.8 %all-gather.2.cloned.1.call-start = ((), (), s32[]{:S(2)}) async-start(), calls=%async_computation.5 | async-start | bytes 1179648 | tf_op jit(solution)/shard_map/all_gather | solution.py:121
  27.1 21.5 %collective-permute-start = (bf16[128,768]{0,1:T(8,128)(2,1)S(1)}, bf16[128,768]{0,1:T(8,128)(2,1)S(1)}, u32[]{:S(2)}, u32[]{:S(2)}) collective-permute-start(bf16[128,768]{0,1:T(8,128)(2,1)S(1)} %slice.13), channel_id=1, source_target_pairs={{0,4},{4,0},{1,5},{5,1},{2,6},{6,2},{3,7},{7,3},{8,12},{12,8},{9,1... | collective-permute-start | bytes 589832 | tf_op jit(solution)/shard_map/ppermute | solution.py:29
  52.7 7.9 %collective-permute-start.1 = (bf16[128,512]{1,0:T(8,128)(2,1)S(1)}, bf16[128,512]{1,0:T(8,128)(2,1)S(1)}, u32[]{:S(2)}, u32[]{:S(2)}) collective-permute-start(bf16[128,512]{1,0:T(8,128)(2,1)S(1)} %convolution_convert_fusion.2), channel_id=1, source_target_pairs={{0,4},{4,0},{1,5},{5,1},{2,6},{6,2},{3,7},{7,3},{8,12},{12,8},{9,1... | collective-permute-start | bytes 393224 | tf_op jit(solution)/shard_map/ppermute | solution.py:29
  77.5 3.6 %copy-start.2 = (bf16[512,512]{1,0:T(8,128)(2,1)}, bf16[512,512]{1,0:T(8,128)(2,1)S(1)}, u32[]{:S(2)}) copy-start(bf16[512,512]{1,0:T(8,128)(2,1)S(1)} %all_gather.6.images) | copy-start | bytes 1572868
  81.7 15.6 %all-to-all-start.1 = ((f32[8,8,128]{2,1,0:T(8,128)}), f32[8,8,128]{2,1,0:T(8,128)S(1)}, u32[]{:S(2)}, u32[]{:S(2)}) async-start(f32[8,8,128]{2,1,0:T(8,128)} %broadcast_in_dim.34), calls=%async_computation.1 | async-start | bytes 65536 | tf_op jit(solution)/shard_map/all_to_all | solution.py:25
  97.3 0.6 copy-start.4
  102.5 15.3 %copy-start.3 = (f32[128,512]{1,0:T(8,128)S(1)}, f32[128,512]{1,0:T(8,128)}, u32[]{:S(2)}) copy-start(f32[128,512]{1,0:T(8,128)} %get-tuple-element.6) | copy-start | bytes 786436
  102.5 15.1 %all-to-all-start.2 = ((bf16[4,128,512]{2,1,0:T(8,128)(2,1)}), bf16[4,128,512]{2,1,0:T(8,128)(2,1)S(1)}, u32[]{:S(2)}, u32[]{:S(2)}) async-start(bf16[4,128,512]{2,1,0:T(8,128)(2,1)} %bitcast.33), calls=%async_computation.2 | async-start | bytes 1048576 | tf_op jit(solution)/shard_map/all_to_all | solution.py:139
  106.2 55.7 %reduce-scatter.2.cloned.1.call-start = ((), (), s32[]{:S(2)}) async-start(), calls=%async_computation.6 | async-start | bytes 1179648 | tf_op jit(solution)/shard_map/reduce_scatter | solution.py:138
  118.1 6.9 %collective-permute-start.2 = (bf16[128,512]{1,0:T(8,128)(2,1)S(1)}, bf16[128,512]{1,0:T(8,128)(2,1)S(1)}, u32[]{:S(2)}, u32[]{:S(2)}) collective-permute-start(bf16[128,512]{1,0:T(8,128)(2,1)S(1)} %subtract_convert_fusion), channel_id=1, source_target_pairs={{0,4},{4,0},{1,5},{5,1},{2,6},{6,2},{3,7},{7,3},{8,12},{12,8},{9,1... | collective-permute-start | bytes 393224 | tf_op jit(solution)/shard_map/ppermute | solution.py:29
  126.2 38.4 %all-to-all-start.3 = ((bf16[16,48,512]{2,1,0:T(8,128)(2,1)}), bf16[16,48,512]{2,1,0:T(8,128)(2,1)S(1)}, u32[]{:S(2)}, u32[]{:S(2)}) async-start(bf16[16,48,512]{2,1,0:T(8,128)(2,1)} %bitcast.8), calls=%async_computation.4 | async-start | bytes 1572864 | tf_op jit(solution)/shard_map/all_to_all | solution.py:146
  135.8 23.5 %collective-permute-start.3 = (bf16[128,768]{1,0:T(8,128)(2,1)S(1)}, bf16[128,768]{1,0:T(8,128)(2,1)S(1)}, u32[]{:S(2)}, u32[]{:S(2)}) collective-permute-start(bf16[128,768]{1,0:T(8,128)(2,1)S(1)} %convolution_convert_fusion), channel_id=1, source_target_pairs={{0,4},{4,0},{1,5},{5,1},{2,6},{6,2},{3,7},{7,3},{8,12},{12,8},{9,1... | collective-permute-start | bytes 589832 | tf_op jit(solution)/shard_map/ppermute | solution.py:29
Sparse Core Ops, SparseCore 0:
  28.2 42.2 all-gather.1
  109.9 49.9 reduce-scatter.1
